TPU v7x, 256 devices: a whole 4x4x8 slice. The times are simulated.
256 devices in a mesh: row: 32 (over z, x), src: 8 (over y, core).
Axes of the slice: x: 4, y: 4, z: 8, core: 2. Of those that a mesh axis runs over, the one named last changes fastest.
Arguments:
- sub_source: float32 [32768, 4096], P('row', 'src'), may hold values from -6 to 6
- sub_inverse: bfloat16 [32768, 1024], P('row'), as said below
- coupling: bfloat16 [32, 2, 512, 1024], P('row'), may hold values from -0.0625 to 0.0625
- update_lists: int32 [32, 2], P('row'), may hold values from 0 to 3, as said below
- sep_source: float32 [2048, 4096], P('row', 'src'), may hold values from -6 to 6
- sep_inverse: bfloat16 [16384, 512], P(('row', 'src')), as said below
- sep_lower: bfloat16 [16384, 1024], P(('row', 'src')), may hold values from -0.125 to 0.125
- factor_owner_slots: int32 [4], replicated, may hold values from 0 to 31, as said below
- sep_links: int32 [4, 2], replicated, may hold values from -1 to 2, as said below
Outputs:
- sub_field: float32 [32768, 4096], P('row', 'src')
- sep_field: float32 [2048, 4096], P('row', 'src')
Inputs may be any that keep to these rules, and one draw needn't show every extreme that they name: `update_lists`: each subtree lists two different separator blocks. `factor_owner_slots`: the 4 entries are different slots. `sep_links`: for block k the first entry is k - 1 and the second is -1 or a block below k - 1; -1 means no link. `sub_inverse`: each slot of 1024 rows is lower triangular. `sep_inverse`: each slot of 512 rows is lower triangular.
All inputs are finite; a program needn't handle non-finite values.
Results may differ from a plain program's by a relative error of at most 0.006.
Values may be sent and summed in bfloat16 or wider, within the bound.
A program may use at most 64 MiB of HBM per device.

v0:
```python
import jax
import jax.numpy as jnp
from jax import lax
from jax.sharding import PartitionSpec as P

SEP_BLOCK = 512
STEPS = 4
LINKS = 2
SEP_ROWS = 2048


def from_root(shard, axis, root):
    mine = lax.axis_index(axis) == root
    return lax.psum(jnp.where(mine, shard, jnp.zeros_like(shard)), axis)


def per_device(
    sub_source,
    sub_inverse,
    coupling,
    update_lists,
    sep_source,
    sep_inverse,
    sep_lower,
    factor_owner_slots,
    sep_links,
):
    sources = sub_source.shape[1]
    sub_field = jnp.dot(
        sub_inverse, sub_source.astype(jnp.bfloat16), preferred_element_type=jnp.float32
    )
    padded_length = sub_field.astype(jnp.bfloat16)
    pending_updates = jnp.einsum(
        "rmf,ft->rmt", coupling[0], padded_length, preferred_element_type=jnp.float32
    )
    picks = update_lists[0][:, None] == jnp.arange(STEPS, dtype=jnp.int32)[None, :]
    dense = jnp.sum(jnp.where(picks[:, :, None, None], pending_updates[:, None], 0.0), axis=0)
    local_rows = sep_source.shape[0]
    my_row = lax.axis_index("row")
    placed = lax.dynamic_update_slice(
        jnp.zeros((SEP_ROWS, sources), jnp.float32),
        sep_source,
        (my_row * local_rows, jnp.zeros((), jnp.int32)),
    )
    terms = placed - dense.reshape(SEP_ROWS, sources)
    totals = lax.psum(terms, "row")
    inverse_row_block, lower_rows = (
        lax.all_gather(sep_inverse, "src", axis=0, tiled=True),
        lax.all_gather(sep_lower, "src", axis=0, tiled=True),
    )
    solved = jnp.zeros((STEPS, SEP_BLOCK, sources), jnp.float32)
    for block_id in range(STEPS):
        pending = totals[block_id * SEP_BLOCK : (block_id + 1) * SEP_BLOCK]
        pieces = []
        for link_pos in range(LINKS):
            target = sep_links[block_id, link_pos]
            chosen = solved[jnp.maximum(target, 0)]
            pieces.append(jnp.where(target >= 0, chosen, 0.0).astype(jnp.bfloat16))
        stacked = jnp.concatenate(pieces, axis=0)
        remaining_source = pending - jnp.dot(
            lower_rows, stacked, preferred_element_type=jnp.float32
        )
        candidate = jnp.dot(
            inverse_row_block,
            remaining_source.astype(jnp.bfloat16),
            preferred_element_type=jnp.float32,
        )
        result = from_root(candidate, "row", factor_owner_slots[block_id])
        solved = solved.at[block_id].set(result)
    whole_field = solved.reshape(SEP_ROWS, sources)
    own_rows = lax.dynamic_slice_in_dim(whole_field, my_row * local_rows, local_rows, 0)
    return (sub_field, own_rows)


def solution(mesh):
    return jax.shard_map(
        per_device,
        mesh=mesh,
        in_specs=(
            P("row", "src"),
            P("row", None),
            P("row", None, None, None),
            P("row", None),
            P("row", "src"),
            P(("row", "src"), None),
            P(("row", "src"), None),
            P(),
            P(),
        ),
        out_specs=(P("row", "src"), P("row", "src")),
        check_vma=False,
    )
```

profile of v0, /device:TPU:16, one launch (start us, length us, event | category | flops | bytes accessed | tf_op | source)
XLA Modules:
  0.0 840.6 jit_solution(14617722687658571348)
XLA Ops:
  9.9 3.0 fusion.32
  14.2 2.6 fusion.2
  16.8 2.9 copy.18
  19.8 4.9 select_reduce_fusion
  24.7 5.4 copy.23
  30.1 2.5 broadcast_in_dim.36
  34.4 6.7 sub.15
  43.1 13.0 %all_gather.7 = bf16[512,512]{1,0:T(8,128)(2,1)S(1)} all-gather(bf16[64,512]{1,0:T(8,128)(2,1)S(1)} %copy-done.3), channel_id=1, replica_groups=mesh['row'=32,'src'=8] {'src'}, dimensions={0}, use_global_device_ids=true | all-gather | bytes 589824 | tf_op jit(solution)/shard_map/all_gather | solution.py:48
  56.1 152.2 %all-reduce.8.cloned.1.call-done = f32[2048,512]{0,1:T(8,128)} async-done(((f32[2048,512]{0,1:T(8,128)}), f32[2048,512]{0,1:T(8,128)}) %all-reduce.8.cloned.1.call-update) | async-done | bytes 4194320 | tf_op jit(solution)/shard_map/psum | solution.py:46
  208.3 3.8 fusion.8
  215.8 143.8 %all-reduce.10.cloned.1.call-done = f32[1,512,512]{1,2,0:T(8,128)} async-done(((f32[1,512,512]{1,2,0:T(8,128)}), f32[1,512,512]{1,2,0:T(8,128)}) %all-reduce.10.cloned.1.call-update) | async-done | bytes 1048592 | tf_op jit(solution)/shard_map/psum | solution.py:14
  359.6 2.7 fusion.45
  362.4 4.0 fusion.7
  369.6 2.6 scatter.14
  372.2 141.5 %all-reduce.12.cloned.1.call-done = f32[1,512,512]{1,2,0:T(8,128)} async-done(((f32[1,512,512]{1,2,0:T(8,128)}), f32[1,512,512]{1,2,0:T(8,128)}) %all-reduce.12.cloned.1.call-update) | async-done | bytes 1048592 | tf_op jit(solution)/shard_map/psum | solution.py:14
  513.7 2.3 constant_dynamic-update-slice_fusion.2
  516.0 1.8 fusion.40
  517.8 3.7 fusion.6
  524.6 144.2 %all-reduce.14.cloned.1.call-done = f32[1,512,512]{1,2,0:T(8,128)} async-done(((f32[1,512,512]{1,2,0:T(8,128)}), f32[1,512,512]{1,2,0:T(8,128)}) %all-reduce.14.cloned.1.call-update) | async-done | bytes 1048592 | tf_op jit(solution)/shard_map/psum | solution.py:14
  668.8 2.3 constant_dynamic-update-slice_fusion.1
  672.9 3.7 fusion.5
  676.6 147.3 %all-reduce.16.cloned.1.call-done = f32[1,512,512]{1,2,0:T(8,128)} async-done(((f32[1,512,512]{1,2,0:T(8,128)}), f32[1,512,512]{1,2,0:T(8,128)}) %all-reduce.16.cloned.1.call-update) | async-done | bytes 1048592 | tf_op jit(solution)/shard_map/psum | solution.py:14
  824.0 2.3 constant_dynamic-update-slice_fusion
  826.2 5.2 copy.20
  (40 shorter events, 10.6 us)
Async XLA Ops:
  8.0 1.8 copy-start
  8.0 48.1 %all-gather.2.cloned.1.call-start = ((), (), s32[]{:S(2)}) async-start(), calls=%async_computation.1 | async-start | bytes 1179648 | tf_op jit(solution)/shard_map/all_gather | solution.py:49
  8.7 199.6 %all-reduce.8.cloned.1.call-start = ((), (), s32[]{:S(2)}) async-start(), calls=%async_computation | async-start | bytes 8388608 | tf_op jit(solution)/shard_map/psum | solution.py:46
  9.8 4.3 copy-start.6
  12.8 1.3 copy-start.8
  14.2 5.6 copy-start.7
  41.1 0.7 copy-start.5
  41.1 2.0 copy-start.3
  41.1 171.1 %copy-start.4 = (s32[4,2]{0,1:T(2,128)S(1)}, s32[4,2]{0,1:T(2,128)}, u32[]{:S(2)}) copy-start(s32[4,2]{0,1:T(2,128)} %param.25) | copy-start | bytes 100
  41.1 318.5 %all-reduce.10.cloned.1.call-start = ((), (), s32[]{:S(2)}) async-start(), calls=%async_computation.2 | async-start | bytes 2097152 | tf_op jit(solution)/shard_map/psum | solution.py:14
  56.1 303.5 %copy-start.2 = (bf16[512,512]{1,0:T(8,128)(2,1)}, bf16[512,512]{1,0:T(8,128)(2,1)S(1)}, u32[]{:S(2)}) copy-start(bf16[512,512]{1,0:T(8,128)(2,1)S(1)} %all_gather.7) | copy-start | bytes 1572868
  212.1 301.6 %all-reduce.12.cloned.1.call-start = ((), (), s32[]{:S(2)}) async-start(), calls=%async_computation.3 | async-start | bytes 2097152 | tf_op jit(solution)/shard_map/psum | solution.py:14
  359.6 10.0 %copy-start.1 = (f32[1,512,512]{1,2,0:T(8,128)S(1)}, f32[1,512,512]{1,2,0:T(8,128)}, u32[]{:S(2)}) copy-start(f32[1,512,512]{1,2,0:T(8,128)} %all-reduce.10.cloned.1.call-done) | copy-start | bytes 3145732
  366.4 302.4 %all-reduce.14.cloned.1.call-start = ((), (), s32[]{:S(2)}) async-start(), calls=%async_computation.4 | async-start | bytes 2097152 | tf_op jit(solution)/shard_map/psum | solution.py:14
  521.5 302.5 %all-reduce.16.cloned.1.call-start = ((), (), s32[]{:S(2)}) async-start(), calls=%async_computation.5 | async-start | bytes 2097152 | tf_op jit(solution)/shard_map/psum | solution.py:14
Sparse Core Ops, SparseCore 0:
  10.7 27.3 all-gather.1
Sparse Core Ops, SparseCore 1:
  41.2 167.1 all-reduce.7
  212.2 147.3 all-reduce.9
  366.5 147.2 all-reduce.11
  521.6 147.2 all-reduce.13
  676.7 147.2 all-reduce.15
where the time goes:
time: 842 us; the launch traced here: 841 us
  waiting for transfers between devices  730 us (87%)
  local copies, waits for them, and re-layouts  33.2 us (4%)
  between operations  25.6 us (3%)
  matrix products  20.7 us (2%)
  other arithmetic  18 us (2%)
  blocking collectives  13 us (2%)
    psum x4, waiting for transfers between devices, from_root(): return lax.psum(jnp.where(mine, shard, jnp.zeros_like(shard)), axis)  577 us
    psum x1, waiting for transfers between devices, per_device(): totals = lax.psum(terms, 'row')  152 us
  transfers between devices with their start and end apart: 6, of which 5 were waited for; matrix products, arithmetic and copies ran while one was open for 4% of the time, Pallas kernels for 0%

commit v1 on v0

v1 whole, which is shorter than its diff:
```python
import jax
import jax.numpy as jnp
from jax import lax
from jax.sharding import PartitionSpec as P

STEPS = 4
LINKS = 2
PAIR = 2


def gather_row(x, n_row):
    spread = jnp.broadcast_to(x[None], (n_row,) + x.shape)
    return lax.all_to_all(spread, "row", 0, 0, tiled=False)


def per_device(
    sub_source,
    sub_inverse,
    coupling,
    update_lists,
    sep_source,
    sep_inverse,
    sep_lower,
    factor_owner_slots,
    sep_links,
):
    n_row = lax.psum(1, "row")
    n_src = lax.psum(1, "src")
    cols = sub_source.shape[1]
    local_rows = sep_source.shape[0]
    block = sep_inverse.shape[1]
    span = PAIR * n_src
    my_row = lax.axis_index("row")

    sub_field = jnp.dot(
        sub_inverse, sub_source.astype(jnp.bfloat16), preferred_element_type=jnp.float32
    )
    rounded = sub_field.astype(jnp.bfloat16)
    updates = jnp.einsum(
        "lmf,ft->lmt", coupling[0], rounded, preferred_element_type=jnp.float32
    )
    per_dest = updates.reshape(LINKS, n_src, n_row, PAIR, cols).transpose(2, 0, 1, 3, 4)
    per_dest = per_dest.reshape(n_row, LINKS * span, cols)
    src_rows = sep_source.reshape(n_row, PAIR, cols)
    lists = jnp.zeros((cols,), jnp.float32).at[:LINKS].set(update_lists[0].astype(jnp.float32))
    lists = jnp.broadcast_to(lists[None, None], (n_row, 1, cols))
    payload = jnp.concatenate([per_dest, src_rows, lists], axis=1)
    got = lax.all_to_all(payload, "row", 0, 0, tiled=False)
    got_updates = got[:, : LINKS * span].reshape(n_row, LINKS, span, cols)
    got_src = got[:, LINKS * span : LINKS * span + PAIR].reshape(STEPS, span, cols)
    got_lists = got[:, LINKS * span + PAIR, :LINKS]
    pending = []
    for k in range(STEPS):
        hit = (got_lists == k)[:, :, None, None]
        pending.append(got_src[k] - jnp.sum(jnp.where(hit, got_updates, 0.0), axis=(0, 1)))

    factors = jnp.concatenate([sep_lower, sep_inverse], axis=1)
    width = factors.shape[1]
    slot_rows = lax.all_to_all(factors.reshape(n_row, PAIR, width), "row", 0, 0, tiled=False)
    owned = slot_rows[factor_owner_slots]
    owned = lax.all_gather(owned, "src", axis=0, tiled=False)
    owned = owned.transpose(1, 0, 2, 3).reshape(STEPS, span, width)
    lower_rows = owned[:, :, : LINKS * block]
    inverse_rows = owned[:, :, LINKS * block :]
    inverse_all = lax.all_gather(inverse_rows, "row", axis=0, tiled=False)
    inverse_full = inverse_all.reshape(n_row, STEPS, n_src, PAIR, block)
    inverse_full = inverse_full.transpose(1, 2, 0, 3, 4).reshape(STEPS, block, block)

    solved = jnp.zeros((STEPS, block, cols), jnp.float32)
    for k in range(STEPS):
        pieces = []
        for link_pos in range(LINKS):
            target = sep_links[k, link_pos]
            chosen = solved[jnp.maximum(target, 0)]
            pieces.append(jnp.where(target >= 0, chosen, 0.0).astype(jnp.bfloat16))
        stacked = jnp.concatenate(pieces, axis=0)
        residue = pending[k] - jnp.dot(
            lower_rows[k], stacked, preferred_element_type=jnp.float32
        )
        everyone = gather_row(residue.astype(jnp.bfloat16), n_row)
        everyone = everyone.reshape(n_row, n_src, PAIR, cols).transpose(1, 0, 2, 3)
        full_residue = everyone.reshape(block, cols)
        result = jnp.dot(inverse_full[k], full_residue, preferred_element_type=jnp.float32)
        solved = solved.at[k].set(result)
    whole_field = solved.reshape(STEPS * block, cols)
    own_rows = lax.dynamic_slice_in_dim(whole_field, my_row * local_rows, local_rows, 0)
    return (sub_field, own_rows)


def solution(mesh):
    return jax.shard_map(
        per_device,
        mesh=mesh,
        in_specs=(
            P("row", "src"),
            P("row", None),
            P("row", None, None, None),
            P("row", None),
            P("row", "src"),
            P(("row", "src"), None),
            P(("row", "src"), None),
            P(),
            P(),
        ),
        out_specs=(P("row", "src"), P("row", "src")),
        check_vma=False,
    )
```

time: 842 us -> 260 us (0.31)
  waiting for transfers between devices: 730 us -> 102 us
  starting transfers between devices: 0.26 us -> 43.4 us
  local copies, waits for them, and re-layouts: 33.2 us -> 51.8 us
    psum x5 -> x0, waiting for transfers between devices: 729 us -> none  [the longest x4 577 us: from_root(): return lax.psum(jnp.where(mine, shard, jnp.zeros_like(shard)), axis)]
    all_to_all x0 -> x6, waiting for transfers between devices: none -> 81.3 us  [the longest x1 49.8 us: per_device(): got = lax.all_to_all(payload, 'row', 0, 0, tiled=False)]
    all_to_all x0 -> x6, starting transfers between devices: none -> 43.4 us  [the longest x4 22 us: gather_row(): return lax.all_to_all(spread, 'row', 0, 0, tiled=False)]
    all_gather x1, waiting for transfers between devices: 0.01 us -> 20.8 us  [per_device(): inverse_all = lax.all_gather(inverse_rows, 'row', axis=0, tiled=False)]
    reshape x1 -> x10, local copies, waits for them, and re-layouts: 5.43 us -> 20.8 us  [the longest x2 7.9 us: per_device(): inverse_full = inverse_all.reshape(n_row, STEPS, n_src, PAIR, block)]
    scatter x5 -> x2, local copies, waits for them, and re-layouts: 14.7 us -> 2.51 us  [the longest x1 2.51 us: per_device(): solved = solved.at[k].set(result)]
    dot_general x5 -> x9, matrix products: 17.7 us -> 12.7 us  [the longest x4 9.07 us: per_device(): jnp.dot(inverse_full[k], full_residue, preferred_element_type=jnp.float32)]
  transfers between devices with their start and end apart: 6 -> 7, of which waited for: 5 -> 5; matrix products, arithmetic and copies ran while one was open for 4% -> 19% of each run, Pallas kernels for 0% -> 0%
where the time goes in v1:
time: 260 us; the launch traced here: 258 us
  waiting for transfers between devices  102 us (39%)
  local copies, waits for them, and re-layouts  51.8 us (20%)
  starting transfers between devices  43.4 us (17%)
  between operations  21.8 us (8%)
  matrix products  15.7 us (6%)
  other arithmetic  12.1 us (5%)
  blocking collectives  11.6 us (4%)
    all_to_all x1, waiting for transfers between devices, per_device(): got = lax.all_to_all(payload, 'row', 0, 0, tiled=False)  49.8 us
    all_to_all x4, waiting for transfers between devices, gather_row(): return lax.all_to_all(spread, 'row', 0, 0, tiled=False)  31.4 us
    all_to_all x4, starting transfers between devices, gather_row(): return lax.all_to_all(spread, 'row', 0, 0, tiled=False)  22 us
    all_gather x1, waiting for transfers between devices, per_device(): inverse_all = lax.all_gather(inverse_rows, 'row', axis=0, tiled=False)  20.8 us
    all_gather x1, blocking collectives, per_device(): owned = lax.all_gather(owned, 'src', axis=0, tiled=False)  11.6 us
    all_to_all x1, starting transfers between devices, per_device(): lax.all_to_all(factors.reshape(n_row, PAIR, width), 'row', 0, 0, tiled=Fa...  11.3 us
    all_to_all x1, starting transfers between devices, per_device(): got = lax.all_to_all(payload, 'row', 0, 0, tiled=False)  10 us
    dot_general x4, matrix products, per_device(): jnp.dot(inverse_full[k], full_residue, preferred_element_type=jnp.float32)  9.07 us
  transfers between devices with their start and end apart: 7, of which 5 were waited for; matrix products, arithmetic and copies ran while one was open for 19% of the time, Pallas kernels for 0%

profile of v1, /device:TPU:16, one launch (start us, length us, event | category | flops | bytes accessed | tf_op | source)
XLA Modules:
  0.0 258.5 jit_solution(3832663980114977547)
XLA Ops:
  9.0 11.3 %all-to-all-start = ((bf16[32,2,1536]{2,1,0:T(2,128)(2,1)}), bf16[32,2,1536]{2,1,0:T(2,128)(2,1)S(1)}, u32[]{:S(2)}, u32[]{:S(2)}) async-start(bf16[32,2,1536]{2,1,0:T(2,128)(2,1)} %reshape.309), calls=%async_computation | async-start | bytes 393216 | tf_op jit(solution)/shard_map/all_to_all | solution.py:59
  21.3 3.0 %fusion.27 = f32[1024,512]{1,0:T(8,128)S(1)} fusion(bf16[1024,1024]{1,0:T(8,128)(2,1)S(1)} %copy-done, f32[1024,512]{1,0:T(8,128)} %param.19), kind=kOutput, calls=%fused_computation.46 | convolution fusion | flops 1074266112 | bytes 6291456 | tf_op jit(solution)/shard_map/dot_general | solution.py:35
  25.7 2.6 fusion.2
  28.2 3.5 %reshape.312 = f32[2,8,32,2,512]{4,3,2,1,0:T(2,128)} reshape(f32[2,512,512]{2,1,0:T(8,128)} %fusion.2) | data formatting | bytes 4194304 | tf_op jit(solution)/shard_map/reshape | solution.py:42
  31.7 4.1 %copy.102 = f32[32,2,8,2,512]{4,3,2,1,0:T(2,128)} copy(f32[32,2,8,2,512]{4,3,0,2,1:T(2,128)} %bitcast.110) | data formatting | bytes 4194304 | tf_op jit(solution)/shard_map/transpose | solution.py:42
  35.9 3.7 %reshape.313 = f32[32,32,512]{2,1,0:T(8,128)} reshape(f32[32,2,8,2,512]{4,3,2,1,0:T(2,128)} %copy.102) | data formatting | bytes 4194304 | tf_op jit(solution)/shard_map/reshape | solution.py:43
  39.6 3.5 %pad_maximum_fusion = f32[32,35,512]{2,1,0:T(8,128)} fusion(f32[32,1,512]{2,1,0:T(1,128)S(1)} %broadcast_in_dim.95, f32[32,2,512]{2,1,0:T(2,128)S(1)} %reshape.314, f32[32,32,512]{2,1,0:T(8,128)} %reshape.313), kind=kLoop, calls=%fused_computation.3 | loop fusion | flops 1146880 | bytes 4587520 | tf_op jit(solution)/shard_map/concatenate | solution.py:47
  43.1 10.0 %all-to-all-start.1 = ((f32[32,35,512]{2,1,0:T(8,128)}), f32[32,35,512]{2,1,0:T(8,128)}, u32[]{:S(2)}, u32[]{:S(2)}) async-start(f32[32,35,512]{2,1,0:T(8,128)} %pad_maximum_fusion), calls=%async_computation.1 | async-start | bytes 5242880 | tf_op jit(solution)/shard_map/all_to_all | solution.py:48
  53.8 11.6 %all-gather = bf16[32,2,1536]{2,1,0:T(2,128)(2,1)S(1)} all-gather(bf16[4,2,1536]{2,1,0:T(2,128)(2,1)S(1)} %gather_fusion), channel_id=2, replica_groups=mesh['row'=32,'src'=8] {'src'}, dimensions={0}, use_global_device_ids=true | all-gather | bytes 221184 | tf_op jit(solution)/shard_map/all_gather | solution.py:61
  66.4 49.8 %all-to-all-done.1 = f32[32,35,512]{2,1,0:T(8,128)} async-done(((f32[32,35,512]{2,1,0:T(8,128)}), f32[32,35,512]{2,1,0:T(8,128)}, u32[]{:S(2)}, u32[]{:S(2)}) %all-to-all-start.1) | async-done | bytes 2293792 | tf_op jit(solution)/shard_map/all_to_all | solution.py:48
  118.9 2.9 %select_reduce_fusion = (f32[32,512]{1,0:T(8,128)S(1)}, f32[32,512]{1,0:T(8,128)S(1)}, f32[32,512]{1,0:T(8,128)S(1)}, f32[32,512]{1,0:T(8,128)S(1)}) fusion(f32[32,35,512]{2,1,0:T(8,128)} %all-to-all-done.1, pred[32,32]{1,0:T(8,128)(4,1)S(1)} %copy.113, pred[32,32]{1,0:T(8,128)(4,1)S(1)} %copy.107, pred[32,32]{1,0:T(8,128)(4,1)S(1)} %copy.110, ...), kind=kLoop, calls=%fused_computation.7 | loop fusion | flops 4128768 | bytes 2363392 | tf_op jit(solution)/shard_map/reduce_sum | solution.py:55
  123.0 6.3 %all-to-all-start.2 = ((bf16[32,16,512]{2,1,0:T(8,128)(2,1)}), bf16[32,16,512]{2,1,0:T(8,128)(2,1)S(1)}, u32[]{:S(2)}, u32[]{:S(2)}) async-start(bf16[32,16,512]{2,1,0:T(8,128)(2,1)} %broadcast_in_dim.100), calls=%async_computation.2 | async-start | bytes 1048576 | tf_op jit(solution)/shard_map/all_to_all | solution.py:13
  133.7 20.8 %all-gather.4.cloned.1.call-done = bf16[128,16,512]{2,1,0:T(8,128)(2,1)} async-done(((bf16[4,16,512]{2,1,0:T(8,128)(2,1)}), bf16[128,16,512]{2,1,0:T(8,128)(2,1)}) %all-gather.4.cloned.1.call-update) | async-done | bytes 2097168 | tf_op jit(solution)/shard_map/all_gather | solution.py:65
  154.6 4.1 %reshape.311 = bf16[32,4,8,2,512]{4,3,2,1,0:T(2,128)(2,1)} reshape(bf16[128,16,512]{2,1,0:T(8,128)(2,1)} %all-gather.4.cloned.1.call-done) | data formatting | bytes 4194304 | tf_op jit(solution)/shard_map/reshape | solution.py:66
  158.7 3.8 %copy.136 = bf16[32,4,8,2,512]{4,3,0,2,1:T(2,128)(2,1)S(1)} copy(bf16[32,4,8,2,512]{4,3,2,1,0:T(2,128)(2,1)} %reshape.311) | data formatting | bytes 4194304 | tf_op jit(solution)/shard_map/reshape | solution.py:66
  162.5 2.5 fusion.46
  170.9 7.6 %all-to-all-start.3 = ((bf16[32,16,512]{2,1,0:T(8,128)(2,1)}), bf16[32,16,512]{2,1,0:T(8,128)(2,1)}, u32[]{:S(2)}, u32[]{:S(2)}) async-start(bf16[32,16,512]{2,1,0:T(8,128)(2,1)} %broadcast_in_dim.104), calls=%async_computation.3 | async-start | bytes 1048576 | tf_op jit(solution)/shard_map/all_to_all | solution.py:13
  183.0 2.5 scatter.19
  185.5 8.0 %all-to-all-done.3 = bf16[32,16,512]{2,1,0:T(8,128)(2,1)} async-done(((bf16[32,16,512]{2,1,0:T(8,128)(2,1)}), bf16[32,16,512]{2,1,0:T(8,128)(2,1)}, u32[]{:S(2)}, u32[]{:S(2)}) %all-to-all-start.3) | async-done | bytes 524320 | tf_op jit(solution)/shard_map/all_to_all | solution.py:13
  196.4 2.5 fusion.7
  201.8 4.0 %all-to-all-start.4 = ((bf16[32,16,512]{2,1,0:T(8,128)(2,1)}), bf16[32,16,512]{2,1,0:T(8,128)(2,1)S(1)}, u32[]{:S(2)}, u32[]{:S(2)}) async-start(bf16[32,16,512]{2,1,0:T(8,128)(2,1)} %broadcast_in_dim.108), calls=%async_computation.4 | async-start | bytes 1048576 | tf_op jit(solution)/shard_map/all_to_all | solution.py:13
  209.7 10.7 %all-to-all-done.4 = bf16[32,16,512]{2,1,0:T(8,128)(2,1)S(1)} async-done(((bf16[32,16,512]{2,1,0:T(8,128)(2,1)}), bf16[32,16,512]{2,1,0:T(8,128)(2,1)S(1)}, u32[]{:S(2)}, u32[]{:S(2)}) %all-to-all-start.4) | async-done | bytes 524320 | tf_op jit(solution)/shard_map/all_to_all | solution.py:13
  227.6 4.1 %all-to-all-start.5 = ((bf16[32,16,512]{2,1,0:T(8,128)(2,1)}), bf16[32,16,512]{2,1,0:T(8,128)(2,1)S(1)}, u32[]{:S(2)}, u32[]{:S(2)}) async-start(bf16[32,16,512]{2,1,0:T(8,128)(2,1)} %broadcast_in_dim.112), calls=%async_computation.5 | async-start | bytes 1048576 | tf_op jit(solution)/shard_map/all_to_all | solution.py:13
  233.0 12.8 %all-to-all-done.5 = bf16[32,16,512]{2,1,0:T(8,128)(2,1)S(1)} async-done(((bf16[32,16,512]{2,1,0:T(8,128)(2,1)}), bf16[32,16,512]{2,1,0:T(8,128)(2,1)S(1)}, u32[]{:S(2)}, u32[]{:S(2)}) %all-to-all-start.5) | async-done | bytes 524320 | tf_op jit(solution)/shard_map/all_to_all | solution.py:13
  (89 shorter events, 40.9 us)
Async XLA Ops:
  7.2 14.2 %copy-start = (bf16[1024,1024]{1,0:T(8,128)(2,1)S(1)}, bf16[1024,1024]{1,0:T(8,128)(2,1)}, u32[]{:S(2)}) copy-start(bf16[1024,1024]{1,0:T(8,128)(2,1)} %param.20) | copy-start | bytes 6291460
  9.0 34.1 %all-to-all-start = ((bf16[32,2,1536]{2,1,0:T(2,128)(2,1)}), bf16[32,2,1536]{2,1,0:T(2,128)(2,1)S(1)}, u32[]{:S(2)}, u32[]{:S(2)}) async-start(bf16[32,2,1536]{2,1,0:T(2,128)(2,1)} %reshape.309), calls=%async_computation | async-start | bytes 393216 | tf_op jit(solution)/shard_map/all_to_all | solution.py:59
  21.3 4.3 %copy-start.5 = (bf16[1,2,512,1024]{3,2,1,0:T(8,128)(2,1)S(1)}, bf16[1,2,512,1024]{3,2,1,0:T(8,128)(2,1)}, u32[]{:S(2)}) copy-start(bf16[1,2,512,1024]{3,2,1,0:T(8,128)(2,1)} %param.21) | copy-start | bytes 6291460
  24.3 1.3 copy-start.8
  35.9 3.7 %copy-start.6 = (s32[1,2]{1,0:T(1,128)S(1)}, s32[1,2]{1,0:T(1,128)}, u32[]{:S(2)}) copy-start(s32[1,2]{1,0:T(1,128)} %param.22) | copy-start | bytes 28
  43.1 10.1 %copy-start.7 = (s32[4]{0:T(128)S(1)}, s32[4]{0:T(128)}, u32[]{:S(2)}) copy-start(s32[4]{0:T(128)} %param.26) | copy-start | bytes 52
  43.1 73.1 %all-to-all-start.1 = ((f32[32,35,512]{2,1,0:T(8,128)}), f32[32,35,512]{2,1,0:T(8,128)}, u32[]{:S(2)}, u32[]{:S(2)}) async-start(f32[32,35,512]{2,1,0:T(8,128)} %pad_maximum_fusion), calls=%async_computation.1 | async-start | bytes 5242880 | tf_op jit(solution)/shard_map/all_to_all | solution.py:48
  53.1 101.4 %all-gather.4.cloned.1.call-start = ((), (), s32[]{:S(2)}) async-start(), calls=%async_computation.6 | async-start | bytes 2162688 | tf_op jit(solution)/shard_map/all_gather | solution.py:65
  118.8 10.4 %copy-start.4 = (s32[4,2]{0,1:T(2,128)S(1)}, s32[4,2]{0,1:T(2,128)}, u32[]{:S(2)}) copy-start(s32[4,2]{0,1:T(2,128)} %param.27) | copy-start | bytes 100
  123.0 43.0 %all-to-all-start.2 = ((bf16[32,16,512]{2,1,0:T(8,128)(2,1)}), bf16[32,16,512]{2,1,0:T(8,128)(2,1)S(1)}, u32[]{:S(2)}, u32[]{:S(2)}) async-start(bf16[32,16,512]{2,1,0:T(8,128)(2,1)} %broadcast_in_dim.100), calls=%async_computation.2 | async-start | bytes 1048576 | tf_op jit(solution)/shard_map/all_to_all | solution.py:13
  167.8 2.0 copy-start.2
  167.8 2.0 copy-start.3
  170.9 22.6 %all-to-all-start.3 = ((bf16[32,16,512]{2,1,0:T(8,128)(2,1)}), bf16[32,16,512]{2,1,0:T(8,128)(2,1)}, u32[]{:S(2)}, u32[]{:S(2)}) async-start(bf16[32,16,512]{2,1,0:T(8,128)(2,1)} %broadcast_in_dim.104), calls=%async_computation.3 | async-start | bytes 1048576 | tf_op jit(solution)/shard_map/all_to_all | solution.py:13
  185.5 10.9 %copy-start.1 = (bf16[512,512]{1,0:T(8,128)(2,1)S(1)}, bf16[512,512]{1,0:T(8,128)(2,1)}, u32[]{:S(2)}) copy-start(bf16[512,512]{1,0:T(8,128)(2,1)} %squeeze.59) | copy-start | bytes 1572868
  201.8 18.6 %all-to-all-start.4 = ((bf16[32,16,512]{2,1,0:T(8,128)(2,1)}), bf16[32,16,512]{2,1,0:T(8,128)(2,1)S(1)}, u32[]{:S(2)}, u32[]{:S(2)}) async-start(bf16[32,16,512]{2,1,0:T(8,128)(2,1)} %broadcast_in_dim.108), calls=%async_computation.4 | async-start | bytes 1048576 | tf_op jit(solution)/shard_map/all_to_all | solution.py:13
  227.6 18.1 %all-to-all-start.5 = ((bf16[32,16,512]{2,1,0:T(8,128)(2,1)}), bf16[32,16,512]{2,1,0:T(8,128)(2,1)S(1)}, u32[]{:S(2)}, u32[]{:S(2)}) async-start(bf16[32,16,512]{2,1,0:T(8,128)(2,1)} %broadcast_in_dim.112), calls=%async_computation.5 | async-start | bytes 1048576 | tf_op jit(solution)/shard_map/all_to_all | solution.py:13
Sparse Core Ops, SparseCore 0:
  66.3 88.2 all-gather.3

commit v2 on v1

v2 whole, which is shorter than its diff:
```python
import jax
import jax.numpy as jnp
from jax import lax
from jax.sharding import PartitionSpec as P

STEPS = 4
LINKS = 2
PAIR = 2


def gather_row(x, n_row):
    spread = jnp.broadcast_to(x[None], (n_row,) + x.shape)
    return lax.all_to_all(spread, "row", 0, 0, tiled=False)


def per_device(
    sub_source,
    sub_inverse,
    coupling,
    update_lists,
    sep_source,
    sep_inverse,
    sep_lower,
    factor_owner_slots,
    sep_links,
):
    n_row = lax.psum(1, "row")
    n_src = lax.psum(1, "src")
    cols = sub_source.shape[1]
    local_rows = sep_source.shape[0]
    block = sep_inverse.shape[1]
    span = PAIR * n_src
    my_row = lax.axis_index("row")

    factors = jnp.concatenate([sep_lower, sep_inverse], axis=1)
    width = factors.shape[1]
    slot_rows = lax.all_to_all(factors.reshape(n_row, PAIR, width), "row", 0, 0, tiled=False)
    owned = slot_rows[factor_owner_slots]
    owned = owned.reshape(STEPS, PAIR, width // block, n_src, n_row, PAIR)
    owned = owned.transpose(0, 1, 2, 4, 3, 5).reshape(STEPS, PAIR, width)
    owned = lax.all_gather(owned, "src", axis=0, tiled=False)
    owned, sub_source = lax.optimization_barrier((owned, sub_source))
    owned = owned.transpose(1, 0, 2, 3).reshape(STEPS, span, width)
    lower_rows = owned[:, :, : LINKS * block]
    inverse_rows = owned[:, :, LINKS * block :]
    inverse_all = lax.all_gather(inverse_rows, "row", axis=0, tiled=False)

    sub_field = jnp.dot(
        sub_inverse, sub_source.astype(jnp.bfloat16), preferred_element_type=jnp.float32
    )
    rounded = sub_field.astype(jnp.bfloat16)
    updates = jnp.einsum(
        "lmf,ft->lmt", coupling[0], rounded, preferred_element_type=jnp.float32
    )
    per_dest = updates.astype(jnp.bfloat16).reshape(LINKS, n_src, n_row, PAIR, cols)
    per_dest = per_dest.transpose(2, 0, 1, 3, 4).reshape(n_row, LINKS * span, cols)
    src_rows = sep_source.astype(jnp.bfloat16).reshape(n_row, PAIR, cols)
    lists = jnp.zeros((cols,), jnp.bfloat16).at[:LINKS].set(update_lists[0].astype(jnp.bfloat16))
    lists = jnp.broadcast_to(lists[None, None], (n_row, 1, cols))
    payload = jnp.concatenate([per_dest, src_rows, lists], axis=1)
    got = lax.all_to_all(payload, "row", 0, 0, tiled=False).astype(jnp.float32)
    got_updates = got[:, : LINKS * span].reshape(n_row, LINKS, span, cols)
    got_src = got[:, LINKS * span : LINKS * span + PAIR].reshape(STEPS, span, cols)
    got_lists = got[:, LINKS * span + PAIR, :LINKS]
    pending = []
    for k in range(STEPS):
        hit = (got_lists == k)[:, :, None, None]
        pending.append(got_src[k] - jnp.sum(jnp.where(hit, got_updates, 0.0), axis=(0, 1)))

    solved = jnp.zeros((STEPS, block, cols), jnp.float32)
    for k in range(STEPS):
        pieces = []
        for link_pos in range(LINKS):
            target = sep_links[k, link_pos]
            chosen = solved[jnp.maximum(target, 0)]
            pieces.append(jnp.where(target >= 0, chosen, 0.0).astype(jnp.bfloat16))
        stacked = jnp.concatenate(pieces, axis=0)
        residue = pending[k] - jnp.dot(
            lower_rows[k], stacked, preferred_element_type=jnp.float32
        )
        everyone = gather_row(residue.astype(jnp.bfloat16), n_row)
        full_residue = everyone.reshape(block, cols)
        inverse = inverse_all[:, k].reshape(block, block)
        result = jnp.dot(inverse, full_residue, preferred_element_type=jnp.float32)
        solved = solved.at[k].set(result)
    blocks_per = block // local_rows
    whole_field = solved.reshape(STEPS, n_row, n_src, PAIR, cols)
    own_rows = lax.dynamic_slice(
        whole_field,
        (my_row // blocks_per, 0, my_row % blocks_per, 0, 0),
        (1, n_row, 1, PAIR, cols),
    ).reshape(local_rows, cols)
    return (sub_field, own_rows)


def solution(mesh):
    return jax.shard_map(
        per_device,
        mesh=mesh,
        in_specs=(
            P("row", "src"),
            P("row", None),
            P("row", None, None, None),
            P("row", None),
            P("row", "src"),
            P(("row", "src"), None),
            P(("row", "src"), None),
            P(),
            P(),
        ),
        out_specs=(P("row", "src"), P("row", "src")),
        check_vma=False,
    )
```

time: 260 us -> 251 us (0.965)
  other arithmetic: 12.1 us -> 27.2 us
  local copies, waits for them, and re-layouts: 51.8 us -> 43.5 us
  waiting for transfers between devices: 102 us -> 94 us
  starting transfers between devices: 43.4 us -> 36.1 us
    all_to_all x1, waiting for transfers between devices: 49.8 us -> 31.2 us  [per_device(): got = lax.all_to_all(payload, 'row', 0, 0, tiled=False).astype(jnp.float32)]
    reshape x9 -> x5, local copies, waits for them, and re-layouts: 20.1 us -> 9.56 us  [the longest x1 5.85 us: per_device(): whole_field = solved.reshape(STEPS, n_row, n_src, PAIR, cols)]
    all_to_all x1, waiting for transfers between devices: 0.01 us -> 9.34 us  [per_device(): lax.all_to_all(factors.reshape(n_row, PAIR, width), 'row', 0, 0, tiled=Fa...]
    convert_element_type x1 -> x3, other arithmetic: 0.01 us -> 8.54 us  [the longest x1 6.96 us: per_device(): got = lax.all_to_all(payload, 'row', 0, 0, tiled=False).astype(jnp.float32)]
    reduce_sum x5, other arithmetic: 3.53 us -> 11 us  [per_device(): jnp.sum(jnp.where(hit, got_updates, 0.0), axis=(0, 1))]
    all_to_all x1, starting transfers between devices: 10 us -> 3.95 us  [per_device(): got = lax.all_to_all(payload, 'row', 0, 0, tiled=False).astype(jnp.float32)]
    squeeze x4 -> x0, local copies, waits for them, and re-layouts: 5.52 us -> none  [per_device(): inverse_full[k]]
    unnamed x19, local copies, waits for them, and re-layouts: 1.43 us -> 5.08 us
  transfers between devices with their start and end apart: 7 -> 7, of which waited for: 5 -> 6; matrix products, arithmetic and copies ran while one was open for 19% -> 17% of each run, Pallas kernels for 0% -> 0%
where the time goes in v2:
time: 251 us; the launch traced here: 250 us
  waiting for transfers between devices  94 us (37%)
  local copies, waits for them, and re-layouts  43.5 us (17%)
  starting transfers between devices  36.1 us (14%)
  other arithmetic  27.2 us (11%)
  between operations  21.9 us (9%)
  matrix products  14.5 us (6%)
  blocking collectives  12.6 us (5%)
    all_to_all x4, waiting for transfers between devices, gather_row(): return lax.all_to_all(spread, 'row', 0, 0, tiled=False)  34 us
    all_to_all x1, waiting for transfers between devices, per_device(): got = lax.all_to_all(payload, 'row', 0, 0, tiled=False).astype(jnp.float32)  31.2 us
    all_to_all x4, starting transfers between devices, gather_row(): return lax.all_to_all(spread, 'row', 0, 0, tiled=False)  20.6 us
    all_gather x1, waiting for transfers between devices, per_device(): inverse_all = lax.all_gather(inverse_rows, 'row', axis=0, tiled=False)  19.4 us
    all_gather x1, blocking collectives, per_device(): owned = lax.all_gather(owned, 'src', axis=0, tiled=False)  12.6 us
    all_to_all x1, starting transfers between devices, per_device(): lax.all_to_all(factors.reshape(n_row, PAIR, width), 'row', 0, 0, tiled=Fa...  11.3 us
    reduce_sum x5, other arithmetic, per_device(): jnp.sum(jnp.where(hit, got_updates, 0.0), axis=(0, 1))  11 us
    all_to_all x1, waiting for transfers between devices, per_device(): lax.all_to_all(factors.reshape(n_row, PAIR, width), 'row', 0, 0, tiled=Fa...  9.34 us
  transfers between devices with their start and end apart: 7, of which 6 were waited for; matrix products, arithmetic and copies ran while one was open for 17% of the time, Pallas kernels for 0%

profile of v2, /device:TPU:16, one launch (start us, length us, event | category | flops | bytes accessed | tf_op | source)
XLA Modules:
  0.0 249.9 jit_solution(17284632337545258972)
XLA Ops:
  9.0 11.3 %all-to-all-start = ((bf16[32,2,1536]{2,1,0:T(2,128)(2,1)}), bf16[32,2,1536]{2,1,0:T(2,128)(2,1)S(1)}, u32[]{:S(2)}, u32[]{:S(2)}) async-start(bf16[32,2,1536]{2,1,0:T(2,128)(2,1)} %reshape.291), calls=%async_computation | async-start | bytes 393216 | tf_op jit(solution)/shard_map/all_to_all | solution.py:37
  22.7 9.3 %all-to-all-done = bf16[32,2,1536]{2,1,0:T(2,128)(2,1)S(1)} async-done(((bf16[32,2,1536]{2,1,0:T(2,128)(2,1)}), bf16[32,2,1536]{2,1,0:T(2,128)(2,1)S(1)}, u32[]{:S(2)}, u32[]{:S(2)}) %all-to-all-start) | async-done | bytes 196640 | tf_op jit(solution)/shard_map/all_to_all | solution.py:37
  35.9 12.6 %all_gather.9 = bf16[8,4,2,1536]{3,1,2,0:T(4,128)(2,1)} all-gather(bf16[1,4,2,1536]{3,1,2,0:T(4,128)(2,1)S(1)} %copy.102), channel_id=1, replica_groups=mesh['row'=32,'src'=8] {'src'}, dimensions={0}, use_global_device_ids=true | all-gather | bytes 221184 | tf_op jit(solution)/shard_map/all_gather | solution.py:41
  48.5 3.0 %convolution_bitcast_fusion = f32[1024,512]{0,1:T(8,128)S(1)} fusion(bf16[1024,1024]{1,0:T(8,128)(2,1)S(1)} %copy-done, f32[1024,512]{1,0:T(8,128)} %param.19), kind=kOutput, calls=%fused_computation.9 | convolution fusion | flops 1074266112 | bytes 6291456 | tf_op jit(solution)/shard_map/dot_general | solution.py:48
  61.5 4.0 %all-to-all-start.1 = ((bf16[32,35,512]{2,1,0:T(8,128)(2,1)}), bf16[32,35,512]{2,1,0:T(8,128)(2,1)S(1)}, u32[]{:S(2)}, u32[]{:S(2)}) async-start(bf16[32,35,512]{2,1,0:T(8,128)(2,1)} %pad_maximum_fusion), calls=%async_computation.1 | async-start | bytes 2621440 | tf_op jit(solution)/shard_map/all_to_all | solution.py:61
  69.3 31.2 %all-to-all-done.1 = bf16[32,35,512]{2,1,0:T(8,128)(2,1)S(1)} async-done(((bf16[32,35,512]{2,1,0:T(8,128)(2,1)}), bf16[32,35,512]{2,1,0:T(8,128)(2,1)S(1)}, u32[]{:S(2)}, u32[]{:S(2)}) %all-to-all-start.1) | async-done | bytes 1146912 | tf_op jit(solution)/shard_map/all_to_all | solution.py:61
  100.5 3.4 %copy.106 = bf16[32,35,512]{0,2,1:T(8,128)(2,1)} copy(bf16[32,35,512]{2,1,0:T(8,128)(2,1)S(1)} %all-to-all-done.1) | data formatting | bytes 2293760 | tf_op jit(solution)/shard_map/all_to_all | solution.py:61
  104.0 7.0 %convert_element_type.84 = f32[32,35,512]{0,2,1:T(8,128)} convert(bf16[32,35,512]{0,2,1:T(8,128)(2,1)} %copy.106) | non-fusion elementwise | flops 573440 | bytes 3440640 | tf_op jit(solution)/shard_map/convert_element_type | solution.py:61
  110.9 2.7 %fusion.47 = (f32[8,2,512]{0,2,1:T(8,128)}, f32[8,2,512]{0,2,1:T(8,128)}, f32[8,2,512]{0,2,1:T(8,128)S(1)}, f32[8,2,512]{0,2,1:T(8,128)S(1)}) fusion(bf16[32,35,512]{0,2,1:T(8,128)(2,1)} %copy.106), kind=kLoop, calls=%fused_computation.74 | loop fusion | bytes 262144 | tf_op jit(solution)/shard_map/slice | solution.py:68
  114.6 11.0 %select_reduce_fusion = (f32[32,512]{1,0:T(8,128)S(1)}, f32[32,512]{1,0:T(8,128)S(1)}, f32[32,512]{1,0:T(8,128)S(1)}, f32[32,512]{1,0:T(8,128)S(1)}) fusion(f32[32,35,512]{0,2,1:T(8,128)} %convert_element_type.84, pred[32,32]{0,1:T(8,128)(4,1)S(1)} %bitcast.128, pred[32,32]{0,1:T(8,128)(4,1)S(1)} %bitcast.126, pred[32,32]{0,1:T(8,128)(4,1)S(1)} %bitcast.127, ...), kind=kLoop, calls=%fused_computation.1 | loop fusion | flops 4128768 | bytes 2363392 | tf_op jit(solution)/shard_map/reduce_sum | solution.py:68
  126.8 5.7 %all-to-all-start.2 = ((bf16[32,16,512]{2,1,0:T(8,128)(2,1)}), bf16[32,16,512]{2,1,0:T(8,128)(2,1)S(1)}, u32[]{:S(2)}, u32[]{:S(2)}) async-start(bf16[32,16,512]{2,1,0:T(8,128)(2,1)} %broadcast_in_dim.103), calls=%async_computation.2 | async-start | bytes 1048576 | tf_op jit(solution)/shard_map/all_to_all | solution.py:13
  136.0 19.4 %all-gather.3.cloned.1.call-done = bf16[128,16,512]{2,1,0:T(8,128)(2,1)} async-done(((bf16[4,16,512]{2,1,0:T(8,128)(2,1)}), bf16[128,16,512]{2,1,0:T(8,128)(2,1)}) %all-gather.3.cloned.1.call-update) | async-done | bytes 2097168 | tf_op jit(solution)/shard_map/all_gather | solution.py:46
  155.4 2.9 %fusion.48 = (bf16[32,1,16,512]{3,2,1,0:T(8,128)(2,1)}, bf16[32,1,16,512]{3,2,1,0:T(8,128)(2,1)}, bf16[32,1,16,512]{3,2,1,0:T(8,128)(2,1)}, bf16[32,1,16,512]{3,2,1,0:T(8,128)(2,1)}) fusion(bf16[32,4,16,512]{3,2,1,0:T(8,128)(2,1)} %bitcast.111), kind=kLoop, calls=%fused_computation.75 | loop fusion | bytes 4194304 | tf_op jit(solution)/shard_map/slice | solution.py:83
  162.2 6.2 %all-to-all-start.3 = ((bf16[32,16,512]{2,1,0:T(8,128)(2,1)}), bf16[32,16,512]{2,1,0:T(8,128)(2,1)}, u32[]{:S(2)}, u32[]{:S(2)}) async-start(bf16[32,16,512]{2,1,0:T(8,128)(2,1)} %broadcast_in_dim.107), calls=%async_computation.3 | async-start | bytes 1048576 | tf_op jit(solution)/shard_map/all_to_all | solution.py:13
  172.1 2.5 %scatter.19 = f32[4,512,512]{2,1,0:T(8,128)} pad(f32[1,512,512]{2,1,0:T(8,128)S(1)} %convolution_bitcast_fusion.4, f32[]{:T(128)} %constant.190.clone.1), padding=0_3x0_0x0_0 | pad | bytes 5242884 | tf_op jit(solution)/shard_map/scatter | solution.py:85
  174.6 9.5 %all-to-all-done.3 = bf16[32,16,512]{2,1,0:T(8,128)(2,1)} async-done(((bf16[32,16,512]{2,1,0:T(8,128)(2,1)}), bf16[32,16,512]{2,1,0:T(8,128)(2,1)}, u32[]{:S(2)}, u32[]{:S(2)}) %all-to-all-start.3) | async-done | bytes 524320 | tf_op jit(solution)/shard_map/all_to_all | solution.py:13
  184.1 2.7 %fusion.10 = f32[4,512,512]{2,1,0:T(8,128)} fusion(f32[4,512,512]{2,1,0:T(8,128)} %scatter.19, bf16[512,512]{1,0:T(8,128)(2,1)} %bitcast.117, bf16[512,512]{1,0:T(8,128)(2,1)} %bitcast.29), kind=kOutput, calls=%fused_computation.17 | convolution fusion | flops 268435456 | bytes 2097152 | tf_op jit(solution)/shard_map/dot_general | solution.py:84
  189.7 4.4 %all-to-all-start.4 = ((bf16[32,16,512]{2,1,0:T(8,128)(2,1)}), bf16[32,16,512]{2,1,0:T(8,128)(2,1)S(1)}, u32[]{:S(2)}, u32[]{:S(2)}) async-start(bf16[32,16,512]{2,1,0:T(8,128)(2,1)} %broadcast_in_dim.111), calls=%async_computation.4 | async-start | bytes 1048576 | tf_op jit(solution)/shard_map/all_to_all | solution.py:13
  196.8 12.4 %all-to-all-done.4 = bf16[32,16,512]{2,1,0:T(8,128)(2,1)S(1)} async-done(((bf16[32,16,512]{2,1,0:T(8,128)(2,1)}), bf16[32,16,512]{2,1,0:T(8,128)(2,1)S(1)}, u32[]{:S(2)}, u32[]{:S(2)}) %all-to-all-start.4) | async-done | bytes 524320 | tf_op jit(solution)/shard_map/all_to_all | solution.py:13
  209.2 2.5 fusion.9
  214.6 4.4 %all-to-all-start.5 = ((bf16[32,16,512]{2,1,0:T(8,128)(2,1)}), bf16[32,16,512]{2,1,0:T(8,128)(2,1)S(1)}, u32[]{:S(2)}, u32[]{:S(2)}) async-start(bf16[32,16,512]{2,1,0:T(8,128)(2,1)} %broadcast_in_dim.115), calls=%async_computation.5 | async-start | bytes 1048576 | tf_op jit(solution)/shard_map/all_to_all | solution.py:13
  219.0 2.9 %copy.111 = f32[1024,512]{1,0:T(8,128)} copy(f32[1024,512]{0,1:T(8,128)} %copy-done.1) | data formatting | bytes 4194304
  222.0 12.1 %all-to-all-done.5 = bf16[32,16,512]{2,1,0:T(8,128)(2,1)S(1)} async-done(((bf16[32,16,512]{2,1,0:T(8,128)(2,1)}), bf16[32,16,512]{2,1,0:T(8,128)(2,1)S(1)}, u32[]{:S(2)}, u32[]{:S(2)}) %all-to-all-start.5) | async-done | bytes 524320 | tf_op jit(solution)/shard_map/all_to_all | solution.py:13
  235.5 5.9 %reshape.305 = f32[4,32,8,2,512]{4,3,2,1,0:T(2,128)} reshape(f32[4,512,512]{2,1,0:T(8,128)} %fusion.8) | data formatting | bytes 8388608 | tf_op jit(solution)/shard_map/reshape | solution.py:87
  (77 shorter events, 39.1 us)
Async XLA Ops:
  7.2 41.4 %copy-start = (bf16[1024,1024]{1,0:T(8,128)(2,1)S(1)}, bf16[1024,1024]{1,0:T(8,128)(2,1)}, u32[]{:S(2)}) copy-start(bf16[1024,1024]{1,0:T(8,128)(2,1)} %param.20) | copy-start | bytes 6291460
  9.0 23.0 %all-to-all-start = ((bf16[32,2,1536]{2,1,0:T(2,128)(2,1)}), bf16[32,2,1536]{2,1,0:T(2,128)(2,1)S(1)}, u32[]{:S(2)}, u32[]{:S(2)}) async-start(bf16[32,2,1536]{2,1,0:T(2,128)(2,1)} %reshape.291), calls=%async_computation | async-start | bytes 393216 | tf_op jit(solution)/shard_map/all_to_all | solution.py:37
  48.5 4.4 %copy-start.8 = (bf16[1,2,512,1024]{3,2,1,0:T(8,128)(2,1)S(1)}, bf16[1,2,512,1024]{3,2,1,0:T(8,128)(2,1)}, u32[]{:S(2)}) copy-start(bf16[1,2,512,1024]{3,2,1,0:T(8,128)(2,1)} %param.21) | copy-start | bytes 6291460
  51.6 1.3 copy-start.1
  61.5 39.0 %all-to-all-start.1 = ((bf16[32,35,512]{2,1,0:T(8,128)(2,1)}), bf16[32,35,512]{2,1,0:T(8,128)(2,1)S(1)}, u32[]{:S(2)}, u32[]{:S(2)}) async-start(bf16[32,35,512]{2,1,0:T(8,128)(2,1)} %pad_maximum_fusion), calls=%async_computation.1 | async-start | bytes 2621440 | tf_op jit(solution)/shard_map/all_to_all | solution.py:61
  65.5 89.9 %all-gather.3.cloned.1.call-start = ((), (), s32[]{:S(2)}) async-start(), calls=%async_computation.6 | async-start | bytes 2162688 | tf_op jit(solution)/shard_map/all_gather | solution.py:46
  114.5 11.1 %copy-start.6 = (bf16[1,16,1024]{2,0,1:T(2,128)(2,1)S(1)}, bf16[1,16,1024]{2,0,1:T(2,128)(2,1)}, u32[]{:S(2)}) copy-start(bf16[1,16,1024]{2,0,1:T(2,128)(2,1)} %get-tuple-element.107) | copy-start | bytes 98308
  125.6 6.9 %copy-start.7 = (s32[4,2]{0,1:T(2,128)S(1)}, s32[4,2]{0,1:T(2,128)}, u32[]{:S(2)}) copy-start(s32[4,2]{0,1:T(2,128)} %param.27) | copy-start | bytes 100
  126.8 31.4 %all-to-all-start.2 = ((bf16[32,16,512]{2,1,0:T(8,128)(2,1)}), bf16[32,16,512]{2,1,0:T(8,128)(2,1)S(1)}, u32[]{:S(2)}, u32[]{:S(2)}) async-start(bf16[32,16,512]{2,1,0:T(8,128)(2,1)} %broadcast_in_dim.103), calls=%async_computation.2 | async-start | bytes 1048576 | tf_op jit(solution)/shard_map/all_to_all | solution.py:13
  158.2 0.8 copy-start.2
  159.0 2.0 copy-start.5
  162.2 21.9 %all-to-all-start.3 = ((bf16[32,16,512]{2,1,0:T(8,128)(2,1)}), bf16[32,16,512]{2,1,0:T(8,128)(2,1)}, u32[]{:S(2)}, u32[]{:S(2)}) async-start(bf16[32,16,512]{2,1,0:T(8,128)(2,1)} %broadcast_in_dim.107), calls=%async_computation.3 | async-start | bytes 1048576 | tf_op jit(solution)/shard_map/all_to_all | solution.py:13
  188.6 8.1 %copy-start.3 = (f32[8,2,512]{0,2,1:T(8,128)S(1)}, f32[8,2,512]{0,2,1:T(8,128)}, u32[]{:S(2)}) copy-start(f32[8,2,512]{0,2,1:T(8,128)} %get-tuple-element.90) | copy-start | bytes 98308
  189.7 19.5 %all-to-all-start.4 = ((bf16[32,16,512]{2,1,0:T(8,128)(2,1)}), bf16[32,16,512]{2,1,0:T(8,128)(2,1)S(1)}, u32[]{:S(2)}, u32[]{:S(2)}) async-start(bf16[32,16,512]{2,1,0:T(8,128)(2,1)} %broadcast_in_dim.111), calls=%async_computation.4 | async-start | bytes 1048576 | tf_op jit(solution)/shard_map/all_to_all | solution.py:13
  214.6 19.4 %all-to-all-start.5 = ((bf16[32,16,512]{2,1,0:T(8,128)(2,1)}), bf16[32,16,512]{2,1,0:T(8,128)(2,1)S(1)}, u32[]{:S(2)}, u32[]{:S(2)}) async-start(bf16[32,16,512]{2,1,0:T(8,128)(2,1)} %broadcast_in_dim.115), calls=%async_computation.5 | async-start | bytes 1048576 | tf_op jit(solution)/shard_map/all_to_all | solution.py:13
  219.0 15.0 %copy-start.4 = (bf16[32,1,16,512]{3,2,1,0:T(8,128)(2,1)S(1)}, bf16[32,1,16,512]{3,2,1,0:T(8,128)(2,1)}, u32[]{:S(2)}) copy-start(bf16[32,1,16,512]{3,2,1,0:T(8,128)(2,1)} %get-tuple-element.98) | copy-start | bytes 1572868
Sparse Core Ops, SparseCore 0:
  69.5 85.8 all-gather.2

commit v3 on v1

--- a/solution.py
+++ b/solution.py
@@ -62,9 +62,20 @@
     owned = owned.transpose(1, 0, 2, 3).reshape(STEPS, span, width)
     lower_rows = owned[:, :, : LINKS * block]
     inverse_rows = owned[:, :, LINKS * block :]
-    inverse_all = lax.all_gather(inverse_rows, "row", axis=0, tiled=False)
-    inverse_full = inverse_all.reshape(n_row, STEPS, n_src, PAIR, block)
-    inverse_full = inverse_full.transpose(1, 2, 0, 3, 4).reshape(STEPS, block, block)
+    seg = block // n_src
+    inverse_rows = inverse_rows.reshape(STEPS, n_src, PAIR, block)
+    packed = jnp.concatenate(
+        [inverse_rows[:, s, :, : (s + 1) * seg].reshape(STEPS, -1) for s in range(n_src)], axis=1
+    )
+    packed = lax.all_gather(packed, "row", axis=0, tiled=False)
+    pieces, at = [], 0
+    for s in range(n_src):
+        size = PAIR * (s + 1) * seg
+        piece = packed[:, :, at : at + size].reshape(n_row, STEPS, PAIR, (s + 1) * seg)
+        pieces.append(jnp.pad(piece, ((0, 0), (0, 0), (0, 0), (0, block - (s + 1) * seg))))
+        at += size
+    inverse_full = jnp.stack(pieces, axis=0)
+    inverse_full = inverse_full.transpose(2, 0, 1, 3, 4).reshape(STEPS, block, block)
 
     solved = jnp.zeros((STEPS, block, cols), jnp.float32)
     for k in range(STEPS):

time: 260 us -> 283 us (1.088)
  local copies, waits for them, and re-layouts: 51.8 us -> 63.8 us
  waiting for transfers between devices: 102 us -> 110 us
  starting transfers between devices: 43.4 us -> 46.4 us
    all_gather x1, waiting for transfers between devices: 20.8 us -> 80.4 us  [per_device(): packed = lax.all_gather(packed, 'row', axis=0, tiled=False)]
    all_to_all x1, waiting for transfers between devices: 49.8 us -> 0.01 us  [per_device(): got = lax.all_to_all(payload, 'row', 0, 0, tiled=False)]
    unnamed x19 -> x51, local copies, waits for them, and re-layouts: 1.43 us -> 13 us
    reshape x2 -> x7, local copies, waits for them, and re-layouts: 7.9 us -> 4.09 us  [per_device(): packed[:, :, at:at + size].reshape(n_row, STEPS, PAIR, (s + 1) * seg)]
    all_to_all x4, starting transfers between devices: 22 us -> 25 us  [gather_row(): return lax.all_to_all(spread, 'row', 0, 0, tiled=False)]
  transfers between devices with their start and end apart: 7 -> 7, of which waited for: 5 -> 4; matrix products, arithmetic and copies ran while one was open for 19% -> 19% of each run, Pallas kernels for 0% -> 0%
where the time goes in v3:
time: 283 us; the launch traced here: 281 us
  waiting for transfers between devices  110 us (39%)
  local copies, waits for them, and re-layouts  63.8 us (23%)
  starting transfers between devices  46.4 us (16%)
  between operations  21.7 us (8%)
  matrix products  15.7 us (6%)
  other arithmetic  12.2 us (4%)
  blocking collectives  11.6 us (4%)
    all_gather x1, waiting for transfers between devices, per_device(): packed = lax.all_gather(packed, 'row', axis=0, tiled=False)  80.4 us
    all_to_all x4, waiting for transfers between devices, gather_row(): return lax.all_to_all(spread, 'row', 0, 0, tiled=False)  29.4 us
    all_to_all x4, starting transfers between devices, gather_row(): return lax.all_to_all(spread, 'row', 0, 0, tiled=False)  25 us
    unnamed x51, local copies, waits for them, and re-layouts  13 us
    all_gather x1, blocking collectives, per_device(): owned = lax.all_gather(owned, 'src', axis=0, tiled=False)  11.6 us
    all_to_all x1, starting transfers between devices, per_device(): lax.all_to_all(factors.reshape(n_row, PAIR, width), 'row', 0, 0, tiled=Fa...  11.3 us
    all_to_all x1, starting transfers between devices, per_device(): got = lax.all_to_all(payload, 'row', 0, 0, tiled=False)  10 us
    dot_general x4, matrix products, per_device(): jnp.dot(inverse_full[k], full_residue, preferred_element_type=jnp.float32)  9.07 us
  transfers between devices with their start and end apart: 7, of which 4 were waited for; matrix products, arithmetic and copies ran while one was open for 19% of the time, Pallas kernels for 0%

profile of v3, /device:TPU:16, one launch (start us, length us, event | category | flops | bytes accessed | tf_op | source)
XLA Modules:
  0.0 281.1 jit_solution(9826705303434385855)
XLA Ops:
  9.0 11.3 %all-to-all-start = ((bf16[32,2,1536]{2,1,0:T(2,128)(2,1)}), bf16[32,2,1536]{2,1,0:T(2,128)(2,1)S(1)}, u32[]{:S(2)}, u32[]{:S(2)}) async-start(bf16[32,2,1536]{2,1,0:T(2,128)(2,1)} %reshape.332), calls=%async_computation | async-start | bytes 393216 | tf_op jit(solution)/shard_map/all_to_all | solution.py:59
  21.4 3.0 %fusion.27 = f32[1024,512]{1,0:T(8,128)S(1)} fusion(bf16[1024,1024]{1,0:T(8,128)(2,1)S(1)} %copy-done, f32[1024,512]{1,0:T(8,128)} %param.19), kind=kOutput, calls=%fused_computation.45 | convolution fusion | flops 1074266112 | bytes 6291456 | tf_op jit(solution)/shard_map/dot_general | solution.py:35
  25.7 2.6 fusion.2
  28.3 3.4 %reshape.342 = f32[2,8,32,2,512]{4,3,2,1,0:T(2,128)} reshape(f32[2,512,512]{2,1,0:T(8,128)} %fusion.2) | data formatting | bytes 4194304 | tf_op jit(solution)/shard_map/reshape | solution.py:42
  31.7 4.1 %copy.112 = f32[32,2,8,2,512]{4,3,2,1,0:T(2,128)} copy(f32[32,2,8,2,512]{4,3,0,2,1:T(2,128)} %bitcast.146) | data formatting | bytes 4194304 | tf_op jit(solution)/shard_map/transpose | solution.py:42
  35.8 3.6 %reshape.343 = f32[32,32,512]{2,1,0:T(8,128)} reshape(f32[32,2,8,2,512]{4,3,2,1,0:T(2,128)} %copy.112) | data formatting | bytes 4194304 | tf_op jit(solution)/shard_map/reshape | solution.py:43
  39.5 3.5 %pad_maximum_fusion = f32[32,35,512]{2,1,0:T(8,128)} fusion(f32[32,1,512]{2,1,0:T(1,128)S(1)} %broadcast_in_dim.95, f32[32,2,512]{2,1,0:T(2,128)S(1)} %reshape.344, f32[32,32,512]{2,1,0:T(8,128)} %reshape.343), kind=kLoop, calls=%fused_computation.3 | loop fusion | flops 1146880 | bytes 4587520 | tf_op jit(solution)/shard_map/concatenate | solution.py:47
  43.1 10.0 %all-to-all-start.1 = ((f32[32,35,512]{2,1,0:T(8,128)}), f32[32,35,512]{2,1,0:T(8,128)}, u32[]{:S(2)}, u32[]{:S(2)}) async-start(f32[32,35,512]{2,1,0:T(8,128)} %pad_maximum_fusion), calls=%async_computation.1 | async-start | bytes 5242880 | tf_op jit(solution)/shard_map/all_to_all | solution.py:48
  53.8 11.6 %all-gather = bf16[32,2,1536]{2,1,0:T(2,128)(2,1)S(1)} all-gather(bf16[4,2,1536]{2,1,0:T(2,128)(2,1)S(1)} %gather_fusion), channel_id=2, replica_groups=mesh['row'=32,'src'=8] {'src'}, dimensions={0}, use_global_device_ids=true | all-gather | bytes 221184 | tf_op jit(solution)/shard_map/all_gather | solution.py:61
  70.5 80.4 %all-gather.5.cloned.1.call-done = bf16[32,4,4608]{2,1,0:T(4,128)(2,1)} async-done(((bf16[1,4,4608]{2,1,0:T(4,128)(2,1)}), bf16[32,4,4608]{2,1,0:T(4,128)(2,1)}) %all-gather.5.cloned.1.call-update) | async-done | bytes 1179664 | tf_op jit(solution)/shard_map/all_gather | solution.py:70
  157.4 3.6 %select_reduce_fusion = (f32[32,512]{1,0:T(8,128)S(1)}, f32[32,512]{1,0:T(8,128)}, f32[32,512]{1,0:T(8,128)}, f32[32,512]{1,0:T(8,128)S(1)}) fusion(f32[32,35,512]{2,1,0:T(8,128)} %all-to-all-done.1, pred[32,32]{1,0:T(8,128)(4,1)S(1)} %copy.123, pred[32,32]{1,0:T(8,128)(4,1)S(1)} %copy.117, pred[32,32]{1,0:T(8,128)(4,1)S(1)} %copy.120, ...), kind=kLoop, calls=%fused_computation.6 | loop fusion | flops 4128768 | bytes 2363392 | tf_op jit(solution)/shard_map/reduce_sum | solution.py:55
  162.2 6.5 %all-to-all-start.2 = ((bf16[32,16,512]{2,1,0:T(8,128)(2,1)}), bf16[32,16,512]{2,1,0:T(8,128)(2,1)S(1)}, u32[]{:S(2)}, u32[]{:S(2)}) async-start(bf16[32,16,512]{2,1,0:T(8,128)(2,1)} %broadcast_in_dim.100), calls=%async_computation.2 | async-start | bytes 1048576 | tf_op jit(solution)/shard_map/all_to_all | solution.py:13
  183.0 3.8 %fusion.46 = (bf16[1,8,32,2,512]{4,3,0,2,1:T(2,128)(2,1)}, bf16[1,8,32,2,512]{4,3,0,2,1:T(2,128)(2,1)}, bf16[1,8,32,2,512]{4,3,0,2,1:T(2,128)(2,1)}, bf16[1,8,32,2,512]{4,3,0,2,1:T(2,128)(2,1)S(1)}) fusion(bf16[4,8,32,2,512]{4,3,0,2,1:T(2,128)(2,1)} %bitcast.147), kind=kLoop, calls=%fused_computation.91 | loop fusion | bytes 4194304 | tf_op jit(solution)/shard_map/slice | solution.py:94
  192.8 9.7 %all-to-all-start.3 = ((bf16[32,16,512]{2,1,0:T(8,128)(2,1)}), bf16[32,16,512]{2,1,0:T(8,128)(2,1)}, u32[]{:S(2)}, u32[]{:S(2)}) async-start(bf16[32,16,512]{2,1,0:T(8,128)(2,1)} %broadcast_in_dim.104), calls=%async_computation.3 | async-start | bytes 1048576 | tf_op jit(solution)/shard_map/all_to_all | solution.py:13
  205.2 2.1 squeeze.59
  207.3 2.5 scatter.19
  209.8 6.6 %all-to-all-done.3 = bf16[32,16,512]{2,1,0:T(8,128)(2,1)} async-done(((bf16[32,16,512]{2,1,0:T(8,128)(2,1)}), bf16[32,16,512]{2,1,0:T(8,128)(2,1)}, u32[]{:S(2)}, u32[]{:S(2)}) %all-to-all-start.3) | async-done | bytes 524320 | tf_op jit(solution)/shard_map/all_to_all | solution.py:13
  219.2 2.5 fusion.7
  224.7 4.4 %all-to-all-start.4 = ((bf16[32,16,512]{2,1,0:T(8,128)(2,1)}), bf16[32,16,512]{2,1,0:T(8,128)(2,1)S(1)}, u32[]{:S(2)}, u32[]{:S(2)}) async-start(bf16[32,16,512]{2,1,0:T(8,128)(2,1)} %broadcast_in_dim.108), calls=%async_computation.4 | async-start | bytes 1048576 | tf_op jit(solution)/shard_map/all_to_all | solution.py:13
  232.6 10.3 %all-to-all-done.4 = bf16[32,16,512]{2,1,0:T(8,128)(2,1)S(1)} async-done(((bf16[32,16,512]{2,1,0:T(8,128)(2,1)}), bf16[32,16,512]{2,1,0:T(8,128)(2,1)S(1)}, u32[]{:S(2)}, u32[]{:S(2)}) %all-to-all-start.4) | async-done | bytes 524320 | tf_op jit(solution)/shard_map/all_to_all | solution.py:13
  244.7 2.5 fusion.6
  250.2 4.4 %all-to-all-start.5 = ((bf16[32,16,512]{2,1,0:T(8,128)(2,1)}), bf16[32,16,512]{2,1,0:T(8,128)(2,1)S(1)}, u32[]{:S(2)}, u32[]{:S(2)}) async-start(bf16[32,16,512]{2,1,0:T(8,128)(2,1)} %broadcast_in_dim.112), calls=%async_computation.5 | async-start | bytes 1048576 | tf_op jit(solution)/shard_map/all_to_all | solution.py:13
  255.8 12.6 %all-to-all-done.5 = bf16[32,16,512]{2,1,0:T(8,128)(2,1)S(1)} async-done(((bf16[32,16,512]{2,1,0:T(8,128)(2,1)}), bf16[32,16,512]{2,1,0:T(8,128)(2,1)S(1)}, u32[]{:S(2)}, u32[]{:S(2)}) %all-to-all-start.5) | async-done | bytes 524320 | tf_op jit(solution)/shard_map/all_to_all | solution.py:13
  270.2 2.4 fusion.5
  (153 shorter events, 52.2 us)
Async XLA Ops:
  7.2 14.2 %copy-start = (bf16[1024,1024]{1,0:T(8,128)(2,1)S(1)}, bf16[1024,1024]{1,0:T(8,128)(2,1)}, u32[]{:S(2)}) copy-start(bf16[1024,1024]{1,0:T(8,128)(2,1)} %param.20) | copy-start | bytes 6291460
  9.0 34.0 %all-to-all-start = ((bf16[32,2,1536]{2,1,0:T(2,128)(2,1)}), bf16[32,2,1536]{2,1,0:T(2,128)(2,1)S(1)}, u32[]{:S(2)}, u32[]{:S(2)}) async-start(bf16[32,2,1536]{2,1,0:T(2,128)(2,1)} %reshape.332), calls=%async_computation | async-start | bytes 393216 | tf_op jit(solution)/shard_map/all_to_all | solution.py:59
  21.4 4.3 %copy-start.12 = (bf16[1,2,512,1024]{3,2,1,0:T(8,128)(2,1)S(1)}, bf16[1,2,512,1024]{3,2,1,0:T(8,128)(2,1)}, u32[]{:S(2)}) copy-start(bf16[1,2,512,1024]{3,2,1,0:T(8,128)(2,1)} %param.21) | copy-start | bytes 6291460
  43.0 10.1 %copy-start.14 = (s32[4]{0:T(128)S(1)}, s32[4]{0:T(128)}, u32[]{:S(2)}) copy-start(s32[4]{0:T(128)} %param.26) | copy-start | bytes 52
  43.1 23.7 %copy-start.11 = (s32[4,2]{0,1:T(2,128)S(1)}, s32[4,2]{0,1:T(2,128)}, u32[]{:S(2)}) copy-start(s32[4,2]{0,1:T(2,128)} %param.27) | copy-start | bytes 100
  43.1 111.1 %all-to-all-start.1 = ((f32[32,35,512]{2,1,0:T(8,128)}), f32[32,35,512]{2,1,0:T(8,128)}, u32[]{:S(2)}, u32[]{:S(2)}) async-start(f32[32,35,512]{2,1,0:T(8,128)} %pad_maximum_fusion), calls=%async_computation.1 | async-start | bytes 5242880 | tf_op jit(solution)/shard_map/all_to_all | solution.py:48
  53.1 97.8 %all-gather.5.cloned.1.call-start = ((), (), s32[]{:S(2)}) async-start(), calls=%async_computation.6 | async-start | bytes 1216512 | tf_op jit(solution)/shard_map/all_gather | solution.py:70
  157.4 13.0 %slice-start = ((bf16[32,4,4608]{2,1,0:T(4,128)(2,1)}), bf16[32,4,384]{2,1,0:T(4,128)(2,1)S(1)}, s32[]{:S(2)}) async-start(bf16[32,4,4608]{2,1,0:T(4,128)(2,1)} %all-gather.5.cloned.1.call-done), calls=%async_computation.7 | async-start | bytes 196608 | tf_op jit(solution)/shard_map/slice | solution.py:74
  161.0 10.2 %slice-start.1 = ((bf16[32,4,4608]{2,1,0:T(4,128)(2,1)}), bf16[32,4,512]{2,1,0:T(4,128)(2,1)S(1)}, s32[]{:S(2)}) async-start(bf16[32,4,4608]{2,1,0:T(4,128)(2,1)} %all-gather.5.cloned.1.call-done), calls=%async_computation.8 | async-start | bytes 262144 | tf_op jit(solution)/shard_map/slice | solution.py:74
  161.0 10.9 %slice-start.2 = ((bf16[32,4,4608]{2,1,0:T(4,128)(2,1)}), bf16[32,4,640]{2,1,0:T(4,128)(2,1)S(1)}, s32[]{:S(2)}) async-start(bf16[32,4,4608]{2,1,0:T(4,128)(2,1)} %all-gather.5.cloned.1.call-done), calls=%async_computation.9 | async-start | bytes 327680 | tf_op jit(solution)/shard_map/slice | solution.py:74
  161.3 11.5 %slice-start.3 = ((bf16[32,4,4608]{2,1,0:T(4,128)(2,1)}), bf16[32,4,768]{2,1,0:T(4,128)(2,1)S(1)}, s32[]{:S(2)}) async-start(bf16[32,4,4608]{2,1,0:T(4,128)(2,1)} %all-gather.5.cloned.1.call-done), calls=%async_computation.10 | async-start | bytes 393216 | tf_op jit(solution)/shard_map/slice | solution.py:74
  162.2 11.4 %slice-start.4 = ((bf16[32,4,4608]{2,1,0:T(4,128)(2,1)}), bf16[32,4,1024]{2,1,0:T(4,128)(2,1)S(1)}, s32[]{:S(2)}) async-start(bf16[32,4,4608]{2,1,0:T(4,128)(2,1)} %all-gather.5.cloned.1.call-done), calls=%async_computation.11 | async-start | bytes 524288 | tf_op jit(solution)/shard_map/slice | solution.py:74
  162.2 25.6 %all-to-all-start.2 = ((bf16[32,16,512]{2,1,0:T(8,128)(2,1)}), bf16[32,16,512]{2,1,0:T(8,128)(2,1)S(1)}, u32[]{:S(2)}, u32[]{:S(2)}) async-start(bf16[32,16,512]{2,1,0:T(8,128)(2,1)} %broadcast_in_dim.100), calls=%async_computation.2 | async-start | bytes 1048576 | tf_op jit(solution)/shard_map/all_to_all | solution.py:13
  183.0 4.7 %copy-start.3 = (f32[32,512]{1,0:T(8,128)S(1)}, f32[32,512]{1,0:T(8,128)}, u32[]{:S(2)}) copy-start(f32[32,512]{1,0:T(8,128)} %get-tuple-element.63) | copy-start | bytes 196612
  183.0 4.8 %copy-start.6 = (f32[8,2,512]{2,1,0:T(2,128)S(1)}, f32[8,2,512]{2,1,0:T(2,128)}, u32[]{:S(2)}) copy-start(f32[8,2,512]{2,1,0:T(2,128)} %get-tuple-element.72) | copy-start | bytes 98308
  191.6 15.6 %copy-start.5 = (f32[8,2,512]{2,1,0:T(2,128)S(1)}, f32[8,2,512]{2,1,0:T(2,128)}, u32[]{:S(2)}) copy-start(f32[8,2,512]{2,1,0:T(2,128)} %get-tuple-element.71) | copy-start | bytes 98308
  191.7 15.6 %copy-start.2 = (f32[32,512]{1,0:T(8,128)S(1)}, f32[32,512]{1,0:T(8,128)}, u32[]{:S(2)}) copy-start(f32[32,512]{1,0:T(8,128)} %get-tuple-element.64) | copy-start | bytes 196612
  192.8 23.5 %all-to-all-start.3 = ((bf16[32,16,512]{2,1,0:T(8,128)(2,1)}), bf16[32,16,512]{2,1,0:T(8,128)(2,1)}, u32[]{:S(2)}, u32[]{:S(2)}) async-start(bf16[32,16,512]{2,1,0:T(8,128)(2,1)} %broadcast_in_dim.104), calls=%async_computation.3 | async-start | bytes 1048576 | tf_op jit(solution)/shard_map/all_to_all | solution.py:13
  209.8 9.5 %copy-start.1 = (bf16[512,512]{1,0:T(8,128)(2,1)S(1)}, bf16[512,512]{1,0:T(8,128)(2,1)}, u32[]{:S(2)}) copy-start(bf16[512,512]{1,0:T(8,128)(2,1)} %squeeze.59) | copy-start | bytes 1572868
  219.2 4.3 %copy-start.8 = (bf16[1,16,1024]{2,0,1:T(2,128)(2,1)S(1)}, bf16[1,16,1024]{2,0,1:T(2,128)(2,1)}, u32[]{:S(2)}) copy-start(bf16[1,16,1024]{2,0,1:T(2,128)(2,1)} %get-tuple-element.81) | copy-start | bytes 98308
  223.5 9.1 %copy-start.4 = (f32[8,2,512]{2,1,0:T(2,128)S(1)}, f32[8,2,512]{2,1,0:T(2,128)}, u32[]{:S(2)}) copy-start(f32[8,2,512]{2,1,0:T(2,128)} %get-tuple-element.70) | copy-start | bytes 98308
  224.7 18.2 %all-to-all-start.4 = ((bf16[32,16,512]{2,1,0:T(8,128)(2,1)}), bf16[32,16,512]{2,1,0:T(8,128)(2,1)S(1)}, u32[]{:S(2)}, u32[]{:S(2)}) async-start(bf16[32,16,512]{2,1,0:T(8,128)(2,1)} %broadcast_in_dim.108), calls=%async_computation.4 | async-start | bytes 1048576 | tf_op jit(solution)/shard_map/all_to_all | solution.py:13
  244.7 4.3 %copy-start.7 = (bf16[1,16,1024]{2,0,1:T(2,128)(2,1)S(1)}, bf16[1,16,1024]{2,0,1:T(2,128)(2,1)}, u32[]{:S(2)}) copy-start(bf16[1,16,1024]{2,0,1:T(2,128)(2,1)} %get-tuple-element.80) | copy-start | bytes 98308
  250.2 18.2 %all-to-all-start.5 = ((bf16[32,16,512]{2,1,0:T(8,128)(2,1)}), bf16[32,16,512]{2,1,0:T(8,128)(2,1)S(1)}, u32[]{:S(2)}, u32[]{:S(2)}) async-start(bf16[32,16,512]{2,1,0:T(8,128)(2,1)} %broadcast_in_dim.112), calls=%async_computation.5 | async-start | bytes 1048576 | tf_op jit(solution)/shard_map/all_to_all | solution.py:13
  (5 other events, 9.3 us)
Sparse Core Ops, SparseCore 0:
  66.8 84.0 all-gather.4

commit v4 on v2

--- a/solution.py
+++ b/solution.py
@@ -13,7 +13,7 @@
     return lax.all_to_all(spread, "row", 0, 0, tiled=False)
 
 
-def per_device(
+def solve(
     sub_source,
     sub_inverse,
     coupling,
@@ -39,11 +39,6 @@
     owned = owned.reshape(STEPS, PAIR, width // block, n_src, n_row, PAIR)
     owned = owned.transpose(0, 1, 2, 4, 3, 5).reshape(STEPS, PAIR, width)
     owned = lax.all_gather(owned, "src", axis=0, tiled=False)
-    owned, sub_source = lax.optimization_barrier((owned, sub_source))
-    owned = owned.transpose(1, 0, 2, 3).reshape(STEPS, span, width)
-    lower_rows = owned[:, :, : LINKS * block]
-    inverse_rows = owned[:, :, LINKS * block :]
-    inverse_all = lax.all_gather(inverse_rows, "row", axis=0, tiled=False)
 
     sub_field = jnp.dot(
         sub_inverse, sub_source.astype(jnp.bfloat16), preferred_element_type=jnp.float32
@@ -52,13 +47,17 @@
     updates = jnp.einsum(
         "lmf,ft->lmt", coupling[0], rounded, preferred_element_type=jnp.float32
     )
-    per_dest = updates.astype(jnp.bfloat16).reshape(LINKS, n_src, n_row, PAIR, cols)
-    per_dest = per_dest.transpose(2, 0, 1, 3, 4).reshape(n_row, LINKS * span, cols)
-    src_rows = sep_source.astype(jnp.bfloat16).reshape(n_row, PAIR, cols)
-    lists = jnp.zeros((cols,), jnp.bfloat16).at[:LINKS].set(update_lists[0].astype(jnp.bfloat16))
+    per_dest = updates.reshape(LINKS, n_src, n_row, PAIR, cols).transpose(2, 0, 1, 3, 4)
+    per_dest = per_dest.reshape(n_row, LINKS * span, cols)
+    src_rows = sep_source.reshape(n_row, PAIR, cols)
+    lists = jnp.zeros((cols,), jnp.float32).at[:LINKS].set(update_lists[0].astype(jnp.float32))
     lists = jnp.broadcast_to(lists[None, None], (n_row, 1, cols))
     payload = jnp.concatenate([per_dest, src_rows, lists], axis=1)
-    got = lax.all_to_all(payload, "row", 0, 0, tiled=False).astype(jnp.float32)
+    owned = owned.transpose(1, 0, 2, 3).reshape(STEPS, span, width)
+    lower_rows = owned[:, :, : LINKS * block]
+    inverse_rows = owned[:, :, LINKS * block :]
+    inverse_all = lax.all_gather(inverse_rows, "row", axis=0, tiled=False)
+    got = lax.all_to_all(payload, "row", 0, 0, tiled=False)
     got_updates = got[:, : LINKS * span].reshape(n_row, LINKS, span, cols)
     got_src = got[:, LINKS * span : LINKS * span + PAIR].reshape(STEPS, span, cols)
     got_lists = got[:, LINKS * span + PAIR, :LINKS]
@@ -95,7 +94,7 @@
 
 def solution(mesh):
     return jax.shard_map(
-        per_device,
+        solve,
         mesh=mesh,
         in_specs=(
             P("row", "src"),

time: 251 us -> 251 us (level)
  other arithmetic: 27.2 us -> 12.1 us
  waiting for transfers between devices: 94 us -> 107 us
  starting transfers between devices: 36.1 us -> 42 us
  local copies, waits for them, and re-layouts: 43.5 us -> 40.3 us
    convert_element_type x6 -> x4, other arithmetic: 12.5 us -> 3.92 us  [the longest x3 3.92 us: solve(): pieces.append(jnp.where(target >= 0, chosen, 0.0).astype(jnp.bfloat16))]
    reduce_sum x5, other arithmetic: 11 us -> 3.53 us  [solve(): jnp.sum(jnp.where(hit, got_updates, 0.0), axis=(0, 1))]
    all_to_all x2, waiting for transfers between devices: 40.6 us -> 47.5 us  [the longest x1 47.5 us: solve(): got = lax.all_to_all(payload, 'row', 0, 0, tiled=False)]
    all_to_all x2, starting transfers between devices: 15.3 us -> 21.3 us  [the longest x1 11.3 us: solve(): lax.all_to_all(factors.reshape(n_row, PAIR, width), 'row', 0, 0, tiled=Fa...]
    reshape x6, local copies, waits for them, and re-layouts: 10.3 us -> 15.5 us  [the longest x1 5.86 us: solve(): whole_field = solved.reshape(STEPS, n_row, n_src, PAIR, cols)]
    slice x10 -> x7, local copies, waits for them, and re-layouts: 11.5 us -> 6.48 us  [the longest x1 2.87 us: solve(): inverse = inverse_all[:, k].reshape(block, block)]
    all_gather x1, waiting for transfers between devices: 19.4 us -> 23.2 us  [solve(): inverse_all = lax.all_gather(inverse_rows, 'row', axis=0, tiled=False)]
    all_to_all x1 -> x0, local copies, waits for them, and re-layouts: 3.43 us -> none  [per_device(): got = lax.all_to_all(payload, 'row', 0, 0, tiled=False).astype(jnp.float32)]
  transfers between devices with their start and end apart: 7 -> 7, of which waited for: 6 -> 5; matrix products, arithmetic and copies ran while one was open for 17% -> 16% of each run, Pallas kernels for 0% -> 0%
where the time goes in v4:
time: 251 us; the launch traced here: 249 us
  waiting for transfers between devices  107 us (43%)
  starting transfers between devices  42 us (17%)
  local copies, waits for them, and re-layouts  40.3 us (16%)
  between operations  22.1 us (9%)
  matrix products  13.7 us (5%)
  other arithmetic  12.1 us (5%)
  blocking collectives  11.6 us (5%)
    all_to_all x1, waiting for transfers between devices, solve(): got = lax.all_to_all(payload, 'row', 0, 0, tiled=False)  47.5 us
    all_to_all x4, waiting for transfers between devices, gather_row(): return lax.all_to_all(spread, 'row', 0, 0, tiled=False)  36.7 us
    all_gather x1, waiting for transfers between devices, solve(): inverse_all = lax.all_gather(inverse_rows, 'row', axis=0, tiled=False)  23.2 us
    all_to_all x4, starting transfers between devices, gather_row(): return lax.all_to_all(spread, 'row', 0, 0, tiled=False)  20.6 us
    all_gather x1, blocking collectives, solve(): owned = lax.all_gather(owned, 'src', axis=0, tiled=False)  11.6 us
    all_to_all x1, starting transfers between devices, solve(): lax.all_to_all(factors.reshape(n_row, PAIR, width), 'row', 0, 0, tiled=Fa...  11.3 us
    all_to_all x1, starting transfers between devices, solve(): got = lax.all_to_all(payload, 'row', 0, 0, tiled=False)  10 us
    dot_general x4, matrix products, solve(): result = jnp.dot(inverse, full_residue, preferred_element_type=jnp.float32)  7.14 us
  transfers between devices with their start and end apart: 7, of which 5 were waited for; matrix products, arithmetic and copies ran while one was open for 16% of the time, Pallas kernels for 0%

profile of v4, /device:TPU:16, one launch (start us, length us, event | category | flops | bytes accessed | tf_op | source)
XLA Modules:
  0.0 249.1 jit_solution(14600832937003471228)
XLA Ops:
  9.0 11.3 %all-to-all-start = ((bf16[32,2,1536]{2,1,0:T(2,128)(2,1)}), bf16[32,2,1536]{2,1,0:T(2,128)(2,1)S(1)}, u32[]{:S(2)}, u32[]{:S(2)}) async-start(bf16[32,2,1536]{2,1,0:T(2,128)(2,1)} %reshape.291), calls=%async_computation | async-start | bytes 393216 | tf_op jit(solution)/shard_map/all_to_all | solution.py:37
  21.4 3.0 %fusion.27 = f32[1024,512]{1,0:T(8,128)S(1)} fusion(bf16[1024,1024]{1,0:T(8,128)(2,1)S(1)} %copy-done, f32[1024,512]{1,0:T(8,128)} %param.19), kind=kOutput, calls=%fused_computation.45 | convolution fusion | flops 1074266112 | bytes 6291456 | tf_op jit(solution)/shard_map/dot_general | solution.py:43
  25.7 2.6 %fusion.2 = f32[2,512,512]{2,1,0:T(8,128)} fusion(bf16[1,2,512,1024]{3,2,1,0:T(8,128)(2,1)S(1)} %copy-done.7, f32[1024,512]{1,0:T(8,128)S(1)} %fusion.27), kind=kOutput, calls=%fused_computation.10 | convolution fusion | flops 1074266112 | bytes 6291456 | tf_op jit(solution)/shard_map/lmf,ft->lmt/dot_general | solution.py:47
  28.2 3.5 %reshape.294 = f32[2,8,32,2,512]{4,3,2,1,0:T(2,128)} reshape(f32[2,512,512]{2,1,0:T(8,128)} %fusion.2) | data formatting | bytes 4194304 | tf_op jit(solution)/shard_map/reshape | solution.py:50
  31.7 4.1 %copy.84 = f32[32,2,8,2,512]{4,3,2,1,0:T(2,128)} copy(f32[32,2,8,2,512]{4,3,0,2,1:T(2,128)} %bitcast.104) | data formatting | bytes 4194304 | tf_op jit(solution)/shard_map/transpose | solution.py:50
  35.8 3.7 %reshape.295 = f32[32,32,512]{2,1,0:T(8,128)} reshape(f32[32,2,8,2,512]{4,3,2,1,0:T(2,128)} %copy.84) | data formatting | bytes 4194304 | tf_op jit(solution)/shard_map/reshape | solution.py:51
  39.6 3.5 %pad_maximum_fusion = f32[32,35,512]{2,1,0:T(8,128)} fusion(f32[32,1,512]{2,1,0:T(1,128)S(1)} %broadcast_in_dim.95, f32[32,2,512]{2,1,0:T(2,128)S(1)} %reshape.296, f32[32,32,512]{2,1,0:T(8,128)} %reshape.295), kind=kLoop, calls=%fused_computation.3 | loop fusion | flops 1146880 | bytes 4587520 | tf_op jit(solution)/shard_map/concatenate | solution.py:55
  43.1 10.0 %all-to-all-start.1 = ((f32[32,35,512]{2,1,0:T(8,128)}), f32[32,35,512]{2,1,0:T(8,128)}, u32[]{:S(2)}, u32[]{:S(2)}) async-start(f32[32,35,512]{2,1,0:T(8,128)} %pad_maximum_fusion), calls=%async_computation.1 | async-start | bytes 5242880 | tf_op jit(solution)/shard_map/all_to_all | solution.py:60
  57.1 11.6 %all_gather.9 = bf16[8,4,2,1536]{3,1,2,0:T(4,128)(2,1)S(1)} all-gather(bf16[1,4,2,1536]{3,1,2,0:T(4,128)(2,1)S(1)} %copy.82), channel_id=1, replica_groups=mesh['row'=32,'src'=8] {'src'}, dimensions={0}, use_global_device_ids=true | all-gather | bytes 221184 | tf_op jit(solution)/shard_map/all_gather | solution.py:41
  69.6 47.5 %all-to-all-done.1 = f32[32,35,512]{2,1,0:T(8,128)} async-done(((f32[32,35,512]{2,1,0:T(8,128)}), f32[32,35,512]{2,1,0:T(8,128)}, u32[]{:S(2)}, u32[]{:S(2)}) %all-to-all-start.1) | async-done | bytes 2293792 | tf_op jit(solution)/shard_map/all_to_all | solution.py:60
  119.7 2.9 %select_reduce_fusion = (f32[32,512]{1,0:T(8,128)S(1)}, f32[32,512]{1,0:T(8,128)S(1)}, f32[32,512]{1,0:T(8,128)S(1)}, f32[32,512]{1,0:T(8,128)S(1)}) fusion(f32[32,35,512]{2,1,0:T(8,128)} %all-to-all-done.1, pred[32,32]{1,0:T(8,128)(4,1)S(1)} %copy.89, pred[32,32]{1,0:T(8,128)(4,1)S(1)} %copy.87, pred[32,32]{1,0:T(8,128)(4,1)S(1)} %copy.88, ...), kind=kLoop, calls=%fused_computation.6 | loop fusion | flops 4128768 | bytes 2363392 | tf_op jit(solution)/shard_map/reduce_sum | solution.py:67
  123.8 5.2 %all-to-all-start.2 = ((bf16[32,16,512]{2,1,0:T(8,128)(2,1)}), bf16[32,16,512]{2,1,0:T(8,128)(2,1)S(1)}, u32[]{:S(2)}, u32[]{:S(2)}) async-start(bf16[32,16,512]{2,1,0:T(8,128)(2,1)} %broadcast_in_dim.100), calls=%async_computation.2 | async-start | bytes 1048576 | tf_op jit(solution)/shard_map/all_to_all | solution.py:13
  133.4 23.2 %all-gather.3.cloned.1.call-done = bf16[128,16,512]{2,1,0:T(8,128)(2,1)} async-done(((bf16[4,16,512]{2,1,0:T(8,128)(2,1)}), bf16[128,16,512]{2,1,0:T(8,128)(2,1)}) %all-gather.3.cloned.1.call-update) | async-done | bytes 2097168 | tf_op jit(solution)/shard_map/all_gather | solution.py:59
  156.7 2.9 %fusion.46 = (bf16[32,1,16,512]{3,2,1,0:T(8,128)(2,1)}, bf16[32,1,16,512]{3,2,1,0:T(8,128)(2,1)}, bf16[32,1,16,512]{3,2,1,0:T(8,128)(2,1)}, bf16[32,1,16,512]{3,2,1,0:T(8,128)(2,1)}) fusion(bf16[32,4,16,512]{3,2,1,0:T(8,128)(2,1)} %bitcast.107), kind=kLoop, calls=%fused_computation.74 | loop fusion | bytes 4194304 | tf_op jit(solution)/shard_map/slice | solution.py:82
  163.4 6.9 %all-to-all-start.3 = ((bf16[32,16,512]{2,1,0:T(8,128)(2,1)}), bf16[32,16,512]{2,1,0:T(8,128)(2,1)}, u32[]{:S(2)}, u32[]{:S(2)}) async-start(bf16[32,16,512]{2,1,0:T(8,128)(2,1)} %broadcast_in_dim.104), calls=%async_computation.3 | async-start | bytes 1048576 | tf_op jit(solution)/shard_map/all_to_all | solution.py:13
  172.9 2.5 %scatter.19 = f32[4,512,512]{2,1,0:T(8,128)} pad(f32[1,512,512]{2,1,0:T(8,128)S(1)} %convolution_bitcast_fusion.3, f32[]{:T(128)} %constant.189.clone.1), padding=0_3x0_0x0_0 | pad | bytes 5242884 | tf_op jit(solution)/shard_map/scatter | solution.py:84
  175.4 10.0 %all-to-all-done.3 = bf16[32,16,512]{2,1,0:T(8,128)(2,1)} async-done(((bf16[32,16,512]{2,1,0:T(8,128)(2,1)}), bf16[32,16,512]{2,1,0:T(8,128)(2,1)}, u32[]{:S(2)}, u32[]{:S(2)}) %all-to-all-start.3) | async-done | bytes 524320 | tf_op jit(solution)/shard_map/all_to_all | solution.py:13
  185.4 2.6 %fusion.7 = f32[4,512,512]{2,1,0:T(8,128)} fusion(f32[4,512,512]{2,1,0:T(8,128)} %scatter.19, bf16[512,512]{1,0:T(8,128)(2,1)} %bitcast.113, bf16[512,512]{1,0:T(8,128)(2,1)} %bitcast.28), kind=kOutput, calls=%fused_computation.16 | convolution fusion | flops 268435456 | bytes 2097152 | tf_op jit(solution)/shard_map/dot_general | solution.py:83
  188.0 1.8 fusion.29
  191.0 4.4 %all-to-all-start.4 = ((bf16[32,16,512]{2,1,0:T(8,128)(2,1)}), bf16[32,16,512]{2,1,0:T(8,128)(2,1)S(1)}, u32[]{:S(2)}, u32[]{:S(2)}) async-start(bf16[32,16,512]{2,1,0:T(8,128)(2,1)} %broadcast_in_dim.108), calls=%async_computation.4 | async-start | bytes 1048576 | tf_op jit(solution)/shard_map/all_to_all | solution.py:13
  198.2 12.1 %all-to-all-done.4 = bf16[32,16,512]{2,1,0:T(8,128)(2,1)S(1)} async-done(((bf16[32,16,512]{2,1,0:T(8,128)(2,1)}), bf16[32,16,512]{2,1,0:T(8,128)(2,1)S(1)}, u32[]{:S(2)}, u32[]{:S(2)}) %all-to-all-start.4) | async-done | bytes 524320 | tf_op jit(solution)/shard_map/all_to_all | solution.py:13
  214.7 4.0 %all-to-all-start.5 = ((bf16[32,16,512]{2,1,0:T(8,128)(2,1)}), bf16[32,16,512]{2,1,0:T(8,128)(2,1)S(1)}, u32[]{:S(2)}, u32[]{:S(2)}) async-start(bf16[32,16,512]{2,1,0:T(8,128)(2,1)} %broadcast_in_dim.112), calls=%async_computation.5 | async-start | bytes 1048576 | tf_op jit(solution)/shard_map/all_to_all | solution.py:13
  218.7 14.6 %all-to-all-done.5 = bf16[32,16,512]{2,1,0:T(8,128)(2,1)S(1)} async-done(((bf16[32,16,512]{2,1,0:T(8,128)(2,1)}), bf16[32,16,512]{2,1,0:T(8,128)(2,1)S(1)}, u32[]{:S(2)}, u32[]{:S(2)}) %all-to-all-start.5) | async-done | bytes 524320 | tf_op jit(solution)/shard_map/all_to_all | solution.py:13
  234.8 5.9 %reshape.305 = f32[4,32,8,2,512]{4,3,2,1,0:T(2,128)} reshape(f32[4,512,512]{2,1,0:T(8,128)} %fusion.5) | data formatting | bytes 8388608 | tf_op jit(solution)/shard_map/reshape | solution.py:86
  (79 shorter events, 27.2 us)
Async XLA Ops:
  7.2 14.2 %copy-start = (bf16[1024,1024]{1,0:T(8,128)(2,1)S(1)}, bf16[1024,1024]{1,0:T(8,128)(2,1)}, u32[]{:S(2)}) copy-start(bf16[1024,1024]{1,0:T(8,128)(2,1)} %param.20) | copy-start | bytes 6291460
  9.0 34.1 %all-to-all-start = ((bf16[32,2,1536]{2,1,0:T(2,128)(2,1)}), bf16[32,2,1536]{2,1,0:T(2,128)(2,1)S(1)}, u32[]{:S(2)}, u32[]{:S(2)}) async-start(bf16[32,2,1536]{2,1,0:T(2,128)(2,1)} %reshape.291), calls=%async_computation | async-start | bytes 393216 | tf_op jit(solution)/shard_map/all_to_all | solution.py:37
  21.3 4.3 %copy-start.7 = (bf16[1,2,512,1024]{3,2,1,0:T(8,128)(2,1)S(1)}, bf16[1,2,512,1024]{3,2,1,0:T(8,128)(2,1)}, u32[]{:S(2)}) copy-start(bf16[1,2,512,1024]{3,2,1,0:T(8,128)(2,1)} %param.21) | copy-start | bytes 6291460
  24.3 1.3 copy-start.10
  35.8 3.7 %copy-start.8 = (s32[1,2]{1,0:T(1,128)S(1)}, s32[1,2]{1,0:T(1,128)}, u32[]{:S(2)}) copy-start(s32[1,2]{1,0:T(1,128)} %param.22) | copy-start | bytes 28
  43.1 10.1 %copy-start.9 = (s32[4]{0:T(128)S(1)}, s32[4]{0:T(128)}, u32[]{:S(2)}) copy-start(s32[4]{0:T(128)} %param.26) | copy-start | bytes 52
  43.1 74.0 %all-to-all-start.1 = ((f32[32,35,512]{2,1,0:T(8,128)}), f32[32,35,512]{2,1,0:T(8,128)}, u32[]{:S(2)}, u32[]{:S(2)}) async-start(f32[32,35,512]{2,1,0:T(8,128)} %pad_maximum_fusion), calls=%async_computation.1 | async-start | bytes 5242880 | tf_op jit(solution)/shard_map/all_to_all | solution.py:60
  53.1 103.5 %all-gather.3.cloned.1.call-start = ((), (), s32[]{:S(2)}) async-start(), calls=%async_computation.6 | async-start | bytes 2162688 | tf_op jit(solution)/shard_map/all_gather | solution.py:59
  119.7 9.3 %copy-start.6 = (s32[4,2]{0,1:T(2,128)S(1)}, s32[4,2]{0,1:T(2,128)}, u32[]{:S(2)}) copy-start(s32[4,2]{0,1:T(2,128)} %param.27) | copy-start | bytes 100
  123.8 35.7 %all-to-all-start.2 = ((bf16[32,16,512]{2,1,0:T(8,128)(2,1)}), bf16[32,16,512]{2,1,0:T(8,128)(2,1)S(1)}, u32[]{:S(2)}, u32[]{:S(2)}) async-start(bf16[32,16,512]{2,1,0:T(8,128)(2,1)} %broadcast_in_dim.100), calls=%async_computation.2 | async-start | bytes 1048576 | tf_op jit(solution)/shard_map/all_to_all | solution.py:13
  159.5 0.8 copy-start.1
  160.3 2.0 copy-start.4
  160.3 2.0 copy-start.5
  163.4 22.0 %all-to-all-start.3 = ((bf16[32,16,512]{2,1,0:T(8,128)(2,1)}), bf16[32,16,512]{2,1,0:T(8,128)(2,1)}, u32[]{:S(2)}, u32[]{:S(2)}) async-start(bf16[32,16,512]{2,1,0:T(8,128)(2,1)} %broadcast_in_dim.104), calls=%async_computation.3 | async-start | bytes 1048576 | tf_op jit(solution)/shard_map/all_to_all | solution.py:13
  189.8 20.5 %copy-start.3 = (bf16[32,1,16,512]{3,2,1,0:T(8,128)(2,1)S(1)}, bf16[32,1,16,512]{3,2,1,0:T(8,128)(2,1)}, u32[]{:S(2)}) copy-start(bf16[32,1,16,512]{3,2,1,0:T(8,128)(2,1)} %get-tuple-element.75) | copy-start | bytes 1572868
  191.0 19.3 %all-to-all-start.4 = ((bf16[32,16,512]{2,1,0:T(8,128)(2,1)}), bf16[32,16,512]{2,1,0:T(8,128)(2,1)S(1)}, u32[]{:S(2)}, u32[]{:S(2)}) async-start(bf16[32,16,512]{2,1,0:T(8,128)(2,1)} %broadcast_in_dim.108), calls=%async_computation.4 | async-start | bytes 1048576 | tf_op jit(solution)/shard_map/all_to_all | solution.py:13
  213.6 19.8 %copy-start.2 = (bf16[32,1,16,512]{3,2,1,0:T(8,128)(2,1)S(1)}, bf16[32,1,16,512]{3,2,1,0:T(8,128)(2,1)}, u32[]{:S(2)}) copy-start(bf16[32,1,16,512]{3,2,1,0:T(8,128)(2,1)} %get-tuple-element.74) | copy-start | bytes 1572868
  214.7 18.6 %all-to-all-start.5 = ((bf16[32,16,512]{2,1,0:T(8,128)(2,1)}), bf16[32,16,512]{2,1,0:T(8,128)(2,1)S(1)}, u32[]{:S(2)}, u32[]{:S(2)}) async-start(bf16[32,16,512]{2,1,0:T(8,128)(2,1)} %broadcast_in_dim.112), calls=%async_computation.5 | async-start | bytes 1048576 | tf_op jit(solution)/shard_map/all_to_all | solution.py:13
Sparse Core Ops, SparseCore 0:
  69.5 87.0 all-gather.2

commit v5 on v2

--- a/solution.py
+++ b/solution.py
@@ -67,22 +67,28 @@
         hit = (got_lists == k)[:, :, None, None]
         pending.append(got_src[k] - jnp.sum(jnp.where(hit, got_updates, 0.0), axis=(0, 1)))
 
-    solved = jnp.zeros((STEPS, block, cols), jnp.float32)
+    fields, rounded_fields = [], []
     for k in range(STEPS):
-        pieces = []
-        for link_pos in range(LINKS):
-            target = sep_links[k, link_pos]
-            chosen = solved[jnp.maximum(target, 0)]
-            pieces.append(jnp.where(target >= 0, chosen, 0.0).astype(jnp.bfloat16))
-        stacked = jnp.concatenate(pieces, axis=0)
-        residue = pending[k] - jnp.dot(
-            lower_rows[k], stacked, preferred_element_type=jnp.float32
-        )
+        residue = pending[k]
+        if k >= 2:
+            target = sep_links[k, 1]
+            far = jnp.zeros((block, cols), jnp.bfloat16)
+            for c in range(k - 1):
+                far = jnp.where(target == c, rounded_fields[c], far)
+            residue = residue - jnp.dot(
+                lower_rows[k][:, block:], far, preferred_element_type=jnp.float32
+            )
+        if k >= 1:
+            residue = residue - jnp.dot(
+                lower_rows[k][:, :block], rounded_fields[k - 1], preferred_element_type=jnp.float32
+            )
         everyone = gather_row(residue.astype(jnp.bfloat16), n_row)
         full_residue = everyone.reshape(block, cols)
         inverse = inverse_all[:, k].reshape(block, block)
         result = jnp.dot(inverse, full_residue, preferred_element_type=jnp.float32)
-        solved = solved.at[k].set(result)
+        fields.append(result)
+        rounded_fields.append(result.astype(jnp.bfloat16))
+    solved = jnp.stack(fields, axis=0)
     blocks_per = block // local_rows
     whole_field = solved.reshape(STEPS, n_row, n_src, PAIR, cols)
     own_rows = lax.dynamic_slice(

time: 251 us -> 245 us (0.976)
  local copies, waits for them, and re-layouts: 43.5 us -> 50.4 us
  between operations: 21.9 us -> 16.1 us
  waiting for transfers between devices: 94 us -> 88.8 us
  other arithmetic: 27.2 us -> 24.2 us
    another operation x0 -> x6, local copies, waits for them, and re-layouts: none -> 12.2 us  [per_device(): solved = jnp.stack(fields, axis=0)]
    all_to_all x4, waiting for transfers between devices: 34 us -> 24.2 us  [gather_row(): return lax.all_to_all(spread, 'row', 0, 0, tiled=False)]
    reshape x1 -> x0, local copies, waits for them, and re-layouts: 5.85 us -> none  [per_device(): whole_field = solved.reshape(STEPS, n_row, n_src, PAIR, cols)]
    convert_element_type x3 -> x1, other arithmetic: 3.92 us -> 0.01 us  [per_device(): everyone = gather_row(residue.astype(jnp.bfloat16), n_row)]
    all_gather x1, waiting for transfers between devices: 19.4 us -> 22 us  [per_device(): inverse_all = lax.all_gather(inverse_rows, 'row', axis=0, tiled=False)]
    scatter x1 -> x0, local copies, waits for them, and re-layouts: 2.51 us -> none  [per_device(): solved = solved.at[k].set(result)]
    slice x1 -> x2, local copies, waits for them, and re-layouts: 2.86 us -> 5.14 us  [per_device(): inverse = inverse_all[:, k].reshape(block, block)]
    unnamed x19 -> x34, local copies, waits for them, and re-layouts: 5.08 us -> 7.06 us
  transfers between devices with their start and end apart: 7 -> 7, of which waited for: 6 -> 5; matrix products, arithmetic and copies ran while one was open for 17% -> 23% of each run, Pallas kernels for 0% -> 0%
where the time goes in v5:
time: 245 us; the launch traced here: 243 us
  waiting for transfers between devices  88.8 us (36%)
  local copies, waits for them, and re-layouts  50.4 us (21%)
  starting transfers between devices  36.8 us (15%)
  other arithmetic  24.2 us (10%)
  between operations  16.1 us (7%)
  matrix products  14.3 us (6%)
  blocking collectives  12.6 us (5%)
    all_to_all x1, waiting for transfers between devices, per_device(): got = lax.all_to_all(payload, 'row', 0, 0, tiled=False).astype(jnp.float32)  33.3 us
    all_to_all x4, waiting for transfers between devices, gather_row(): return lax.all_to_all(spread, 'row', 0, 0, tiled=False)  24.2 us
    all_gather x1, waiting for transfers between devices, per_device(): inverse_all = lax.all_gather(inverse_rows, 'row', axis=0, tiled=False)  22 us
    all_to_all x4, starting transfers between devices, gather_row(): return lax.all_to_all(spread, 'row', 0, 0, tiled=False)  21.3 us
    all_gather x1, blocking collectives, per_device(): owned = lax.all_gather(owned, 'src', axis=0, tiled=False)  12.6 us
    another operation x6, local copies, waits for them, and re-layouts, per_device(): solved = jnp.stack(fields, axis=0)  12.2 us
    all_to_all x1, starting transfers between devices, per_device(): lax.all_to_all(factors.reshape(n_row, PAIR, width), 'row', 0, 0, tiled=Fa...  11.3 us
    reduce_sum x5, other arithmetic, per_device(): jnp.sum(jnp.where(hit, got_updates, 0.0), axis=(0, 1))  11.1 us
  transfers between devices with their start and end apart: 7, of which 5 were waited for; matrix products, arithmetic and copies ran while one was open for 23% of the time, Pallas kernels for 0%

profile of v5, /device:TPU:16, one launch (start us, length us, event | category | flops | bytes accessed | tf_op | source)
XLA Modules:
  0.0 243.2 jit_solution(14351415681101263139)
XLA Ops:
  9.0 11.3 %all-to-all-start = ((bf16[32,2,1536]{2,1,0:T(2,128)(2,1)}), bf16[32,2,1536]{2,1,0:T(2,128)(2,1)S(1)}, u32[]{:S(2)}, u32[]{:S(2)}) async-start(bf16[32,2,1536]{2,1,0:T(2,128)(2,1)} %reshape.150), calls=%async_computation | async-start | bytes 393216 | tf_op jit(solution)/shard_map/all_to_all | solution.py:37
  22.7 9.3 %all-to-all-done = bf16[32,2,1536]{2,1,0:T(2,128)(2,1)S(1)} async-done(((bf16[32,2,1536]{2,1,0:T(2,128)(2,1)}), bf16[32,2,1536]{2,1,0:T(2,128)(2,1)S(1)}, u32[]{:S(2)}, u32[]{:S(2)}) %all-to-all-start) | async-done | bytes 196640 | tf_op jit(solution)/shard_map/all_to_all | solution.py:37
  35.9 12.6 %all_gather.9 = bf16[8,4,2,1536]{3,1,2,0:T(4,128)(2,1)} all-gather(bf16[1,4,2,1536]{3,1,2,0:T(4,128)(2,1)S(1)} %copy.134), channel_id=1, replica_groups=mesh['row'=32,'src'=8] {'src'}, dimensions={0}, use_global_device_ids=true | all-gather | bytes 221184 | tf_op jit(solution)/shard_map/all_gather | solution.py:41
  48.5 3.0 %convolution_bitcast_fusion = f32[1024,512]{0,1:T(8,128)S(1)} fusion(bf16[1024,1024]{1,0:T(8,128)(2,1)S(1)} %copy-done, f32[1024,512]{1,0:T(8,128)} %param.11), kind=kOutput, calls=%fused_computation.11 | convolution fusion | flops 1074266112 | bytes 6291456 | tf_op jit(solution)/shard_map/dot_general | solution.py:48
  52.9 2.3 fusion.5
  61.5 4.0 %all-to-all-start.1 = ((bf16[32,35,512]{2,1,0:T(8,128)(2,1)}), bf16[32,35,512]{2,1,0:T(8,128)(2,1)S(1)}, u32[]{:S(2)}, u32[]{:S(2)}) async-start(bf16[32,35,512]{2,1,0:T(8,128)(2,1)} %pad_maximum_fusion), calls=%async_computation.1 | async-start | bytes 2621440 | tf_op jit(solution)/shard_map/all_to_all | solution.py:61
  67.3 33.3 %all-to-all-done.1 = bf16[32,35,512]{2,1,0:T(8,128)(2,1)S(1)} async-done(((bf16[32,35,512]{2,1,0:T(8,128)(2,1)}), bf16[32,35,512]{2,1,0:T(8,128)(2,1)S(1)}, u32[]{:S(2)}, u32[]{:S(2)}) %all-to-all-start.1) | async-done | bytes 1146912 | tf_op jit(solution)/shard_map/all_to_all | solution.py:61
  100.5 3.4 %copy.138 = bf16[32,35,512]{0,2,1:T(8,128)(2,1)} copy(bf16[32,35,512]{2,1,0:T(8,128)(2,1)S(1)} %all-to-all-done.1) | data formatting | bytes 2293760 | tf_op jit(solution)/shard_map/all_to_all | solution.py:61
  104.0 7.0 %convert_element_type.57 = f32[32,35,512]{0,2,1:T(8,128)} convert(bf16[32,35,512]{0,2,1:T(8,128)(2,1)} %copy.138) | non-fusion elementwise | flops 573440 | bytes 3440640 | tf_op jit(solution)/shard_map/convert_element_type | solution.py:61
  110.9 2.7 %fusion.40 = (f32[8,2,512]{0,2,1:T(8,128)}, f32[8,2,512]{0,2,1:T(8,128)}, f32[8,2,512]{0,2,1:T(8,128)S(1)}, f32[8,2,512]{0,2,1:T(8,128)S(1)}) fusion(bf16[32,35,512]{0,2,1:T(8,128)(2,1)} %copy.138), kind=kLoop, calls=%fused_computation.65 | loop fusion | bytes 262144 | tf_op jit(solution)/shard_map/slice | solution.py:68
  114.6 11.1 %select_reduce_fusion.1 = (f32[32,512]{1,0:T(8,128)S(1)}, f32[32,512]{1,0:T(8,128)S(1)}, f32[32,512]{1,0:T(8,128)S(1)}, f32[32,512]{1,0:T(8,128)S(1)}) fusion(f32[32,35,512]{0,2,1:T(8,128)} %convert_element_type.57, pred[32,32]{0,1:T(8,128)(4,1)S(1)} %bitcast.97, pred[32,32]{0,1:T(8,128)(4,1)S(1)} %bitcast.96, pred[32,32]{0,1:T(8,128)(4,1)S(1)} %bitcast.98, ...), kind=kLoop, calls=%fused_computation.2 | loop fusion | flops 4128768 | bytes 2363392 | tf_op jit(solution)/shard_map/reduce_sum | solution.py:68
  126.5 5.6 %all-to-all-start.2 = ((bf16[32,16,512]{2,1,0:T(8,128)(2,1)}), bf16[32,16,512]{2,1,0:T(8,128)(2,1)S(1)}, u32[]{:S(2)}, u32[]{:S(2)}) async-start(bf16[32,16,512]{2,1,0:T(8,128)(2,1)} %broadcast_in_dim.90), calls=%async_computation.2 | async-start | bytes 1048576 | tf_op jit(solution)/shard_map/all_to_all | solution.py:13
  133.3 22.0 %all-gather.3.cloned.1.call-done = bf16[128,16,512]{2,1,0:T(8,128)(2,1)} async-done(((bf16[4,16,512]{2,1,0:T(8,128)(2,1)}), bf16[128,16,512]{2,1,0:T(8,128)(2,1)}) %all-gather.3.cloned.1.call-update) | async-done | bytes 2097168 | tf_op jit(solution)/shard_map/all_gather | solution.py:46
  155.2 2.9 %fusion.41 = (bf16[32,1,16,512]{3,2,1,0:T(8,128)(2,1)}, bf16[32,1,16,512]{3,2,1,0:T(8,128)(2,1)}, bf16[32,1,16,512]{3,2,1,0:T(8,128)(2,1)}, bf16[32,1,16,512]{3,2,1,0:T(8,128)(2,1)}) fusion(bf16[32,4,16,512]{3,2,1,0:T(8,128)(2,1)} %bitcast.78), kind=kLoop, calls=%fused_computation.66 | loop fusion | bytes 4194304 | tf_op jit(solution)/shard_map/slice | solution.py:87
  161.7 6.2 %all-to-all-start.3 = ((bf16[32,16,512]{2,1,0:T(8,128)(2,1)}), bf16[32,16,512]{2,1,0:T(8,128)(2,1)}, u32[]{:S(2)}, u32[]{:S(2)}) async-start(bf16[32,16,512]{2,1,0:T(8,128)(2,1)} %broadcast_in_dim.94), calls=%async_computation.3 | async-start | bytes 1048576 | tf_op jit(solution)/shard_map/all_to_all | solution.py:13
  170.6 13.0 %all-to-all-done.3 = bf16[32,16,512]{2,1,0:T(8,128)(2,1)} async-done(((bf16[32,16,512]{2,1,0:T(8,128)(2,1)}), bf16[32,16,512]{2,1,0:T(8,128)(2,1)}, u32[]{:S(2)}, u32[]{:S(2)}) %all-to-all-start.3) | async-done | bytes 524320 | tf_op jit(solution)/shard_map/all_to_all | solution.py:13
  187.3 4.6 %all-to-all-start.4 = ((bf16[32,16,512]{2,1,0:T(8,128)(2,1)}), bf16[32,16,512]{2,1,0:T(8,128)(2,1)}, u32[]{:S(2)}, u32[]{:S(2)}) async-start(bf16[32,16,512]{2,1,0:T(8,128)(2,1)} %broadcast_in_dim.98), calls=%async_computation.4 | async-start | bytes 1048576 | tf_op jit(solution)/shard_map/all_to_all | solution.py:13
  195.8 11.2 %all-to-all-done.4 = bf16[32,16,512]{2,1,0:T(8,128)(2,1)} async-done(((bf16[32,16,512]{2,1,0:T(8,128)(2,1)}), bf16[32,16,512]{2,1,0:T(8,128)(2,1)}, u32[]{:S(2)}, u32[]{:S(2)}) %all-to-all-start.4) | async-done | bytes 524320 | tf_op jit(solution)/shard_map/all_to_all | solution.py:13
  210.7 4.8 %all-to-all-start.5 = ((bf16[32,16,512]{2,1,0:T(8,128)(2,1)}), bf16[32,16,512]{2,1,0:T(8,128)(2,1)}, u32[]{:S(2)}, u32[]{:S(2)}) async-start(bf16[32,16,512]{2,1,0:T(8,128)(2,1)} %broadcast_in_dim.102), calls=%async_computation.5 | async-start | bytes 1048576 | tf_op jit(solution)/shard_map/all_to_all | solution.py:13
  215.5 2.9 %copy.148 = f32[1024,512]{1,0:T(8,128)} copy(f32[1024,512]{0,1:T(8,128)} %copy-done.8) | data formatting | bytes 4194304
  220.0 2.2 copy.142
  222.3 2.4 copy.145
  226.3 2.5 %copy.146 = f32[1,32,8,2,512]{4,2,3,1,0:T(8,128)} copy(f32[1,32,8,2,512]{4,3,2,1,0:T(2,128)} %stack.14) | data formatting | bytes 2097152 | tf_op jit(solution)/shard_map/stack | solution.py:91
  230.4 2.5 %copy.147 = f32[1,32,8,2,512]{4,2,3,1,0:T(8,128)} copy(f32[1,32,8,2,512]{4,3,2,1,0:T(2,128)} %stack.15) | data formatting | bytes 2097152 | tf_op jit(solution)/shard_map/stack | solution.py:91
  (94 shorter events, 44.2 us)
Async XLA Ops:
  7.2 41.4 %copy-start = (bf16[1024,1024]{1,0:T(8,128)(2,1)S(1)}, bf16[1024,1024]{1,0:T(8,128)(2,1)}, u32[]{:S(2)}) copy-start(bf16[1024,1024]{1,0:T(8,128)(2,1)} %param.12) | copy-start | bytes 6291460
  9.0 23.0 %all-to-all-start = ((bf16[32,2,1536]{2,1,0:T(2,128)(2,1)}), bf16[32,2,1536]{2,1,0:T(2,128)(2,1)S(1)}, u32[]{:S(2)}, u32[]{:S(2)}) async-start(bf16[32,2,1536]{2,1,0:T(2,128)(2,1)} %reshape.150), calls=%async_computation | async-start | bytes 393216 | tf_op jit(solution)/shard_map/all_to_all | solution.py:37
  48.5 4.4 %copy-start.14 = (bf16[1,2,512,1024]{3,2,1,0:T(8,128)(2,1)S(1)}, bf16[1,2,512,1024]{3,2,1,0:T(8,128)(2,1)}, u32[]{:S(2)}) copy-start(bf16[1,2,512,1024]{3,2,1,0:T(8,128)(2,1)} %param.13) | copy-start | bytes 6291460
  51.6 1.3 copy-start.8
  61.5 39.0 %all-to-all-start.1 = ((bf16[32,35,512]{2,1,0:T(8,128)(2,1)}), bf16[32,35,512]{2,1,0:T(8,128)(2,1)S(1)}, u32[]{:S(2)}, u32[]{:S(2)}) async-start(bf16[32,35,512]{2,1,0:T(8,128)(2,1)} %pad_maximum_fusion), calls=%async_computation.1 | async-start | bytes 2621440 | tf_op jit(solution)/shard_map/all_to_all | solution.py:61
  65.5 89.7 %all-gather.3.cloned.1.call-start = ((), (), s32[]{:S(2)}) async-start(), calls=%async_computation.6 | async-start | bytes 2162688 | tf_op jit(solution)/shard_map/all_gather | solution.py:46
  114.6 17.6 %copy-start.10 = (bf16[8,4,2,1536]{3,1,2,0:T(4,128)(2,1)S(1)}, bf16[8,4,2,1536]{3,1,2,0:T(4,128)(2,1)}, u32[]{:S(2)}) copy-start(bf16[8,4,2,1536]{3,1,2,0:T(4,128)(2,1)} %all_gather.9) | copy-start | bytes 589828
  126.5 31.6 %all-to-all-start.2 = ((bf16[32,16,512]{2,1,0:T(8,128)(2,1)}), bf16[32,16,512]{2,1,0:T(8,128)(2,1)S(1)}, u32[]{:S(2)}, u32[]{:S(2)}) async-start(bf16[32,16,512]{2,1,0:T(8,128)(2,1)} %broadcast_in_dim.90), calls=%async_computation.2 | async-start | bytes 1048576 | tf_op jit(solution)/shard_map/all_to_all | solution.py:13
  158.1 0.8 copy-start.9
  158.9 9.0 %copy-start.13 = (s32[4,2]{0,1:T(2,128)S(1)}, s32[4,2]{0,1:T(2,128)}, u32[]{:S(2)}) copy-start(s32[4,2]{0,1:T(2,128)} %param.19) | copy-start | bytes 100
  158.9 10.2 %copy-start.12 = (bf16[1,16,1024]{2,0,1:T(2,128)(2,1)S(1)}, bf16[1,16,1024]{2,0,1:T(2,128)(2,1)}, u32[]{:S(2)}) copy-start(bf16[1,16,1024]{2,0,1:T(2,128)(2,1)} %get-tuple-element.50) | copy-start | bytes 98308
  161.7 22.0 %all-to-all-start.3 = ((bf16[32,16,512]{2,1,0:T(8,128)(2,1)}), bf16[32,16,512]{2,1,0:T(8,128)(2,1)}, u32[]{:S(2)}, u32[]{:S(2)}) async-start(bf16[32,16,512]{2,1,0:T(8,128)(2,1)} %broadcast_in_dim.94), calls=%async_computation.3 | async-start | bytes 1048576 | tf_op jit(solution)/shard_map/all_to_all | solution.py:13
  183.6 9.4 %copy-start.11 = (bf16[1,16,1024]{2,0,1:T(2,128)(2,1)S(1)}, bf16[1,16,1024]{2,0,1:T(2,128)(2,1)}, u32[]{:S(2)}) copy-start(bf16[1,16,1024]{2,0,1:T(2,128)(2,1)} %get-tuple-element.51) | copy-start | bytes 98308
  185.3 1.0 copy-start.1
  187.3 19.6 %all-to-all-start.4 = ((bf16[32,16,512]{2,1,0:T(8,128)(2,1)}), bf16[32,16,512]{2,1,0:T(8,128)(2,1)}, u32[]{:S(2)}, u32[]{:S(2)}) async-start(bf16[32,16,512]{2,1,0:T(8,128)(2,1)} %broadcast_in_dim.98), calls=%async_computation.4 | async-start | bytes 1048576 | tf_op jit(solution)/shard_map/all_to_all | solution.py:13
  208.6 1.0 copy-start.3
  210.7 22.3 %all-to-all-start.5 = ((bf16[32,16,512]{2,1,0:T(8,128)(2,1)}), bf16[32,16,512]{2,1,0:T(8,128)(2,1)}, u32[]{:S(2)}, u32[]{:S(2)}) async-start(bf16[32,16,512]{2,1,0:T(8,128)(2,1)} %broadcast_in_dim.102), calls=%async_computation.5 | async-start | bytes 1048576 | tf_op jit(solution)/shard_map/all_to_all | solution.py:13
  220.0 4.6 %copy-start.2 = (f32[512,512]{1,0:T(8,128)S(1)}, f32[512,512]{1,0:T(8,128)}, u32[]{:S(2)}) copy-start(f32[512,512]{1,0:T(8,128)} %copy-done.1) | copy-start | bytes 3145732
  226.3 2.5 %copy-start.4 = (f32[512,512]{1,0:T(8,128)S(1)}, f32[512,512]{1,0:T(8,128)}, u32[]{:S(2)}) copy-start(f32[512,512]{1,0:T(8,128)} %copy-done.3) | copy-start | bytes 3145732
  230.4 4.3 %copy-start.5 = (f32[1,32,8,2,512]{4,2,3,1,0:T(8,128)S(1)}, f32[1,32,8,2,512]{4,2,3,1,0:T(8,128)}, u32[]{:S(2)}) copy-start(f32[1,32,8,2,512]{4,2,3,1,0:T(8,128)} %copy.145) | copy-start | bytes 3145732
  232.9 1.8 copy-start.6
  232.9 1.9 copy-start.7
Sparse Core Ops, SparseCore 0:
  69.5 85.7 all-gather.2

commit v6 on v5

--- a/solution.py
+++ b/solution.py
@@ -39,7 +39,6 @@
     owned = owned.reshape(STEPS, PAIR, width // block, n_src, n_row, PAIR)
     owned = owned.transpose(0, 1, 2, 4, 3, 5).reshape(STEPS, PAIR, width)
     owned = lax.all_gather(owned, "src", axis=0, tiled=False)
-    owned, sub_source = lax.optimization_barrier((owned, sub_source))
     owned = owned.transpose(1, 0, 2, 3).reshape(STEPS, span, width)
     lower_rows = owned[:, :, : LINKS * block]
     inverse_rows = owned[:, :, LINKS * block :]
@@ -52,13 +51,13 @@
     updates = jnp.einsum(
         "lmf,ft->lmt", coupling[0], rounded, preferred_element_type=jnp.float32
     )
-    per_dest = updates.astype(jnp.bfloat16).reshape(LINKS, n_src, n_row, PAIR, cols)
-    per_dest = per_dest.transpose(2, 0, 1, 3, 4).reshape(n_row, LINKS * span, cols)
-    src_rows = sep_source.astype(jnp.bfloat16).reshape(n_row, PAIR, cols)
-    lists = jnp.zeros((cols,), jnp.bfloat16).at[:LINKS].set(update_lists[0].astype(jnp.bfloat16))
+    per_dest = updates.reshape(LINKS, n_src, n_row, PAIR, cols).transpose(2, 0, 1, 3, 4)
+    per_dest = per_dest.reshape(n_row, LINKS * span, cols)
+    src_rows = sep_source.reshape(n_row, PAIR, cols)
+    lists = jnp.zeros((cols,), jnp.float32).at[:LINKS].set(update_lists[0].astype(jnp.float32))
     lists = jnp.broadcast_to(lists[None, None], (n_row, 1, cols))
     payload = jnp.concatenate([per_dest, src_rows, lists], axis=1)
-    got = lax.all_to_all(payload, "row", 0, 0, tiled=False).astype(jnp.float32)
+    got = lax.all_to_all(payload, "row", 0, 0, tiled=False)
     got_updates = got[:, : LINKS * span].reshape(n_row, LINKS, span, cols)
     got_src = got[:, LINKS * span : LINKS * span + PAIR].reshape(STEPS, span, cols)
     got_lists = got[:, LINKS * span + PAIR, :LINKS]

time: 245 us -> 242 us (0.988)
  other arithmetic: 24.2 us -> 8.41 us
  waiting for transfers between devices: 88.8 us -> 99.6 us
  starting transfers between devices: 36.8 us -> 42.9 us
  local copies, waits for them, and re-layouts: 50.4 us -> 46.5 us
    all_to_all x1, waiting for transfers between devices: 33.3 us -> 47.7 us  [per_device(): got = lax.all_to_all(payload, 'row', 0, 0, tiled=False)]
    all_to_all x1, waiting for transfers between devices: 9.34 us -> 0.01 us  [per_device(): lax.all_to_all(factors.reshape(n_row, PAIR, width), 'row', 0, 0, tiled=Fa...]
    convert_element_type x3 -> x1, other arithmetic: 8.54 us -> 0.01 us  [per_device(): update_lists[0].astype(jnp.float32)]
    reduce_sum x5, other arithmetic: 11.1 us -> 2.92 us  [per_device(): jnp.sum(jnp.where(hit, got_updates, 0.0), axis=(0, 1))]
    all_to_all x1, starting transfers between devices: 3.95 us -> 10 us  [per_device(): got = lax.all_to_all(payload, 'row', 0, 0, tiled=False)]
    all_gather x1, waiting for transfers between devices: 22 us -> 26.8 us  [per_device(): inverse_all = lax.all_gather(inverse_rows, 'row', axis=0, tiled=False)]
    reshape x3, local copies, waits for them, and re-layouts: 2.96 us -> 7.28 us  [the longest x1 3.72 us: per_device(): per_dest = per_dest.reshape(n_row, LINKS * span, cols)]
    slice x5 -> x1, local copies, waits for them, and re-layouts: 5.44 us -> 1.13 us  [per_device(): got_src[k] - jnp.sum(jnp.where(hit, got_updates, 0.0), axis=(0, 1))]
  transfers between devices with their start and end apart: 7 -> 7, of which waited for: 5 -> 4; matrix products, arithmetic and copies ran while one was open for 23% -> 22% of each run, Pallas kernels for 0% -> 0%
where the time goes in v6:
time: 242 us; the launch traced here: 240 us
  waiting for transfers between devices  99.6 us (41%)
  local copies, waits for them, and re-layouts  46.5 us (19%)
  starting transfers between devices  42.9 us (18%)
  between operations  16.2 us (7%)
  matrix products  14.5 us (6%)
  blocking collectives  11.6 us (5%)
  other arithmetic  8.41 us (3%)
    all_to_all x1, waiting for transfers between devices, per_device(): got = lax.all_to_all(payload, 'row', 0, 0, tiled=False)  47.7 us
    all_gather x1, waiting for transfers between devices, per_device(): inverse_all = lax.all_gather(inverse_rows, 'row', axis=0, tiled=False)  26.8 us
    all_to_all x4, waiting for transfers between devices, gather_row(): return lax.all_to_all(spread, 'row', 0, 0, tiled=False)  25 us
    all_to_all x4, starting transfers between devices, gather_row(): return lax.all_to_all(spread, 'row', 0, 0, tiled=False)  21.5 us
    another operation x6, local copies, waits for them, and re-layouts, per_device(): solved = jnp.stack(fields, axis=0)  12.3 us
    all_gather x1, blocking collectives, per_device(): owned = lax.all_gather(owned, 'src', axis=0, tiled=False)  11.6 us
    all_to_all x1, starting transfers between devices, per_device(): lax.all_to_all(factors.reshape(n_row, PAIR, width), 'row', 0, 0, tiled=Fa...  11.3 us
    all_to_all x1, starting transfers between devices, per_device(): got = lax.all_to_all(payload, 'row', 0, 0, tiled=False)  10 us
  transfers between devices with their start and end apart: 7, of which 4 were waited for; matrix products, arithmetic and copies ran while one was open for 22% of the time, Pallas kernels for 0%

profile of v6, /device:TPU:16, one launch (start us, length us, event | category | flops | bytes accessed | tf_op | source)
XLA Modules:
  0.0 239.6 jit_solution(3484683169012590830)
XLA Ops:
  9.0 11.3 %all-to-all-start = ((bf16[32,2,1536]{2,1,0:T(2,128)(2,1)}), bf16[32,2,1536]{2,1,0:T(2,128)(2,1)S(1)}, u32[]{:S(2)}, u32[]{:S(2)}) async-start(bf16[32,2,1536]{2,1,0:T(2,128)(2,1)} %reshape.150), calls=%async_computation | async-start | bytes 393216 | tf_op jit(solution)/shard_map/all_to_all | solution.py:37
  20.4 3.0 %fusion.10 = f32[1024,512]{1,0:T(8,128)S(1)} fusion(bf16[1024,1024]{1,0:T(8,128)(2,1)S(1)} %copy-done, f32[1024,512]{1,0:T(8,128)} %param.11), kind=kOutput, calls=%fused_computation.24 | convolution fusion | flops 1074266112 | bytes 6291456 | tf_op jit(solution)/shard_map/dot_general | solution.py:47
  24.7 2.6 %fusion.2 = f32[2,512,512]{2,1,0:T(8,128)} fusion(bf16[1,2,512,1024]{3,2,1,0:T(8,128)(2,1)S(1)} %copy-done.12, f32[1024,512]{1,0:T(8,128)S(1)} %fusion.10), kind=kOutput, calls=%fused_computation.12 | convolution fusion | flops 1074266112 | bytes 6291456 | tf_op jit(solution)/shard_map/lmf,ft->lmt/dot_general | solution.py:51
  27.3 3.5 %reshape.153 = f32[2,8,32,2,512]{4,3,2,1,0:T(2,128)} reshape(f32[2,512,512]{2,1,0:T(8,128)} %fusion.2) | data formatting | bytes 4194304 | tf_op jit(solution)/shard_map/reshape | solution.py:54
  30.8 4.1 %copy.110 = f32[32,2,8,2,512]{4,3,2,1,0:T(2,128)} copy(f32[32,2,8,2,512]{4,3,0,2,1:T(2,128)} %bitcast.71) | data formatting | bytes 4194304 | tf_op jit(solution)/shard_map/transpose | solution.py:54
  34.9 3.7 %reshape.154 = f32[32,32,512]{2,1,0:T(8,128)} reshape(f32[32,2,8,2,512]{4,3,2,1,0:T(2,128)} %copy.110) | data formatting | bytes 4194304 | tf_op jit(solution)/shard_map/reshape | solution.py:55
  38.8 3.5 %pad_maximum_fusion = f32[32,35,512]{2,1,0:T(8,128)} fusion(f32[32,1,512]{2,1,0:T(1,128)S(1)} %broadcast_in_dim.85, f32[32,2,512]{2,1,0:T(2,128)S(1)} %reshape.155, f32[32,32,512]{2,1,0:T(8,128)} %reshape.154), kind=kLoop, calls=%fused_computation.5 | loop fusion | flops 1146880 | bytes 4587520 | tf_op jit(solution)/shard_map/concatenate | solution.py:59
  42.3 10.0 %all-to-all-start.1 = ((f32[32,35,512]{2,1,0:T(8,128)}), f32[32,35,512]{2,1,0:T(8,128)}, u32[]{:S(2)}, u32[]{:S(2)}) async-start(f32[32,35,512]{2,1,0:T(8,128)} %pad_maximum_fusion), calls=%async_computation.1 | async-start | bytes 5242880 | tf_op jit(solution)/shard_map/all_to_all | solution.py:60
  56.3 11.6 %all_gather.9 = bf16[8,4,2,1536]{3,1,2,0:T(4,128)(2,1)S(1)} all-gather(bf16[1,4,2,1536]{3,1,2,0:T(4,128)(2,1)S(1)} %copy.108), channel_id=1, replica_groups=mesh['row'=32,'src'=8] {'src'}, dimensions={0}, use_global_device_ids=true | all-gather | bytes 221184 | tf_op jit(solution)/shard_map/all_gather | solution.py:41
  68.6 47.7 %all-to-all-done.1 = f32[32,35,512]{2,1,0:T(8,128)} async-done(((f32[32,35,512]{2,1,0:T(8,128)}), f32[32,35,512]{2,1,0:T(8,128)}, u32[]{:S(2)}, u32[]{:S(2)}) %all-to-all-start.1) | async-done | bytes 2293792 | tf_op jit(solution)/shard_map/all_to_all | solution.py:60
  117.7 2.9 %select_reduce_fusion.1 = (f32[32,512]{1,0:T(8,128)S(1)}, f32[32,512]{1,0:T(8,128)S(1)}, f32[32,512]{1,0:T(8,128)S(1)}, f32[32,512]{1,0:T(8,128)S(1)}) fusion(f32[32,35,512]{2,1,0:T(8,128)} %all-to-all-done.1, pred[32,32]{1,0:T(8,128)(4,1)S(1)} %copy.114, pred[32,32]{1,0:T(8,128)(4,1)S(1)} %copy.113, pred[32,32]{1,0:T(8,128)(4,1)S(1)} %copy.116, ...), kind=kLoop, calls=%fused_computation.9 | loop fusion | flops 4128768 | bytes 2363392 | tf_op jit(solution)/shard_map/reduce_sum | solution.py:67
  122.7 5.3 %all-to-all-start.2 = ((bf16[32,16,512]{2,1,0:T(8,128)(2,1)}), bf16[32,16,512]{2,1,0:T(8,128)(2,1)S(1)}, u32[]{:S(2)}, u32[]{:S(2)}) async-start(bf16[32,16,512]{2,1,0:T(8,128)(2,1)} %broadcast_in_dim.90), calls=%async_computation.2 | async-start | bytes 1048576 | tf_op jit(solution)/shard_map/all_to_all | solution.py:13
  128.8 26.8 %all-gather.3.cloned.1.call-done = bf16[128,16,512]{2,1,0:T(8,128)(2,1)} async-done(((bf16[4,16,512]{2,1,0:T(8,128)(2,1)}), bf16[128,16,512]{2,1,0:T(8,128)(2,1)}) %all-gather.3.cloned.1.call-update) | async-done | bytes 2097168 | tf_op jit(solution)/shard_map/all_gather | solution.py:45
  155.6 2.9 %fusion.39 = (bf16[32,1,16,512]{3,2,1,0:T(8,128)(2,1)}, bf16[32,1,16,512]{3,2,1,0:T(8,128)(2,1)}, bf16[32,1,16,512]{3,2,1,0:T(8,128)(2,1)}, bf16[32,1,16,512]{3,2,1,0:T(8,128)(2,1)}) fusion(bf16[32,4,16,512]{3,2,1,0:T(8,128)(2,1)} %bitcast.74), kind=kLoop, calls=%fused_computation.65 | loop fusion | bytes 4194304 | tf_op jit(solution)/shard_map/slice | solution.py:86
  162.0 6.8 %all-to-all-start.3 = ((bf16[32,16,512]{2,1,0:T(8,128)(2,1)}), bf16[32,16,512]{2,1,0:T(8,128)(2,1)}, u32[]{:S(2)}, u32[]{:S(2)}) async-start(bf16[32,16,512]{2,1,0:T(8,128)(2,1)} %broadcast_in_dim.94), calls=%async_computation.3 | async-start | bytes 1048576 | tf_op jit(solution)/shard_map/all_to_all | solution.py:13
  170.3 13.5 %all-to-all-done.3 = bf16[32,16,512]{2,1,0:T(8,128)(2,1)} async-done(((bf16[32,16,512]{2,1,0:T(8,128)(2,1)}), bf16[32,16,512]{2,1,0:T(8,128)(2,1)}, u32[]{:S(2)}, u32[]{:S(2)}) %all-to-all-start.3) | async-done | bytes 524320 | tf_op jit(solution)/shard_map/all_to_all | solution.py:13
  187.5 4.6 %all-to-all-start.4 = ((bf16[32,16,512]{2,1,0:T(8,128)(2,1)}), bf16[32,16,512]{2,1,0:T(8,128)(2,1)}, u32[]{:S(2)}, u32[]{:S(2)}) async-start(bf16[32,16,512]{2,1,0:T(8,128)(2,1)} %broadcast_in_dim.98), calls=%async_computation.4 | async-start | bytes 1048576 | tf_op jit(solution)/shard_map/all_to_all | solution.py:13
  194.8 11.5 %all-to-all-done.4 = bf16[32,16,512]{2,1,0:T(8,128)(2,1)} async-done(((bf16[32,16,512]{2,1,0:T(8,128)(2,1)}), bf16[32,16,512]{2,1,0:T(8,128)(2,1)}, u32[]{:S(2)}, u32[]{:S(2)}) %all-to-all-start.4) | async-done | bytes 524320 | tf_op jit(solution)/shard_map/all_to_all | solution.py:13
  210.0 4.8 %all-to-all-start.5 = ((bf16[32,16,512]{2,1,0:T(8,128)(2,1)}), bf16[32,16,512]{2,1,0:T(8,128)(2,1)}, u32[]{:S(2)}, u32[]{:S(2)}) async-start(bf16[32,16,512]{2,1,0:T(8,128)(2,1)} %broadcast_in_dim.102), calls=%async_computation.5 | async-start | bytes 1048576 | tf_op jit(solution)/shard_map/all_to_all | solution.py:13
  214.8 2.2 copy.115
  218.6 2.5 %copy.118 = f32[1,32,8,2,512]{4,2,3,1,0:T(8,128)} copy(f32[1,32,8,2,512]{4,3,2,1,0:T(2,128)} %stack.13) | data formatting | bytes 2097152 | tf_op jit(solution)/shard_map/stack | solution.py:90
  222.7 2.5 %copy.119 = f32[1,32,8,2,512]{4,2,3,1,0:T(8,128)} copy(f32[1,32,8,2,512]{4,3,2,1,0:T(2,128)} %stack.14) | data formatting | bytes 2097152 | tf_op jit(solution)/shard_map/stack | solution.py:90
  226.8 2.5 %copy.120 = f32[1,32,8,2,512]{4,2,3,1,0:T(8,128)} copy(f32[1,32,8,2,512]{4,3,2,1,0:T(2,128)} %stack.15) | data formatting | bytes 2097152 | tf_op jit(solution)/shard_map/stack | solution.py:90
  229.3 1.8 convolution_bitcast_fusion
  (94 shorter events, 31.8 us)
Async XLA Ops:
  7.2 13.2 %copy-start = (bf16[1024,1024]{1,0:T(8,128)(2,1)S(1)}, bf16[1024,1024]{1,0:T(8,128)(2,1)}, u32[]{:S(2)}) copy-start(bf16[1024,1024]{1,0:T(8,128)(2,1)} %param.12) | copy-start | bytes 6291460
  9.0 33.3 %all-to-all-start = ((bf16[32,2,1536]{2,1,0:T(2,128)(2,1)}), bf16[32,2,1536]{2,1,0:T(2,128)(2,1)S(1)}, u32[]{:S(2)}, u32[]{:S(2)}) async-start(bf16[32,2,1536]{2,1,0:T(2,128)(2,1)} %reshape.150), calls=%async_computation | async-start | bytes 393216 | tf_op jit(solution)/shard_map/all_to_all | solution.py:37
  20.4 4.3 %copy-start.12 = (bf16[1,2,512,1024]{3,2,1,0:T(8,128)(2,1)S(1)}, bf16[1,2,512,1024]{3,2,1,0:T(8,128)(2,1)}, u32[]{:S(2)}) copy-start(bf16[1,2,512,1024]{3,2,1,0:T(8,128)(2,1)} %param.13) | copy-start | bytes 6291460
  23.4 1.3 copy-start.15
  34.9 3.7 %copy-start.9 = (f32[64,512]{1,0:T(8,128)S(1)}, f32[64,512]{1,0:T(8,128)}, u32[]{:S(2)}) copy-start(f32[64,512]{1,0:T(8,128)} %param.15) | copy-start | bytes 393220
  34.9 3.8 %copy-start.13 = (s32[1,2]{1,0:T(1,128)S(1)}, s32[1,2]{1,0:T(1,128)}, u32[]{:S(2)}) copy-start(s32[1,2]{1,0:T(1,128)} %param.14) | copy-start | bytes 28
  42.3 10.1 %copy-start.14 = (s32[4]{0:T(128)S(1)}, s32[4]{0:T(128)}, u32[]{:S(2)}) copy-start(s32[4]{0:T(128)} %param.18) | copy-start | bytes 52
  42.3 74.0 %all-to-all-start.1 = ((f32[32,35,512]{2,1,0:T(8,128)}), f32[32,35,512]{2,1,0:T(8,128)}, u32[]{:S(2)}, u32[]{:S(2)}) async-start(f32[32,35,512]{2,1,0:T(8,128)} %pad_maximum_fusion), calls=%async_computation.1 | async-start | bytes 5242880 | tf_op jit(solution)/shard_map/all_to_all | solution.py:60
  52.3 103.3 %all-gather.3.cloned.1.call-start = ((), (), s32[]{:S(2)}) async-start(), calls=%async_computation.6 | async-start | bytes 2162688 | tf_op jit(solution)/shard_map/all_gather | solution.py:45
  122.7 35.8 %all-to-all-start.2 = ((bf16[32,16,512]{2,1,0:T(8,128)(2,1)}), bf16[32,16,512]{2,1,0:T(8,128)(2,1)S(1)}, u32[]{:S(2)}, u32[]{:S(2)}) async-start(bf16[32,16,512]{2,1,0:T(8,128)(2,1)} %broadcast_in_dim.90), calls=%async_computation.2 | async-start | bytes 1048576 | tf_op jit(solution)/shard_map/all_to_all | solution.py:13
  158.5 0.8 copy-start.8
  158.5 2.5 %copy-start.10 = (bf16[1,16,1024]{2,1,0:T(8,128)(2,1)S(1)}, bf16[1,16,1024]{2,1,0:T(8,128)(2,1)}, u32[]{:S(2)}) copy-start(bf16[1,16,1024]{2,1,0:T(8,128)(2,1)} %copy.134) | copy-start | bytes 98308
  159.3 9.6 %copy-start.11 = (s32[4,2]{0,1:T(2,128)S(1)}, s32[4,2]{0,1:T(2,128)}, u32[]{:S(2)}) copy-start(s32[4,2]{0,1:T(2,128)} %param.19) | copy-start | bytes 100
  162.0 21.9 %all-to-all-start.3 = ((bf16[32,16,512]{2,1,0:T(8,128)(2,1)}), bf16[32,16,512]{2,1,0:T(8,128)(2,1)}, u32[]{:S(2)}, u32[]{:S(2)}) async-start(bf16[32,16,512]{2,1,0:T(8,128)(2,1)} %broadcast_in_dim.94), calls=%async_computation.3 | async-start | bytes 1048576 | tf_op jit(solution)/shard_map/all_to_all | solution.py:13
  185.5 1.0 copy-start.1
  187.5 18.8 %all-to-all-start.4 = ((bf16[32,16,512]{2,1,0:T(8,128)(2,1)}), bf16[32,16,512]{2,1,0:T(8,128)(2,1)}, u32[]{:S(2)}, u32[]{:S(2)}) async-start(bf16[32,16,512]{2,1,0:T(8,128)(2,1)} %broadcast_in_dim.98), calls=%async_computation.4 | async-start | bytes 1048576 | tf_op jit(solution)/shard_map/all_to_all | solution.py:13
  207.9 1.0 copy-start.3
  210.0 19.4 %all-to-all-start.5 = ((bf16[32,16,512]{2,1,0:T(8,128)(2,1)}), bf16[32,16,512]{2,1,0:T(8,128)(2,1)}, u32[]{:S(2)}, u32[]{:S(2)}) async-start(bf16[32,16,512]{2,1,0:T(8,128)(2,1)} %broadcast_in_dim.102), calls=%async_computation.5 | async-start | bytes 1048576 | tf_op jit(solution)/shard_map/all_to_all | solution.py:13
  218.6 2.5 %copy-start.2 = (f32[512,512]{1,0:T(8,128)S(1)}, f32[512,512]{1,0:T(8,128)}, u32[]{:S(2)}) copy-start(f32[512,512]{1,0:T(8,128)} %copy-done.1) | copy-start | bytes 3145732
  222.7 2.5 %copy-start.4 = (f32[512,512]{1,0:T(8,128)S(1)}, f32[512,512]{1,0:T(8,128)}, u32[]{:S(2)}) copy-start(f32[512,512]{1,0:T(8,128)} %copy-done.3) | copy-start | bytes 3145732
  226.8 4.3 %copy-start.5 = (f32[1,32,8,2,512]{4,2,3,1,0:T(8,128)S(1)}, f32[1,32,8,2,512]{4,2,3,1,0:T(8,128)}, u32[]{:S(2)}) copy-start(f32[1,32,8,2,512]{4,2,3,1,0:T(8,128)} %copy.118) | copy-start | bytes 3145732
  229.3 1.8 copy-start.6
  229.3 1.9 copy-start.7
Sparse Core Ops, SparseCore 0:
  68.7 86.8 all-gather.2

commit v7 on v6

--- a/solution.py
+++ b/solution.py
@@ -87,14 +87,17 @@
         result = jnp.dot(inverse, full_residue, preferred_element_type=jnp.float32)
         fields.append(result)
         rounded_fields.append(result.astype(jnp.bfloat16))
-    solved = jnp.stack(fields, axis=0)
     blocks_per = block // local_rows
-    whole_field = solved.reshape(STEPS, n_row, n_src, PAIR, cols)
-    own_rows = lax.dynamic_slice(
-        whole_field,
-        (my_row // blocks_per, 0, my_row % blocks_per, 0, 0),
-        (1, n_row, 1, PAIR, cols),
-    ).reshape(local_rows, cols)
+    my_block = my_row // blocks_per
+    my_part = my_row % blocks_per
+    own_rows = jnp.zeros((local_rows, cols), jnp.float32)
+    for k in range(STEPS):
+        part = lax.dynamic_slice(
+            fields[k].reshape(n_row, n_src, PAIR, cols),
+            (0, my_part, 0, 0),
+            (n_row, 1, PAIR, cols),
+        ).reshape(local_rows, cols)
+        own_rows = jnp.where(my_block == k, part, own_rows)
     return (sub_field, own_rows)
 
 

time: 242 us -> 240 us (level)
  local copies, waits for them, and re-layouts: 46.5 us -> 43.2 us
    another operation x6 -> x0, local copies, waits for them, and re-layouts: 12.3 us -> none  [per_device(): solved = jnp.stack(fields, axis=0)]
    reshape x1 -> x3, local copies, waits for them, and re-layouts: 0.75 us -> 6.06 us  [per_device(): fields[k].reshape(n_row, n_src, PAIR, cols)]
    dynamic_slice x0 -> x3, local copies, waits for them, and re-layouts: none -> 2.83 us  [per_device(): lax.dynamic_slice(fields[k].reshape(n_row, n_src, PAIR, cols), (0, my_par...]
    unnamed x36 -> x28, local copies, waits for them, and re-layouts: 4.88 us -> 4.88 us
  transfers between devices with their start and end apart: 7 -> 7, of which waited for: 4 -> 5; matrix products, arithmetic and copies ran while one was open for 22% -> 20% of each run, Pallas kernels for 0% -> 0%
where the time goes in v7:
time: 240 us; the launch traced here: 238 us
  waiting for transfers between devices  101 us (42%)
  starting transfers between devices  43.3 us (18%)
  local copies, waits for them, and re-layouts  43.2 us (18%)
  between operations  16.4 us (7%)
  matrix products  14.3 us (6%)
  blocking collectives  11.6 us (5%)
  other arithmetic  8.27 us (3%)
    all_to_all x1, waiting for transfers between devices, per_device(): got = lax.all_to_all(payload, 'row', 0, 0, tiled=False)  47.7 us
    all_to_all x4, waiting for transfers between devices, gather_row(): return lax.all_to_all(spread, 'row', 0, 0, tiled=False)  27.2 us
    all_gather x1, waiting for transfers between devices, per_device(): inverse_all = lax.all_gather(inverse_rows, 'row', axis=0, tiled=False)  26.5 us
    all_to_all x4, starting transfers between devices, gather_row(): return lax.all_to_all(spread, 'row', 0, 0, tiled=False)  21.9 us
    all_gather x1, blocking collectives, per_device(): owned = lax.all_gather(owned, 'src', axis=0, tiled=False)  11.6 us
    all_to_all x1, starting transfers between devices, per_device(): lax.all_to_all(factors.reshape(n_row, PAIR, width), 'row', 0, 0, tiled=Fa...  11.3 us
    all_to_all x1, starting transfers between devices, per_device(): got = lax.all_to_all(payload, 'row', 0, 0, tiled=False)  10 us
    dot_general x4, matrix products, per_device(): result = jnp.dot(inverse, full_residue, preferred_element_type=jnp.float32)  6.56 us
  transfers between devices with their start and end apart: 7, of which 5 were waited for; matrix products, arithmetic and copies ran while one was open for 20% of the time, Pallas kernels for 0%

profile of v7, /device:TPU:16, one launch (start us, length us, event | category | flops | bytes accessed | tf_op | source)
XLA Modules:
  0.0 238.4 jit_solution(8356768279733029893)
XLA Ops:
  9.0 11.3 %all-to-all-start = ((bf16[32,2,1536]{2,1,0:T(2,128)(2,1)}), bf16[32,2,1536]{2,1,0:T(2,128)(2,1)S(1)}, u32[]{:S(2)}, u32[]{:S(2)}) async-start(bf16[32,2,1536]{2,1,0:T(2,128)(2,1)} %reshape.156), calls=%async_computation | async-start | bytes 393216 | tf_op jit(solution)/shard_map/all_to_all | solution.py:37
  20.4 3.0 %fusion.10 = f32[1024,512]{1,0:T(8,128)S(1)} fusion(bf16[1024,1024]{1,0:T(8,128)(2,1)S(1)} %copy-done, f32[1024,512]{1,0:T(8,128)} %param.11), kind=kOutput, calls=%fused_computation.19 | convolution fusion | flops 1074266112 | bytes 6291456 | tf_op jit(solution)/shard_map/dot_general | solution.py:47
  24.7 2.6 %fusion.2 = f32[2,512,512]{2,1,0:T(8,128)} fusion(bf16[1,2,512,1024]{3,2,1,0:T(8,128)(2,1)S(1)} %copy-done.8, f32[1024,512]{1,0:T(8,128)S(1)} %fusion.10), kind=kOutput, calls=%fused_computation.8 | convolution fusion | flops 1074266112 | bytes 6291456 | tf_op jit(solution)/shard_map/lmf,ft->lmt/dot_general | solution.py:51
  27.3 3.5 %reshape.159 = f32[2,8,32,2,512]{4,3,2,1,0:T(2,128)} reshape(f32[2,512,512]{2,1,0:T(8,128)} %fusion.2) | data formatting | bytes 4194304 | tf_op jit(solution)/shard_map/reshape | solution.py:54
  30.8 4.1 %copy.113 = f32[32,2,8,2,512]{4,3,2,1,0:T(2,128)} copy(f32[32,2,8,2,512]{4,3,0,2,1:T(2,128)} %bitcast.69) | data formatting | bytes 4194304 | tf_op jit(solution)/shard_map/transpose | solution.py:54
  34.9 3.7 %reshape.160 = f32[32,32,512]{2,1,0:T(8,128)} reshape(f32[32,2,8,2,512]{4,3,2,1,0:T(2,128)} %copy.113) | data formatting | bytes 4194304 | tf_op jit(solution)/shard_map/reshape | solution.py:55
  38.8 3.5 %pad_maximum_fusion = f32[32,35,512]{2,1,0:T(8,128)} fusion(f32[32,1,512]{2,1,0:T(1,128)S(1)} %broadcast_in_dim.88, f32[32,2,512]{2,1,0:T(2,128)S(1)} %reshape.161, f32[32,32,512]{2,1,0:T(8,128)} %reshape.160), kind=kLoop, calls=%fused_computation.1 | loop fusion | flops 1146880 | bytes 4587520 | tf_op jit(solution)/shard_map/concatenate | solution.py:59
  42.3 10.0 %all-to-all-start.1 = ((f32[32,35,512]{2,1,0:T(8,128)}), f32[32,35,512]{2,1,0:T(8,128)}, u32[]{:S(2)}, u32[]{:S(2)}) async-start(f32[32,35,512]{2,1,0:T(8,128)} %pad_maximum_fusion), calls=%async_computation.1 | async-start | bytes 5242880 | tf_op jit(solution)/shard_map/all_to_all | solution.py:60
  56.3 11.6 %all_gather.9 = bf16[8,4,2,1536]{3,1,2,0:T(4,128)(2,1)S(1)} all-gather(bf16[1,4,2,1536]{3,1,2,0:T(4,128)(2,1)S(1)} %copy.110), channel_id=1, replica_groups=mesh['row'=32,'src'=8] {'src'}, dimensions={0}, use_global_device_ids=true | all-gather | bytes 221184 | tf_op jit(solution)/shard_map/all_gather | solution.py:41
  68.6 47.7 %all-to-all-done.1 = f32[32,35,512]{2,1,0:T(8,128)} async-done(((f32[32,35,512]{2,1,0:T(8,128)}), f32[32,35,512]{2,1,0:T(8,128)}, u32[]{:S(2)}, u32[]{:S(2)}) %all-to-all-start.1) | async-done | bytes 2293792 | tf_op jit(solution)/shard_map/all_to_all | solution.py:60
  117.7 2.9 %select_reduce_fusion.3 = (f32[32,512]{1,0:T(8,128)S(1)}, f32[32,512]{1,0:T(8,128)S(1)}, f32[32,512]{1,0:T(8,128)S(1)}, f32[32,512]{1,0:T(8,128)S(1)}) fusion(f32[32,35,512]{2,1,0:T(8,128)} %all-to-all-done.1, pred[32,32]{1,0:T(8,128)(4,1)S(1)} %copy.115, pred[32,32]{1,0:T(8,128)(4,1)S(1)} %copy.116, pred[32,32]{1,0:T(8,128)(4,1)S(1)} %copy.117, ...), kind=kLoop, calls=%fused_computation.7 | loop fusion | flops 4128768 | bytes 2363392 | tf_op jit(solution)/shard_map/reduce_sum | solution.py:67
  122.7 5.2 %all-to-all-start.2 = ((bf16[32,16,512]{2,1,0:T(8,128)(2,1)}), bf16[32,16,512]{2,1,0:T(8,128)(2,1)S(1)}, u32[]{:S(2)}, u32[]{:S(2)}) async-start(bf16[32,16,512]{2,1,0:T(8,128)(2,1)} %broadcast_in_dim.99), calls=%async_computation.2 | async-start | bytes 1048576 | tf_op jit(solution)/shard_map/all_to_all | solution.py:13
  128.8 26.5 %all-gather.3.cloned.1.call-done = bf16[128,16,512]{2,1,0:T(8,128)(2,1)} async-done(((bf16[4,16,512]{2,1,0:T(8,128)(2,1)}), bf16[128,16,512]{2,1,0:T(8,128)(2,1)}) %all-gather.3.cloned.1.call-update) | async-done | bytes 2097168 | tf_op jit(solution)/shard_map/all_gather | solution.py:45
  155.3 2.9 %fusion.37 = (bf16[32,1,16,512]{3,2,1,0:T(8,128)(2,1)}, bf16[32,1,16,512]{3,2,1,0:T(8,128)(2,1)}, bf16[32,1,16,512]{3,2,1,0:T(8,128)(2,1)}, bf16[32,1,16,512]{3,2,1,0:T(8,128)(2,1)}) fusion(bf16[32,4,16,512]{3,2,1,0:T(8,128)(2,1)} %bitcast.72), kind=kLoop, calls=%fused_computation.65 | loop fusion | bytes 4194304 | tf_op jit(solution)/shard_map/slice | solution.py:86
  159.0 1.6 fusion.40
  161.7 7.2 %all-to-all-start.3 = ((bf16[32,16,512]{2,1,0:T(8,128)(2,1)}), bf16[32,16,512]{2,1,0:T(8,128)(2,1)}, u32[]{:S(2)}, u32[]{:S(2)}) async-start(bf16[32,16,512]{2,1,0:T(8,128)(2,1)} %broadcast_in_dim.100), calls=%async_computation.3 | async-start | bytes 1048576 | tf_op jit(solution)/shard_map/all_to_all | solution.py:13
  170.6 13.3 %all-to-all-done.3 = bf16[32,16,512]{2,1,0:T(8,128)(2,1)} async-done(((bf16[32,16,512]{2,1,0:T(8,128)(2,1)}), bf16[32,16,512]{2,1,0:T(8,128)(2,1)}, u32[]{:S(2)}, u32[]{:S(2)}) %all-to-all-start.3) | async-done | bytes 524320 | tf_op jit(solution)/shard_map/all_to_all | solution.py:13
  187.6 4.6 %all-to-all-start.4 = ((bf16[32,16,512]{2,1,0:T(8,128)(2,1)}), bf16[32,16,512]{2,1,0:T(8,128)(2,1)}, u32[]{:S(2)}, u32[]{:S(2)}) async-start(bf16[32,16,512]{2,1,0:T(8,128)(2,1)} %broadcast_in_dim.104), calls=%async_computation.4 | async-start | bytes 1048576 | tf_op jit(solution)/shard_map/all_to_all | solution.py:13
  195.0 11.1 %all-to-all-done.4 = bf16[32,16,512]{2,1,0:T(8,128)(2,1)} async-done(((bf16[32,16,512]{2,1,0:T(8,128)(2,1)}), bf16[32,16,512]{2,1,0:T(8,128)(2,1)}, u32[]{:S(2)}, u32[]{:S(2)}) %all-to-all-start.4) | async-done | bytes 524320 | tf_op jit(solution)/shard_map/all_to_all | solution.py:13
  209.9 4.8 %all-to-all-start.5 = ((bf16[32,16,512]{2,1,0:T(8,128)(2,1)}), bf16[32,16,512]{2,1,0:T(8,128)(2,1)}, u32[]{:S(2)}, u32[]{:S(2)}) async-start(bf16[32,16,512]{2,1,0:T(8,128)(2,1)} %broadcast_in_dim.105), calls=%async_computation.5 | async-start | bytes 1048576 | tf_op jit(solution)/shard_map/all_to_all | solution.py:13
  214.7 2.1 copy.112
  219.5 2.8 %reshape.167 = f32[32,8,2,512]{3,2,1,0:T(2,128)} reshape(f32[512,512]{1,0:T(8,128)} %copy-done.1) | data formatting | bytes 2097152 | tf_op jit(solution)/shard_map/reshape | solution.py:96
  225.8 2.7 %all-to-all-done.5 = bf16[32,16,512]{2,1,0:T(8,128)(2,1)} async-done(((bf16[32,16,512]{2,1,0:T(8,128)(2,1)}), bf16[32,16,512]{2,1,0:T(8,128)(2,1)}, u32[]{:S(2)}, u32[]{:S(2)}) %all-to-all-start.5) | async-done | bytes 524320 | tf_op jit(solution)/shard_map/all_to_all | solution.py:13
  228.5 1.7 fusion.12
  (86 shorter events, 31.3 us)
Async XLA Ops:
  7.2 13.2 %copy-start = (bf16[1024,1024]{1,0:T(8,128)(2,1)S(1)}, bf16[1024,1024]{1,0:T(8,128)(2,1)}, u32[]{:S(2)}) copy-start(bf16[1024,1024]{1,0:T(8,128)(2,1)} %param.12) | copy-start | bytes 6291460
  9.0 33.3 %all-to-all-start = ((bf16[32,2,1536]{2,1,0:T(2,128)(2,1)}), bf16[32,2,1536]{2,1,0:T(2,128)(2,1)S(1)}, u32[]{:S(2)}, u32[]{:S(2)}) async-start(bf16[32,2,1536]{2,1,0:T(2,128)(2,1)} %reshape.156), calls=%async_computation | async-start | bytes 393216 | tf_op jit(solution)/shard_map/all_to_all | solution.py:37
  20.4 4.3 %copy-start.8 = (bf16[1,2,512,1024]{3,2,1,0:T(8,128)(2,1)S(1)}, bf16[1,2,512,1024]{3,2,1,0:T(8,128)(2,1)}, u32[]{:S(2)}) copy-start(bf16[1,2,512,1024]{3,2,1,0:T(8,128)(2,1)} %param.13) | copy-start | bytes 6291460
  23.4 1.3 copy-start.11
  34.9 3.7 %copy-start.5 = (f32[64,512]{1,0:T(8,128)S(1)}, f32[64,512]{1,0:T(8,128)}, u32[]{:S(2)}) copy-start(f32[64,512]{1,0:T(8,128)} %param.15) | copy-start | bytes 393220
  34.9 3.8 %copy-start.9 = (s32[1,2]{1,0:T(1,128)S(1)}, s32[1,2]{1,0:T(1,128)}, u32[]{:S(2)}) copy-start(s32[1,2]{1,0:T(1,128)} %param.14) | copy-start | bytes 28
  42.3 10.1 %copy-start.10 = (s32[4]{0:T(128)S(1)}, s32[4]{0:T(128)}, u32[]{:S(2)}) copy-start(s32[4]{0:T(128)} %param.18) | copy-start | bytes 52
  42.3 74.0 %all-to-all-start.1 = ((f32[32,35,512]{2,1,0:T(8,128)}), f32[32,35,512]{2,1,0:T(8,128)}, u32[]{:S(2)}, u32[]{:S(2)}) async-start(f32[32,35,512]{2,1,0:T(8,128)} %pad_maximum_fusion), calls=%async_computation.1 | async-start | bytes 5242880 | tf_op jit(solution)/shard_map/all_to_all | solution.py:60
  52.3 102.9 %all-gather.3.cloned.1.call-start = ((), (), s32[]{:S(2)}) async-start(), calls=%async_computation.6 | async-start | bytes 2162688 | tf_op jit(solution)/shard_map/all_gather | solution.py:45
  122.7 35.5 %all-to-all-start.2 = ((bf16[32,16,512]{2,1,0:T(8,128)(2,1)}), bf16[32,16,512]{2,1,0:T(8,128)(2,1)S(1)}, u32[]{:S(2)}, u32[]{:S(2)}) async-start(bf16[32,16,512]{2,1,0:T(8,128)(2,1)} %broadcast_in_dim.99), calls=%async_computation.2 | async-start | bytes 1048576 | tf_op jit(solution)/shard_map/all_to_all | solution.py:13
  158.2 0.8 copy-start.4
  158.2 2.4 %copy-start.6 = (bf16[1,16,1024]{2,1,0:T(8,128)(2,1)S(1)}, bf16[1,16,1024]{2,1,0:T(8,128)(2,1)}, u32[]{:S(2)}) copy-start(bf16[1,16,1024]{2,1,0:T(8,128)(2,1)} %copy.141) | copy-start | bytes 98308
  159.0 10.0 %copy-start.7 = (s32[4,2]{0,1:T(2,128)S(1)}, s32[4,2]{0,1:T(2,128)}, u32[]{:S(2)}) copy-start(s32[4,2]{0,1:T(2,128)} %param.19) | copy-start | bytes 100
  161.7 22.2 %all-to-all-start.3 = ((bf16[32,16,512]{2,1,0:T(8,128)(2,1)}), bf16[32,16,512]{2,1,0:T(8,128)(2,1)}, u32[]{:S(2)}, u32[]{:S(2)}) async-start(bf16[32,16,512]{2,1,0:T(8,128)(2,1)} %broadcast_in_dim.100), calls=%async_computation.3 | async-start | bytes 1048576 | tf_op jit(solution)/shard_map/all_to_all | solution.py:13
  185.5 1.0 copy-start.1
  187.6 18.6 %all-to-all-start.4 = ((bf16[32,16,512]{2,1,0:T(8,128)(2,1)}), bf16[32,16,512]{2,1,0:T(8,128)(2,1)}, u32[]{:S(2)}, u32[]{:S(2)}) async-start(bf16[32,16,512]{2,1,0:T(8,128)(2,1)} %broadcast_in_dim.104), calls=%async_computation.4 | async-start | bytes 1048576 | tf_op jit(solution)/shard_map/all_to_all | solution.py:13
  207.8 1.0 copy-start.2
  209.9 18.6 %all-to-all-start.5 = ((bf16[32,16,512]{2,1,0:T(8,128)(2,1)}), bf16[32,16,512]{2,1,0:T(8,128)(2,1)}, u32[]{:S(2)}, u32[]{:S(2)}) async-start(bf16[32,16,512]{2,1,0:T(8,128)(2,1)} %broadcast_in_dim.105), calls=%async_computation.5 | async-start | bytes 1048576 | tf_op jit(solution)/shard_map/all_to_all | solution.py:13
  218.5 4.8 %copy-start.3 = (f32[512,512]{1,0:T(8,128)S(1)}, f32[512,512]{1,0:T(8,128)}, u32[]{:S(2)}) copy-start(f32[512,512]{1,0:T(8,128)} %copy-done.2) | copy-start | bytes 3145732
Sparse Core Ops, SparseCore 0:
  68.7 86.5 all-gather.2

commit v8 on v7

--- a/solution.py
+++ b/solution.py
@@ -48,10 +48,10 @@
         sub_inverse, sub_source.astype(jnp.bfloat16), preferred_element_type=jnp.float32
     )
     rounded = sub_field.astype(jnp.bfloat16)
-    updates = jnp.einsum(
-        "lmf,ft->lmt", coupling[0], rounded, preferred_element_type=jnp.float32
-    )
-    per_dest = updates.reshape(LINKS, n_src, n_row, PAIR, cols).transpose(2, 0, 1, 3, 4)
+    sub_rows = coupling.shape[-1]
+    grouped = coupling[0].reshape(LINKS, n_src, n_row, PAIR, sub_rows).transpose(2, 0, 1, 3, 4)
+    grouped = grouped.reshape(n_row * LINKS * span, sub_rows)
+    per_dest = jnp.dot(grouped, rounded, preferred_element_type=jnp.float32)
     per_dest = per_dest.reshape(n_row, LINKS * span, cols)
     src_rows = sep_source.reshape(n_row, PAIR, cols)
     lists = jnp.zeros((cols,), jnp.float32).at[:LINKS].set(update_lists[0].astype(jnp.float32))

time: 240 us -> 246 us (1.025)
  local copies, waits for them, and re-layouts: 43.2 us -> 48.2 us
    another operation x0 -> x2, local copies, waits for them, and re-layouts: none -> 9.35 us  [per_device(): coupling[0].reshape(LINKS, n_src, n_row, PAIR, sub_rows)]
    transpose x1 -> x0, local copies, waits for them, and re-layouts: 4.12 us -> none  [per_device(): updates.reshape(LINKS, n_src, n_row, PAIR, cols).transpose(2, 0, 1, 3, 4)]
    reshape x2 -> x1, local copies, waits for them, and re-layouts: 7.22 us -> 4.12 us  [per_device(): grouped = grouped.reshape(n_row * LINKS * span, sub_rows)]
    dot_general x0 -> x1, local copies, waits for them, and re-layouts: none -> 2.93 us  [per_device(): per_dest = jnp.dot(grouped, rounded, preferred_element_type=jnp.float32)]
  transfers between devices with their start and end apart: 7 -> 7, of which waited for: 5 -> 5; matrix products, arithmetic and copies ran while one was open for 20% -> 22% of each run, Pallas kernels for 0% -> 0%
where the time goes in v8:
time: 246 us; the launch traced here: 243 us
  waiting for transfers between devices  101 us (41%)
  local copies, waits for them, and re-layouts  48.2 us (20%)
  starting transfers between devices  43.2 us (18%)
  between operations  16.4 us (7%)
  matrix products  14.4 us (6%)
  blocking collectives  11.6 us (5%)
  other arithmetic  8.27 us (3%)
    all_to_all x1, waiting for transfers between devices, per_device(): got = lax.all_to_all(payload, 'row', 0, 0, tiled=False)  47.7 us
    all_to_all x4, waiting for transfers between devices, gather_row(): return lax.all_to_all(spread, 'row', 0, 0, tiled=False)  27 us
    all_gather x1, waiting for transfers between devices, per_device(): inverse_all = lax.all_gather(inverse_rows, 'row', axis=0, tiled=False)  26.5 us
    all_to_all x4, starting transfers between devices, gather_row(): return lax.all_to_all(spread, 'row', 0, 0, tiled=False)  21.8 us
    all_gather x1, blocking collectives, per_device(): owned = lax.all_gather(owned, 'src', axis=0, tiled=False)  11.6 us
    all_to_all x1, starting transfers between devices, per_device(): lax.all_to_all(factors.reshape(n_row, PAIR, width), 'row', 0, 0, tiled=Fa...  11.3 us
    all_to_all x1, starting transfers between devices, per_device(): got = lax.all_to_all(payload, 'row', 0, 0, tiled=False)  10 us
    another operation x2, local copies, waits for them, and re-layouts, per_device(): coupling[0].reshape(LINKS, n_src, n_row, PAIR, sub_rows)  9.35 us
  transfers between devices with their start and end apart: 7, of which 5 were waited for; matrix products, arithmetic and copies ran while one was open for 22% of the time, Pallas kernels for 0%

profile of v8, /device:TPU:16, one launch (start us, length us, event | category | flops | bytes accessed | tf_op | source)
XLA Modules:
  0.0 243.3 jit_solution(1076490732720003726)
XLA Ops:
  9.0 11.3 %all-to-all-start = ((bf16[32,2,1536]{2,1,0:T(2,128)(2,1)}), bf16[32,2,1536]{2,1,0:T(2,128)(2,1)S(1)}, u32[]{:S(2)}, u32[]{:S(2)}) async-start(bf16[32,2,1536]{2,1,0:T(2,128)(2,1)} %reshape.156), calls=%async_computation | async-start | bytes 393216 | tf_op jit(solution)/shard_map/all_to_all | solution.py:37
  20.4 4.1 %reshape_squeeze.13 = bf16[2,8,32,2,1024]{4,3,2,1,0:T(2,128)(2,1)} reshape(bf16[1,2,512,1024]{3,2,1,0:T(8,128)(2,1)} %param.13) | data formatting | bytes 4194304 | tf_op jit(solution)/shard_map/reshape;squeeze | solution.py:52
  24.5 5.2 %copy.199 = bf16[2,8,32,2,1024]{4,3,1,0,2:T(2,128)(2,1)} copy(bf16[2,8,32,2,1024]{4,3,2,1,0:T(2,128)(2,1)} %reshape_squeeze.13) | data formatting | bytes 4194304 | tf_op jit(solution)/shard_map/reshape;squeeze | solution.py:52
  29.7 4.1 %reshape.159 = bf16[1024,1024]{1,0:T(8,128)(2,1)} reshape(bf16[32,2,8,2,1024]{4,3,2,1,0:T(2,128)(2,1)} %bitcast.68) | data formatting | bytes 4194304 | tf_op jit(solution)/shard_map/reshape | solution.py:53
  33.8 3.0 %fusion.4 = f32[1024,512]{1,0:T(8,128)S(1)} fusion(bf16[1024,1024]{1,0:T(8,128)(2,1)S(1)} %copy-done, f32[1024,512]{1,0:T(8,128)} %param.11), kind=kOutput, calls=%fused_computation.17 | convolution fusion | flops 1074266112 | bytes 6291456 | tf_op jit(solution)/shard_map/dot_general | solution.py:47
  38.1 2.7 %convolution_bitcast_fusion = f32[1024,512]{0,1:T(8,128)} fusion(bf16[1024,1024]{1,0:T(8,128)(2,1)S(1)} %copy-done.4, f32[1024,512]{1,0:T(8,128)S(1)} %fusion.4), kind=kOutput, calls=%fused_computation.7 | convolution fusion | flops 1074266112 | bytes 6291456 | tf_op jit(solution)/shard_map/dot_general | solution.py:54
  40.8 2.9 %copy.171 = f32[1024,512]{1,0:T(8,128)} copy(f32[1024,512]{0,1:T(8,128)} %convolution_bitcast_fusion) | data formatting | bytes 4194304 | tf_op jit(solution)/shard_map/dot_general | solution.py:54
  43.9 3.5 %pad_maximum_fusion = f32[32,35,512]{2,1,0:T(8,128)} fusion(f32[32,1,512]{2,1,0:T(1,128)S(1)} %broadcast_in_dim.88, f32[32,2,512]{2,1,0:T(2,128)S(1)} %reshape.161, f32[32,32,512]{2,1,0:T(8,128)} %bitcast.67), kind=kLoop, calls=%fused_computation.1 | loop fusion | flops 1146880 | bytes 4587520 | tf_op jit(solution)/shard_map/concatenate | solution.py:59
  47.4 10.0 %all-to-all-start.1 = ((f32[32,35,512]{2,1,0:T(8,128)}), f32[32,35,512]{2,1,0:T(8,128)}, u32[]{:S(2)}, u32[]{:S(2)}) async-start(f32[32,35,512]{2,1,0:T(8,128)} %pad_maximum_fusion), calls=%async_computation.1 | async-start | bytes 5242880 | tf_op jit(solution)/shard_map/all_to_all | solution.py:60
  61.5 11.6 %all_gather.9 = bf16[8,4,2,1536]{3,1,2,0:T(4,128)(2,1)S(1)} all-gather(bf16[1,4,2,1536]{3,1,2,0:T(4,128)(2,1)S(1)} %copy.167), channel_id=1, replica_groups=mesh['row'=32,'src'=8] {'src'}, dimensions={0}, use_global_device_ids=true | all-gather | bytes 221184 | tf_op jit(solution)/shard_map/all_gather | solution.py:41
  73.7 47.7 %all-to-all-done.1 = f32[32,35,512]{2,1,0:T(8,128)} async-done(((f32[32,35,512]{2,1,0:T(8,128)}), f32[32,35,512]{2,1,0:T(8,128)}, u32[]{:S(2)}, u32[]{:S(2)}) %all-to-all-start.1) | async-done | bytes 2293792 | tf_op jit(solution)/shard_map/all_to_all | solution.py:60
  122.9 2.9 %select_reduce_fusion.3 = (f32[32,512]{1,0:T(8,128)S(1)}, f32[32,512]{1,0:T(8,128)S(1)}, f32[32,512]{1,0:T(8,128)S(1)}, f32[32,512]{1,0:T(8,128)S(1)}) fusion(f32[32,35,512]{2,1,0:T(8,128)} %all-to-all-done.1, pred[32,32]{1,0:T(8,128)(4,1)S(1)} %copy.173, pred[32,32]{1,0:T(8,128)(4,1)S(1)} %copy.174, pred[32,32]{1,0:T(8,128)(4,1)S(1)} %copy.175, ...), kind=kLoop, calls=%fused_computation.6 | loop fusion | flops 4128768 | bytes 2363392 | tf_op jit(solution)/shard_map/reduce_sum | solution.py:67
  127.8 5.2 %all-to-all-start.2 = ((bf16[32,16,512]{2,1,0:T(8,128)(2,1)}), bf16[32,16,512]{2,1,0:T(8,128)(2,1)S(1)}, u32[]{:S(2)}, u32[]{:S(2)}) async-start(bf16[32,16,512]{2,1,0:T(8,128)(2,1)} %broadcast_in_dim.99), calls=%async_computation.2 | async-start | bytes 1048576 | tf_op jit(solution)/shard_map/all_to_all | solution.py:13
  133.9 26.5 %all-gather.3.cloned.1.call-done = bf16[128,16,512]{2,1,0:T(8,128)(2,1)} async-done(((bf16[4,16,512]{2,1,0:T(8,128)(2,1)}), bf16[128,16,512]{2,1,0:T(8,128)(2,1)}) %all-gather.3.cloned.1.call-update) | async-done | bytes 2097168 | tf_op jit(solution)/shard_map/all_gather | solution.py:45
  160.5 2.9 %fusion.31 = (bf16[32,1,16,512]{3,2,1,0:T(8,128)(2,1)}, bf16[32,1,16,512]{3,2,1,0:T(8,128)(2,1)}, bf16[32,1,16,512]{3,2,1,0:T(8,128)(2,1)}, bf16[32,1,16,512]{3,2,1,0:T(8,128)(2,1)}) fusion(bf16[32,4,16,512]{3,2,1,0:T(8,128)(2,1)} %bitcast.71), kind=kLoop, calls=%fused_computation.63 | loop fusion | bytes 4194304 | tf_op jit(solution)/shard_map/slice | solution.py:86
  166.8 7.2 %all-to-all-start.3 = ((bf16[32,16,512]{2,1,0:T(8,128)(2,1)}), bf16[32,16,512]{2,1,0:T(8,128)(2,1)}, u32[]{:S(2)}, u32[]{:S(2)}) async-start(bf16[32,16,512]{2,1,0:T(8,128)(2,1)} %broadcast_in_dim.100), calls=%async_computation.3 | async-start | bytes 1048576 | tf_op jit(solution)/shard_map/all_to_all | solution.py:13
  175.6 13.3 %all-to-all-done.3 = bf16[32,16,512]{2,1,0:T(8,128)(2,1)} async-done(((bf16[32,16,512]{2,1,0:T(8,128)(2,1)}), bf16[32,16,512]{2,1,0:T(8,128)(2,1)}, u32[]{:S(2)}, u32[]{:S(2)}) %all-to-all-start.3) | async-done | bytes 524320 | tf_op jit(solution)/shard_map/all_to_all | solution.py:13
  192.6 4.8 %all-to-all-start.4 = ((bf16[32,16,512]{2,1,0:T(8,128)(2,1)}), bf16[32,16,512]{2,1,0:T(8,128)(2,1)}, u32[]{:S(2)}, u32[]{:S(2)}) async-start(bf16[32,16,512]{2,1,0:T(8,128)(2,1)} %broadcast_in_dim.104), calls=%async_computation.4 | async-start | bytes 1048576 | tf_op jit(solution)/shard_map/all_to_all | solution.py:13
  200.2 11.0 %all-to-all-done.4 = bf16[32,16,512]{2,1,0:T(8,128)(2,1)} async-done(((bf16[32,16,512]{2,1,0:T(8,128)(2,1)}), bf16[32,16,512]{2,1,0:T(8,128)(2,1)}, u32[]{:S(2)}, u32[]{:S(2)}) %all-to-all-start.4) | async-done | bytes 524320 | tf_op jit(solution)/shard_map/all_to_all | solution.py:13
  214.9 4.6 %all-to-all-start.5 = ((bf16[32,16,512]{2,1,0:T(8,128)(2,1)}), bf16[32,16,512]{2,1,0:T(8,128)(2,1)}, u32[]{:S(2)}, u32[]{:S(2)}) async-start(bf16[32,16,512]{2,1,0:T(8,128)(2,1)} %broadcast_in_dim.105), calls=%async_computation.5 | async-start | bytes 1048576 | tf_op jit(solution)/shard_map/all_to_all | solution.py:13
  219.6 2.1 copy.169
  224.3 2.8 %reshape.167 = f32[32,8,2,512]{3,2,1,0:T(2,128)} reshape(f32[512,512]{1,0:T(8,128)} %copy-done.1) | data formatting | bytes 2097152 | tf_op jit(solution)/shard_map/reshape | solution.py:96
  230.6 2.7 %all-to-all-done.5 = bf16[32,16,512]{2,1,0:T(8,128)(2,1)} async-done(((bf16[32,16,512]{2,1,0:T(8,128)(2,1)}), bf16[32,16,512]{2,1,0:T(8,128)(2,1)}, u32[]{:S(2)}, u32[]{:S(2)}) %all-to-all-start.5) | async-done | bytes 524320 | tf_op jit(solution)/shard_map/all_to_all | solution.py:13
  233.3 1.7 fusion.6
  (87 shorter events, 33.0 us)
Async XLA Ops:
  7.2 26.7 %copy-start = (bf16[1024,1024]{1,0:T(8,128)(2,1)S(1)}, bf16[1024,1024]{1,0:T(8,128)(2,1)}, u32[]{:S(2)}) copy-start(bf16[1024,1024]{1,0:T(8,128)(2,1)} %param.12) | copy-start | bytes 6291460
  9.0 38.4 %all-to-all-start = ((bf16[32,2,1536]{2,1,0:T(2,128)(2,1)}), bf16[32,2,1536]{2,1,0:T(2,128)(2,1)S(1)}, u32[]{:S(2)}, u32[]{:S(2)}) async-start(bf16[32,2,1536]{2,1,0:T(2,128)(2,1)} %reshape.156), calls=%async_computation | async-start | bytes 393216 | tf_op jit(solution)/shard_map/all_to_all | solution.py:37
  33.8 4.3 %copy-start.4 = (bf16[1024,1024]{1,0:T(8,128)(2,1)S(1)}, bf16[1024,1024]{1,0:T(8,128)(2,1)}, u32[]{:S(2)}) copy-start(bf16[1024,1024]{1,0:T(8,128)(2,1)} %reshape.159) | copy-start | bytes 6291460
  36.8 1.3 copy-start.11
  40.8 2.9 %copy-start.6 = (f32[64,512]{1,0:T(8,128)S(1)}, f32[64,512]{1,0:T(8,128)}, u32[]{:S(2)}) copy-start(f32[64,512]{1,0:T(8,128)} %param.15) | copy-start | bytes 393220
  40.8 3.0 %copy-start.9 = (s32[1,2]{1,0:T(1,128)S(1)}, s32[1,2]{1,0:T(1,128)}, u32[]{:S(2)}) copy-start(s32[1,2]{1,0:T(1,128)} %param.14) | copy-start | bytes 28
  47.4 10.1 %copy-start.10 = (s32[4]{0:T(128)S(1)}, s32[4]{0:T(128)}, u32[]{:S(2)}) copy-start(s32[4]{0:T(128)} %param.18) | copy-start | bytes 52
  47.4 74.0 %all-to-all-start.1 = ((f32[32,35,512]{2,1,0:T(8,128)}), f32[32,35,512]{2,1,0:T(8,128)}, u32[]{:S(2)}, u32[]{:S(2)}) async-start(f32[32,35,512]{2,1,0:T(8,128)} %pad_maximum_fusion), calls=%async_computation.1 | async-start | bytes 5242880 | tf_op jit(solution)/shard_map/all_to_all | solution.py:60
  57.5 103.0 %all-gather.3.cloned.1.call-start = ((), (), s32[]{:S(2)}) async-start(), calls=%async_computation.6 | async-start | bytes 2162688 | tf_op jit(solution)/shard_map/all_gather | solution.py:45
  127.8 35.5 %all-to-all-start.2 = ((bf16[32,16,512]{2,1,0:T(8,128)(2,1)}), bf16[32,16,512]{2,1,0:T(8,128)(2,1)S(1)}, u32[]{:S(2)}, u32[]{:S(2)}) async-start(bf16[32,16,512]{2,1,0:T(8,128)(2,1)} %broadcast_in_dim.99), calls=%async_computation.2 | async-start | bytes 1048576 | tf_op jit(solution)/shard_map/all_to_all | solution.py:13
  163.3 0.8 copy-start.5
  163.3 2.4 %copy-start.7 = (bf16[1,16,1024]{2,1,0:T(8,128)(2,1)S(1)}, bf16[1,16,1024]{2,1,0:T(8,128)(2,1)}, u32[]{:S(2)}) copy-start(bf16[1,16,1024]{2,1,0:T(8,128)(2,1)} %copy.201) | copy-start | bytes 98308
  164.1 9.9 %copy-start.8 = (s32[4,2]{0,1:T(2,128)S(1)}, s32[4,2]{0,1:T(2,128)}, u32[]{:S(2)}) copy-start(s32[4,2]{0,1:T(2,128)} %param.19) | copy-start | bytes 100
  166.8 22.1 %all-to-all-start.3 = ((bf16[32,16,512]{2,1,0:T(8,128)(2,1)}), bf16[32,16,512]{2,1,0:T(8,128)(2,1)}, u32[]{:S(2)}, u32[]{:S(2)}) async-start(bf16[32,16,512]{2,1,0:T(8,128)(2,1)} %broadcast_in_dim.100), calls=%async_computation.3 | async-start | bytes 1048576 | tf_op jit(solution)/shard_map/all_to_all | solution.py:13
  190.6 1.0 copy-start.1
  192.6 18.6 %all-to-all-start.4 = ((bf16[32,16,512]{2,1,0:T(8,128)(2,1)}), bf16[32,16,512]{2,1,0:T(8,128)(2,1)}, u32[]{:S(2)}, u32[]{:S(2)}) async-start(bf16[32,16,512]{2,1,0:T(8,128)(2,1)} %broadcast_in_dim.104), calls=%async_computation.4 | async-start | bytes 1048576 | tf_op jit(solution)/shard_map/all_to_all | solution.py:13
  212.8 1.0 copy-start.2
  214.9 18.4 %all-to-all-start.5 = ((bf16[32,16,512]{2,1,0:T(8,128)(2,1)}), bf16[32,16,512]{2,1,0:T(8,128)(2,1)}, u32[]{:S(2)}, u32[]{:S(2)}) async-start(bf16[32,16,512]{2,1,0:T(8,128)(2,1)} %broadcast_in_dim.105), calls=%async_computation.5 | async-start | bytes 1048576 | tf_op jit(solution)/shard_map/all_to_all | solution.py:13
  223.3 4.8 %copy-start.3 = (f32[512,512]{1,0:T(8,128)S(1)}, f32[512,512]{1,0:T(8,128)}, u32[]{:S(2)}) copy-start(f32[512,512]{1,0:T(8,128)} %copy-done.2) | copy-start | bytes 3145732
Sparse Core Ops, SparseCore 0:
  73.8 86.5 all-gather.2

commit v9 on v7

--- a/solution.py
+++ b/solution.py
@@ -51,16 +51,15 @@
     updates = jnp.einsum(
         "lmf,ft->lmt", coupling[0], rounded, preferred_element_type=jnp.float32
     )
-    per_dest = updates.reshape(LINKS, n_src, n_row, PAIR, cols).transpose(2, 0, 1, 3, 4)
-    per_dest = per_dest.reshape(n_row, LINKS * span, cols)
+    spread = updates.reshape(LINKS, n_src, n_row, PAIR, cols)
+    got_updates = lax.all_to_all(spread, "row", 2, 2, tiled=True)
+    got_updates = got_updates.transpose(2, 0, 1, 3, 4).reshape(n_row, LINKS, span, cols)
     src_rows = sep_source.reshape(n_row, PAIR, cols)
     lists = jnp.zeros((cols,), jnp.float32).at[:LINKS].set(update_lists[0].astype(jnp.float32))
     lists = jnp.broadcast_to(lists[None, None], (n_row, 1, cols))
-    payload = jnp.concatenate([per_dest, src_rows, lists], axis=1)
-    got = lax.all_to_all(payload, "row", 0, 0, tiled=False)
-    got_updates = got[:, : LINKS * span].reshape(n_row, LINKS, span, cols)
-    got_src = got[:, LINKS * span : LINKS * span + PAIR].reshape(STEPS, span, cols)
-    got_lists = got[:, LINKS * span + PAIR, :LINKS]
+    got = lax.all_to_all(jnp.concatenate([src_rows, lists], axis=1), "row", 0, 0, tiled=False)
+    got_src = got[:, :PAIR].reshape(STEPS, span, cols)
+    got_lists = got[:, PAIR, :LINKS]
     pending = []
     for k in range(STEPS):
         hit = (got_lists == k)[:, :, None, None]

time: 240 us -> 242 us (level)
  local copies, waits for them, and re-layouts: 43.2 us -> 36.4 us
  starting transfers between devices: 43.3 us -> 47.2 us
  matrix products: 14.3 us -> 17.7 us
    all_to_all x1 -> x2, starting transfers between devices: 10 us -> 21.4 us  [the longest x1 11.3 us: per_device(): lax.all_to_all(jnp.concatenate([src_rows, lists], axis=1), 'row', 0, 0, t...]
    all_gather x1, waiting for transfers between devices: 26.5 us -> 35.5 us  [per_device(): inverse_all = lax.all_gather(inverse_rows, 'row', axis=0, tiled=False)]
    all_to_all x1 -> x2, waiting for transfers between devices: 47.7 us -> 39.7 us  [the longest x1 32.7 us: per_device(): got_updates = lax.all_to_all(spread, 'row', 2, 2, tiled=True)]
    all_to_all x1, starting transfers between devices: 11.3 us -> 3.97 us  [per_device(): lax.all_to_all(factors.reshape(n_row, PAIR, width), 'row', 0, 0, tiled=Fa...]
    transpose x1 -> x0, local copies, waits for them, and re-layouts: 4.12 us -> none  [per_device(): updates.reshape(LINKS, n_src, n_row, PAIR, cols).transpose(2, 0, 1, 3, 4)]
    reduce_sum x5 -> x1, other arithmetic: 2.92 us -> 6.32 us  [per_device(): jnp.sum(jnp.where(hit, got_updates, 0.0), axis=(0, 1))]
    concatenate x1, other arithmetic: 3.52 us -> 0.82 us  [per_device(): jnp.concatenate([src_rows, lists], axis=1)]
    unnamed x28 -> x18, local copies, waits for them, and re-layouts: 4.88 us -> 2.89 us
  transfers between devices with their start and end apart: 7 -> 8, of which waited for: 5 -> 6; matrix products, arithmetic and copies ran while one was open for 20% -> 20% of each run, Pallas kernels for 0% -> 0%
where the time goes in v9:
time: 242 us; the launch traced here: 241 us
  waiting for transfers between devices  102 us (42%)
  starting transfers between devices  47.2 us (20%)
  local copies, waits for them, and re-layouts  36.4 us (15%)
  matrix products  17.7 us (7%)
  between operations  16.2 us (7%)
  blocking collectives  11.6 us (5%)
  other arithmetic  9.56 us (4%)
    all_gather x1, waiting for transfers between devices, per_device(): inverse_all = lax.all_gather(inverse_rows, 'row', axis=0, tiled=False)  35.5 us
    all_to_all x1, waiting for transfers between devices, per_device(): got_updates = lax.all_to_all(spread, 'row', 2, 2, tiled=True)  32.7 us
    all_to_all x4, waiting for transfers between devices, gather_row(): return lax.all_to_all(spread, 'row', 0, 0, tiled=False)  26.8 us
    all_to_all x4, starting transfers between devices, gather_row(): return lax.all_to_all(spread, 'row', 0, 0, tiled=False)  21.8 us
    all_gather x1, blocking collectives, per_device(): owned = lax.all_gather(owned, 'src', axis=0, tiled=False)  11.6 us
    all_to_all x1, starting transfers between devices, per_device(): lax.all_to_all(jnp.concatenate([src_rows, lists], axis=1), 'row', 0, 0, t...  11.3 us
    all_to_all x1, starting transfers between devices, per_device(): got_updates = lax.all_to_all(spread, 'row', 2, 2, tiled=True)  10 us
    reshape x2, local copies, waits for them, and re-layouts, per_device(): spread = updates.reshape(LINKS, n_src, n_row, PAIR, cols)  7.59 us
  transfers between devices with their start and end apart: 8, of which 6 were waited for; matrix products, arithmetic and copies ran while one was open for 20% of the time, Pallas kernels for 0%

profile of v9, /device:TPU:16, one launch (start us, length us, event | category | flops | bytes accessed | tf_op | source)
XLA Modules:
  0.0 240.6 jit_solution(11038513298567954079)
XLA Ops:
  9.8 11.3 %all-to-all-start.1 = ((f32[32,3,512]{2,1,0:T(4,128)}), f32[32,3,512]{2,1,0:T(4,128)S(1)}, u32[]{:S(2)}, u32[]{:S(2)}) async-start(f32[32,3,512]{2,1,0:T(4,128)} %pad_maximum_fusion), calls=%async_computation.1 | async-start | bytes 524288 | tf_op jit(solution)/shard_map/all_to_all | solution.py:60
  22.9 4.2 %fusion.14 = f32[1024,512]{1,0:T(8,128)} fusion(bf16[1024,1024]{1,0:T(8,128)(2,1)S(1)} %copy-done, f32[1024,512]{1,0:T(8,128)} %param.11), kind=kOutput, calls=%fused_computation.22 | convolution fusion | flops 1074266112 | bytes 6291456 | tf_op jit(solution)/shard_map/dot_general | solution.py:47
  27.0 6.9 %all-to-all-done.1 = f32[32,3,512]{2,1,0:T(4,128)S(1)} async-done(((f32[32,3,512]{2,1,0:T(4,128)}), f32[32,3,512]{2,1,0:T(4,128)S(1)}, u32[]{:S(2)}, u32[]{:S(2)}) %all-to-all-start.1) | async-done | bytes 196640 | tf_op jit(solution)/shard_map/all_to_all | solution.py:60
  34.0 4.0 %all-to-all-start = ((bf16[32,2,1536]{2,1,0:T(2,128)(2,1)}), bf16[32,2,1536]{2,1,0:T(2,128)(2,1)S(1)}, u32[]{:S(2)}, u32[]{:S(2)}) async-start(bf16[32,2,1536]{2,1,0:T(2,128)(2,1)} %reshape.161), calls=%async_computation | async-start | bytes 393216 | tf_op jit(solution)/shard_map/all_to_all | solution.py:37
  38.0 4.8 %fusion.6 = f32[2,512,512]{2,1,0:T(8,128)} fusion(bf16[1,2,512,1024]{3,2,1,0:T(8,128)(2,1)} %param.13, f32[1024,512]{1,0:T(8,128)} %fusion.14), kind=kOutput, calls=%fused_computation.11 | convolution fusion | flops 1074266112 | bytes 6291456 | tf_op jit(solution)/shard_map/lmf,ft->lmt/dot_general | solution.py:51
  42.7 3.5 %reshape.165 = f32[2,8,32,2,512]{4,3,2,1,0:T(2,128)} reshape(f32[2,512,512]{2,1,0:T(8,128)} %fusion.6) | data formatting | bytes 4194304 | tf_op jit(solution)/shard_map/reshape | solution.py:54
  46.2 4.1 %copy.124 = f32[2,8,32,2,512]{4,3,1,0,2:T(2,128)} copy(f32[2,8,32,2,512]{4,3,2,1,0:T(2,128)} %reshape.165) | data formatting | bytes 4194304 | tf_op jit(solution)/shard_map/reshape | solution.py:54
  50.3 10.0 %all-to-all-start.2 = ((f32[2,8,32,2,512]{4,3,1,0,2:T(2,128)}), f32[2,8,32,2,512]{4,3,1,0,2:T(2,128)}, u32[]{:S(2)}, u32[]{:S(2)}) async-start(f32[2,8,32,2,512]{4,3,1,0,2:T(2,128)} %copy.124), calls=%async_computation.2 | async-start | bytes 4194304 | tf_op jit(solution)/shard_map/all_to_all | solution.py:55
  64.4 11.6 %all_gather.9 = bf16[8,4,2,1536]{3,1,2,0:T(4,128)(2,1)S(1)} all-gather(bf16[1,4,2,1536]{3,1,2,0:T(4,128)(2,1)S(1)} %copy.119), channel_id=1, replica_groups=mesh['row'=32,'src'=8] {'src'}, dimensions={0}, use_global_device_ids=true | all-gather | bytes 221184 | tf_op jit(solution)/shard_map/all_gather | solution.py:41
  77.2 32.7 %all-to-all-done.2 = f32[2,8,32,2,512]{4,3,1,0,2:T(2,128)} async-done(((f32[2,8,32,2,512]{4,3,1,0,2:T(2,128)}), f32[2,8,32,2,512]{4,3,1,0,2:T(2,128)}, u32[]{:S(2)}, u32[]{:S(2)}) %all-to-all-start.2) | async-done | bytes 2097184 | tf_op jit(solution)/shard_map/all_to_all | solution.py:55
  109.9 6.3 %fusion = (f32[8,2,512]{2,1,0:T(2,128)S(1)}, f32[8,2,512]{2,1,0:T(2,128)S(1)}, f32[8,2,512]{2,1,0:T(2,128)S(1)}, f32[8,2,512]{2,1,0:T(2,128)S(1)}) fusion(f32[2,8,32,2,512]{4,3,1,0,2:T(2,128)} %all-to-all-done.2, pred[32,2]{1,0:T(8,128)(4,1)S(1)} %copy.123, pred[32,2]{1,0:T(8,128)(4,1)S(1)} %copy.126, pred[32,2]{1,0:T(8,128)(4,1)S(1)} %copy.128, ...), kind=kLoop, calls=%fused_computation.5 | loop fusion | flops 4161536 | bytes 2228480 | tf_op jit(solution)/shard_map/reduce_sum | solution.py:66
  117.2 6.2 %all-to-all-start.3 = ((bf16[32,16,512]{2,1,0:T(8,128)(2,1)}), bf16[32,16,512]{2,1,0:T(8,128)(2,1)S(1)}, u32[]{:S(2)}, u32[]{:S(2)}) async-start(bf16[32,16,512]{2,1,0:T(8,128)(2,1)} %broadcast_in_dim.77), calls=%async_computation.3 | async-start | bytes 1048576 | tf_op jit(solution)/shard_map/all_to_all | solution.py:13
  123.6 35.5 %all-gather.3.cloned.1.call-done = bf16[128,16,512]{2,1,0:T(8,128)(2,1)} async-done(((bf16[4,16,512]{2,1,0:T(8,128)(2,1)}), bf16[128,16,512]{2,1,0:T(8,128)(2,1)}) %all-gather.3.cloned.1.call-update) | async-done | bytes 2097168 | tf_op jit(solution)/shard_map/all_gather | solution.py:45
  159.1 2.9 %fusion.41 = (bf16[32,1,16,512]{3,2,1,0:T(8,128)(2,1)}, bf16[32,1,16,512]{3,2,1,0:T(8,128)(2,1)}, bf16[32,1,16,512]{3,2,1,0:T(8,128)(2,1)}, bf16[32,1,16,512]{3,2,1,0:T(8,128)(2,1)}) fusion(bf16[32,4,16,512]{3,2,1,0:T(8,128)(2,1)} %bitcast.75), kind=kLoop, calls=%fused_computation.72 | loop fusion | bytes 4194304 | tf_op jit(solution)/shard_map/slice | solution.py:85
  162.8 1.6 fusion.44
  165.5 6.4 %all-to-all-start.4 = ((bf16[32,16,512]{2,1,0:T(8,128)(2,1)}), bf16[32,16,512]{2,1,0:T(8,128)(2,1)}, u32[]{:S(2)}, u32[]{:S(2)}) async-start(bf16[32,16,512]{2,1,0:T(8,128)(2,1)} %broadcast_in_dim.78), calls=%async_computation.4 | async-start | bytes 1048576 | tf_op jit(solution)/shard_map/all_to_all | solution.py:13
  173.4 13.1 %all-to-all-done.4 = bf16[32,16,512]{2,1,0:T(8,128)(2,1)} async-done(((bf16[32,16,512]{2,1,0:T(8,128)(2,1)}), bf16[32,16,512]{2,1,0:T(8,128)(2,1)}, u32[]{:S(2)}, u32[]{:S(2)}) %all-to-all-start.4) | async-done | bytes 524320 | tf_op jit(solution)/shard_map/all_to_all | solution.py:13
  190.2 4.6 %all-to-all-start.5 = ((bf16[32,16,512]{2,1,0:T(8,128)(2,1)}), bf16[32,16,512]{2,1,0:T(8,128)(2,1)}, u32[]{:S(2)}, u32[]{:S(2)}) async-start(bf16[32,16,512]{2,1,0:T(8,128)(2,1)} %broadcast_in_dim.80), calls=%async_computation.5 | async-start | bytes 1048576 | tf_op jit(solution)/shard_map/all_to_all | solution.py:13
  197.6 10.9 %all-to-all-done.5 = bf16[32,16,512]{2,1,0:T(8,128)(2,1)} async-done(((bf16[32,16,512]{2,1,0:T(8,128)(2,1)}), bf16[32,16,512]{2,1,0:T(8,128)(2,1)}, u32[]{:S(2)}, u32[]{:S(2)}) %all-to-all-start.5) | async-done | bytes 524320 | tf_op jit(solution)/shard_map/all_to_all | solution.py:13
  212.2 4.6 %all-to-all-start.6 = ((bf16[32,16,512]{2,1,0:T(8,128)(2,1)}), bf16[32,16,512]{2,1,0:T(8,128)(2,1)}, u32[]{:S(2)}, u32[]{:S(2)}) async-start(bf16[32,16,512]{2,1,0:T(8,128)(2,1)} %broadcast_in_dim.81), calls=%async_computation.6 | async-start | bytes 1048576 | tf_op jit(solution)/shard_map/all_to_all | solution.py:13
  216.9 2.1 copy.121
  221.6 2.8 %reshape.171 = f32[32,8,2,512]{3,2,1,0:T(2,128)} reshape(f32[512,512]{1,0:T(8,128)} %copy-done.1) | data formatting | bytes 2097152 | tf_op jit(solution)/shard_map/reshape | solution.py:95
  227.9 2.8 %all-to-all-done.6 = bf16[32,16,512]{2,1,0:T(8,128)(2,1)} async-done(((bf16[32,16,512]{2,1,0:T(8,128)(2,1)}), bf16[32,16,512]{2,1,0:T(8,128)(2,1)}, u32[]{:S(2)}, u32[]{:S(2)}) %all-to-all-start.6) | async-done | bytes 524320 | tf_op jit(solution)/shard_map/all_to_all | solution.py:13
  230.7 1.7 fusion.16
  (68 shorter events, 29.7 us)
Async XLA Ops:
  7.2 15.7 %copy-start = (bf16[1024,1024]{1,0:T(8,128)(2,1)S(1)}, bf16[1024,1024]{1,0:T(8,128)(2,1)}, u32[]{:S(2)}) copy-start(bf16[1024,1024]{1,0:T(8,128)(2,1)} %param.12) | copy-start | bytes 6291460
  9.8 24.1 %all-to-all-start.1 = ((f32[32,3,512]{2,1,0:T(4,128)}), f32[32,3,512]{2,1,0:T(4,128)S(1)}, u32[]{:S(2)}, u32[]{:S(2)}) async-start(f32[32,3,512]{2,1,0:T(4,128)} %pad_maximum_fusion), calls=%async_computation.1 | async-start | bytes 524288 | tf_op jit(solution)/shard_map/all_to_all | solution.py:60
  34.0 16.4 %all-to-all-start = ((bf16[32,2,1536]{2,1,0:T(2,128)(2,1)}), bf16[32,2,1536]{2,1,0:T(2,128)(2,1)S(1)}, u32[]{:S(2)}, u32[]{:S(2)}) async-start(bf16[32,2,1536]{2,1,0:T(2,128)(2,1)} %reshape.161), calls=%async_computation | async-start | bytes 393216 | tf_op jit(solution)/shard_map/all_to_all | solution.py:37
  50.3 10.1 %copy-start.6 = (s32[4]{0:T(128)S(1)}, s32[4]{0:T(128)}, u32[]{:S(2)}) copy-start(s32[4]{0:T(128)} %param.18) | copy-start | bytes 52
  50.3 59.6 %all-to-all-start.2 = ((f32[2,8,32,2,512]{4,3,1,0,2:T(2,128)}), f32[2,8,32,2,512]{4,3,1,0,2:T(2,128)}, u32[]{:S(2)}, u32[]{:S(2)}) async-start(f32[2,8,32,2,512]{4,3,1,0,2:T(2,128)} %copy.124), calls=%async_computation.2 | async-start | bytes 4194304 | tf_op jit(solution)/shard_map/all_to_all | solution.py:55
  60.4 98.7 %all-gather.3.cloned.1.call-start = ((), (), s32[]{:S(2)}) async-start(), calls=%async_computation.7 | async-start | bytes 2162688 | tf_op jit(solution)/shard_map/all_gather | solution.py:45
  117.2 44.8 %all-to-all-start.3 = ((bf16[32,16,512]{2,1,0:T(8,128)(2,1)}), bf16[32,16,512]{2,1,0:T(8,128)(2,1)S(1)}, u32[]{:S(2)}, u32[]{:S(2)}) async-start(bf16[32,16,512]{2,1,0:T(8,128)(2,1)} %broadcast_in_dim.77), calls=%async_computation.3 | async-start | bytes 1048576 | tf_op jit(solution)/shard_map/all_to_all | solution.py:13
  162.0 0.8 copy-start.4
  162.8 9.1 %copy-start.5 = (s32[4,2]{0,1:T(2,128)S(1)}, s32[4,2]{0,1:T(2,128)}, u32[]{:S(2)}) copy-start(s32[4,2]{0,1:T(2,128)} %param.19) | copy-start | bytes 100
  165.5 21.0 %all-to-all-start.4 = ((bf16[32,16,512]{2,1,0:T(8,128)(2,1)}), bf16[32,16,512]{2,1,0:T(8,128)(2,1)}, u32[]{:S(2)}, u32[]{:S(2)}) async-start(bf16[32,16,512]{2,1,0:T(8,128)(2,1)} %broadcast_in_dim.78), calls=%async_computation.4 | async-start | bytes 1048576 | tf_op jit(solution)/shard_map/all_to_all | solution.py:13
  188.1 1.0 copy-start.1
  190.2 18.3 %all-to-all-start.5 = ((bf16[32,16,512]{2,1,0:T(8,128)(2,1)}), bf16[32,16,512]{2,1,0:T(8,128)(2,1)}, u32[]{:S(2)}, u32[]{:S(2)}) async-start(bf16[32,16,512]{2,1,0:T(8,128)(2,1)} %broadcast_in_dim.80), calls=%async_computation.5 | async-start | bytes 1048576 | tf_op jit(solution)/shard_map/all_to_all | solution.py:13
  210.2 1.0 copy-start.2
  212.2 18.4 %all-to-all-start.6 = ((bf16[32,16,512]{2,1,0:T(8,128)(2,1)}), bf16[32,16,512]{2,1,0:T(8,128)(2,1)}, u32[]{:S(2)}, u32[]{:S(2)}) async-start(bf16[32,16,512]{2,1,0:T(8,128)(2,1)} %broadcast_in_dim.81), calls=%async_computation.6 | async-start | bytes 1048576 | tf_op jit(solution)/shard_map/all_to_all | solution.py:13
  220.6 4.7 %copy-start.3 = (f32[512,512]{1,0:T(8,128)S(1)}, f32[512,512]{1,0:T(8,128)}, u32[]{:S(2)}) copy-start(f32[512,512]{1,0:T(8,128)} %copy-done.2) | copy-start | bytes 3145732
Sparse Core Ops, SparseCore 0:
  76.8 82.2 all-gather.2

commit v10 on v9

--- a/solution.py
+++ b/solution.py
@@ -51,15 +51,29 @@
     updates = jnp.einsum(
         "lmf,ft->lmt", coupling[0], rounded, preferred_element_type=jnp.float32
     )
-    spread = updates.reshape(LINKS, n_src, n_row, PAIR, cols)
-    got_updates = lax.all_to_all(spread, "row", 2, 2, tiled=True)
-    got_updates = got_updates.transpose(2, 0, 1, 3, 4).reshape(n_row, LINKS, span, cols)
-    src_rows = sep_source.reshape(n_row, PAIR, cols)
+    blocks_per = block // local_rows
+    my_shard = my_row % blocks_per
+    extra = jnp.zeros((n_src, n_row, PAIR, cols), jnp.float32)
+    extra = lax.dynamic_update_slice(
+        extra, sep_source.reshape(1, n_row, PAIR, cols), (my_shard, 0, 0, 0)
+    )
     lists = jnp.zeros((cols,), jnp.float32).at[:LINKS].set(update_lists[0].astype(jnp.float32))
-    lists = jnp.broadcast_to(lists[None, None], (n_row, 1, cols))
-    got = lax.all_to_all(jnp.concatenate([src_rows, lists], axis=1), "row", 0, 0, tiled=False)
-    got_src = got[:, :PAIR].reshape(STEPS, span, cols)
-    got_lists = got[:, PAIR, :LINKS]
+    lists = jnp.broadcast_to(lists[None, None, None], (1, n_row, PAIR, cols))
+    extra = lax.dynamic_update_slice(extra, lists, ((my_shard + n_src // 2) % n_src, 0, 0, 0))
+    spread = jnp.concatenate(
+        [updates.reshape(LINKS, n_src, n_row, PAIR, cols), extra[None]], axis=0
+    )
+    got = lax.all_to_all(spread, "row", 2, 2, tiled=True)
+    got_updates = got[:LINKS].transpose(2, 0, 1, 3, 4).reshape(n_row, LINKS, span, cols)
+    got_src = jnp.stack(
+        [
+            jnp.stack([got[LINKS, q, k * blocks_per + q] for q in range(n_src)]).reshape(span, cols)
+            for k in range(STEPS)
+        ]
+    )
+    got_lists = jnp.stack(
+        [got[LINKS, (i % blocks_per + n_src // 2) % n_src, i, 0, :LINKS] for i in range(n_row)]
+    )
     pending = []
     for k in range(STEPS):
         hit = (got_lists == k)[:, :, None, None]
@@ -86,7 +100,6 @@
         result = jnp.dot(inverse, full_residue, preferred_element_type=jnp.float32)
         fields.append(result)
         rounded_fields.append(result.astype(jnp.bfloat16))
-    blocks_per = block // local_rows
     my_block = my_row // blocks_per
     my_part = my_row % blocks_per
     own_rows = jnp.zeros((local_rows, cols), jnp.float32)

time: 242 us -> 250 us (1.033)
  local copies, waits for them, and re-layouts: 36.4 us -> 45.6 us
  starting transfers between devices: 47.2 us -> 42.1 us
  other arithmetic: 9.56 us -> 14.2 us
  matrix products: 17.7 us -> 14.3 us
  waiting for transfers between devices: 102 us -> 105 us
    all_gather x1, waiting for transfers between devices: 35.5 us -> 0.02 us  [per_device(): inverse_all = lax.all_gather(inverse_rows, 'row', axis=0, tiled=False)]
    all_to_all x4, waiting for transfers between devices: 26.8 us -> 46.9 us  [gather_row(): return lax.all_to_all(spread, 'row', 0, 0, tiled=False)]
    all_to_all x2 -> x1, waiting for transfers between devices: 39.7 us -> 57.9 us  [per_device(): got = lax.all_to_all(spread, 'row', 2, 2, tiled=True)]
    all_to_all x2 -> x1, starting transfers between devices: 21.4 us -> 10 us  [per_device(): got = lax.all_to_all(spread, 'row', 2, 2, tiled=True)]
    all_to_all x1, starting transfers between devices: 3.97 us -> 11.3 us  [per_device(): lax.all_to_all(factors.reshape(n_row, PAIR, width), 'row', 0, 0, tiled=Fa...]
    unnamed x18 -> x29, local copies, waits for them, and re-layouts: 2.89 us -> 9.75 us
    another operation x0 -> x37, local copies, waits for them, and re-layouts: none -> 6.06 us  [the longest x35 4.58 us: per_device(): jnp.stack([got[LINKS, (i % blocks_per + n_src // 2) % n_src, i, 0, :LINKS...]
    reshape x3 -> x1, local copies, waits for them, and re-layouts: 8.72 us -> 3.49 us  [per_device(): updates.reshape(LINKS, n_src, n_row, PAIR, cols)]
  transfers between devices with their start and end apart: 8 -> 7, of which waited for: 6 -> 5; matrix products, arithmetic and copies ran while one was open for 20% -> 23% of each run, Pallas kernels for 0% -> 0%
where the time goes in v10:
time: 250 us; the launch traced here: 249 us
  waiting for transfers between devices  105 us (42%)
  local copies, waits for them, and re-layouts  45.6 us (18%)
  starting transfers between devices  42.1 us (17%)
  between operations  16.3 us (7%)
  matrix products  14.3 us (6%)
  other arithmetic  14.2 us (6%)
  blocking collectives  11.6 us (5%)
    all_to_all x1, waiting for transfers between devices, per_device(): got = lax.all_to_all(spread, 'row', 2, 2, tiled=True)  57.9 us
    all_to_all x4, waiting for transfers between devices, gather_row(): return lax.all_to_all(spread, 'row', 0, 0, tiled=False)  46.9 us
    all_to_all x4, starting transfers between devices, gather_row(): return lax.all_to_all(spread, 'row', 0, 0, tiled=False)  20.7 us
    all_gather x1, blocking collectives, per_device(): owned = lax.all_gather(owned, 'src', axis=0, tiled=False)  11.6 us
    all_to_all x1, starting transfers between devices, per_device(): lax.all_to_all(factors.reshape(n_row, PAIR, width), 'row', 0, 0, tiled=Fa...  11.3 us
    all_to_all x1, starting transfers between devices, per_device(): got = lax.all_to_all(spread, 'row', 2, 2, tiled=True)  10 us
    unnamed x29, local copies, waits for them, and re-layouts  9.75 us
    dot_general x4, matrix products, per_device(): result = jnp.dot(inverse, full_residue, preferred_element_type=jnp.float32)  6.56 us
  transfers between devices with their start and end apart: 7, of which 5 were waited for; matrix products, arithmetic and copies ran while one was open for 23% of the time, Pallas kernels for 0%

profile of v10, /device:TPU:16, one launch (start us, length us, event | category | flops | bytes accessed | tf_op | source)
XLA Modules:
  0.0 248.9 jit_solution(16278904660787157466)
XLA Ops:
  9.0 11.3 %all-to-all-start = ((bf16[32,2,1536]{2,1,0:T(2,128)(2,1)}), bf16[32,2,1536]{2,1,0:T(2,128)(2,1)S(1)}, u32[]{:S(2)}, u32[]{:S(2)}) async-start(bf16[32,2,1536]{2,1,0:T(2,128)(2,1)} %reshape.1155), calls=%async_computation | async-start | bytes 393216 | tf_op jit(solution)/shard_map/all_to_all | solution.py:37
  22.0 3.0 %fusion.10 = f32[1024,512]{1,0:T(8,128)S(1)} fusion(bf16[1024,1024]{1,0:T(8,128)(2,1)S(1)} %copy-done, f32[1024,512]{1,0:T(8,128)} %param.11), kind=kOutput, calls=%fused_computation.20 | convolution fusion | flops 1074266112 | bytes 6291456 | tf_op jit(solution)/shard_map/dot_general | solution.py:47
  26.4 2.6 %fusion.2 = f32[2,512,512]{2,1,0:T(8,128)} fusion(bf16[1,2,512,1024]{3,2,1,0:T(8,128)(2,1)S(1)} %copy-done.6, f32[1024,512]{1,0:T(8,128)S(1)} %fusion.10), kind=kOutput, calls=%fused_computation.9 | convolution fusion | flops 1074266112 | bytes 6291456 | tf_op jit(solution)/shard_map/lmf,ft->lmt/dot_general | solution.py:51
  28.9 3.5 %reshape.1158 = f32[2,8,32,2,512]{4,3,2,1,0:T(2,128)} reshape(f32[2,512,512]{2,1,0:T(8,128)} %fusion.2) | data formatting | bytes 4194304 | tf_op jit(solution)/shard_map/reshape | solution.py:64
  33.0 5.0 %pad_maximum_fusion = f32[3,8,32,2,512]{4,3,1,0,2:T(2,128)} fusion(f32[1,8,32,2,512]{4,3,1,0,2:T(2,128)S(1)} %broadcast_dynamic-update-slice_fusion, f32[2,8,32,2,512]{4,3,2,1,0:T(2,128)} %reshape.1158), kind=kLoop, calls=%fused_computation.1 | loop fusion | flops 786432 | bytes 6291456 | tf_op jit(solution)/shard_map/concatenate | solution.py:63
  38.0 10.0 %all-to-all-start.1 = ((f32[3,8,32,2,512]{4,3,1,0,2:T(2,128)}), f32[3,8,32,2,512]{4,3,1,0,2:T(2,128)}, u32[]{:S(2)}, u32[]{:S(2)}) async-start(f32[3,8,32,2,512]{4,3,1,0,2:T(2,128)} %pad_maximum_fusion), calls=%async_computation.1 | async-start | bytes 6291456 | tf_op jit(solution)/shard_map/all_to_all | solution.py:66
  52.1 11.6 %all_gather.9 = bf16[8,4,2,1536]{3,1,2,0:T(4,128)(2,1)S(1)} all-gather(bf16[1,4,2,1536]{3,1,2,0:T(4,128)(2,1)S(1)} %copy.122), channel_id=1, replica_groups=mesh['row'=32,'src'=8] {'src'}, dimensions={0}, use_global_device_ids=true | all-gather | bytes 221184 | tf_op jit(solution)/shard_map/all_gather | solution.py:41
  64.3 57.9 %all-to-all-done.1 = f32[3,8,32,2,512]{4,3,1,0,2:T(2,128)} async-done(((f32[3,8,32,2,512]{4,3,1,0,2:T(2,128)}), f32[3,8,32,2,512]{4,3,1,0,2:T(2,128)}, u32[]{:S(2)}, u32[]{:S(2)}) %all-to-all-start.1) | async-done | bytes 3145760 | tf_op jit(solution)/shard_map/all_to_all | solution.py:66
  134.4 6.6 %select_reduce_fusion.3 = (f32[8,2,512]{2,1,0:T(2,128)S(1)}, f32[8,2,512]{2,1,0:T(2,128)S(1)}, f32[8,2,512]{2,1,0:T(2,128)S(1)}, f32[8,2,512]{2,1,0:T(2,128)S(1)}) fusion(pred[32,2]{1,0:T(8,128)(4,1)S(1)} %copy.165, f32[3,8,32,2,512]{4,3,1,0,2:T(2,128)} %all-to-all-done.1, pred[32,2]{1,0:T(8,128)(4,1)S(1)} %copy.173, pred[32,2]{1,0:T(8,128)(4,1)S(1)} %copy.181, ...), kind=kLoop, calls=%fused_computation.8 | loop fusion | flops 4161536 | bytes 2228480 | tf_op jit(solution)/shard_map/reduce_sum | solution.py:80
  141.9 6.8 %all-to-all-start.2 = ((bf16[32,16,512]{2,1,0:T(8,128)(2,1)}), bf16[32,16,512]{2,1,0:T(8,128)(2,1)S(1)}, u32[]{:S(2)}, u32[]{:S(2)}) async-start(bf16[32,16,512]{2,1,0:T(8,128)(2,1)} %broadcast_in_dim.85), calls=%async_computation.2 | async-start | bytes 1048576 | tf_op jit(solution)/shard_map/all_to_all | solution.py:13
  148.9 2.9 %fusion.36 = (bf16[32,1,16,512]{3,2,1,0:T(8,128)(2,1)}, bf16[32,1,16,512]{3,2,1,0:T(8,128)(2,1)}, bf16[32,1,16,512]{3,2,1,0:T(8,128)(2,1)}, bf16[32,1,16,512]{3,2,1,0:T(8,128)(2,1)}) fusion(bf16[32,4,16,512]{3,2,1,0:T(8,128)(2,1)} %bitcast.312), kind=kLoop, calls=%fused_computation.163 | loop fusion | bytes 4194304 | tf_op jit(solution)/shard_map/slice | solution.py:99
  151.8 13.1 %all-to-all-done.2 = bf16[32,16,512]{2,1,0:T(8,128)(2,1)S(1)} async-done(((bf16[32,16,512]{2,1,0:T(8,128)(2,1)}), bf16[32,16,512]{2,1,0:T(8,128)(2,1)S(1)}, u32[]{:S(2)}, u32[]{:S(2)}) %all-to-all-start.2) | async-done | bytes 524320 | tf_op jit(solution)/shard_map/all_to_all | solution.py:13
  165.7 1.6 fusion.39
  168.4 4.6 %all-to-all-start.3 = ((bf16[32,16,512]{2,1,0:T(8,128)(2,1)}), bf16[32,16,512]{2,1,0:T(8,128)(2,1)}, u32[]{:S(2)}, u32[]{:S(2)}) async-start(bf16[32,16,512]{2,1,0:T(8,128)(2,1)} %broadcast_in_dim.86), calls=%async_computation.3 | async-start | bytes 1048576 | tf_op jit(solution)/shard_map/all_to_all | solution.py:13
  174.6 14.9 %all-to-all-done.3 = bf16[32,16,512]{2,1,0:T(8,128)(2,1)} async-done(((bf16[32,16,512]{2,1,0:T(8,128)(2,1)}), bf16[32,16,512]{2,1,0:T(8,128)(2,1)}, u32[]{:S(2)}, u32[]{:S(2)}) %all-to-all-start.3) | async-done | bytes 524320 | tf_op jit(solution)/shard_map/all_to_all | solution.py:13
  189.5 1.6 fusion.40
  193.2 4.6 %all-to-all-start.4 = ((bf16[32,16,512]{2,1,0:T(8,128)(2,1)}), bf16[32,16,512]{2,1,0:T(8,128)(2,1)}, u32[]{:S(2)}, u32[]{:S(2)}) async-start(bf16[32,16,512]{2,1,0:T(8,128)(2,1)} %broadcast_in_dim.88), calls=%async_computation.4 | async-start | bytes 1048576 | tf_op jit(solution)/shard_map/all_to_all | solution.py:13
  200.6 13.6 %all-to-all-done.4 = bf16[32,16,512]{2,1,0:T(8,128)(2,1)} async-done(((bf16[32,16,512]{2,1,0:T(8,128)(2,1)}), bf16[32,16,512]{2,1,0:T(8,128)(2,1)}, u32[]{:S(2)}, u32[]{:S(2)}) %all-to-all-start.4) | async-done | bytes 524320 | tf_op jit(solution)/shard_map/all_to_all | solution.py:13
  214.2 1.6 fusion.41
  217.9 4.6 %all-to-all-start.5 = ((bf16[32,16,512]{2,1,0:T(8,128)(2,1)}), bf16[32,16,512]{2,1,0:T(8,128)(2,1)}, u32[]{:S(2)}, u32[]{:S(2)}) async-start(bf16[32,16,512]{2,1,0:T(8,128)(2,1)} %broadcast_in_dim.89), calls=%async_computation.5 | async-start | bytes 1048576 | tf_op jit(solution)/shard_map/all_to_all | solution.py:13
  222.5 2.1 copy.124
  227.3 2.8 %reshape.1164 = f32[32,8,2,512]{3,2,1,0:T(2,128)} reshape(f32[512,512]{1,0:T(8,128)} %copy-done.1) | data formatting | bytes 2097152 | tf_op jit(solution)/shard_map/reshape | solution.py:108
  233.6 5.3 %all-to-all-done.5 = bf16[32,16,512]{2,1,0:T(8,128)(2,1)} async-done(((bf16[32,16,512]{2,1,0:T(8,128)(2,1)}), bf16[32,16,512]{2,1,0:T(8,128)(2,1)}, u32[]{:S(2)}, u32[]{:S(2)}) %all-to-all-start.5) | async-done | bytes 524320 | tf_op jit(solution)/shard_map/all_to_all | solution.py:13
  238.9 1.7 fusion.12
  (117 shorter events, 39.0 us)
Async XLA Ops:
  7.2 14.9 %copy-start = (bf16[1024,1024]{1,0:T(8,128)(2,1)S(1)}, bf16[1024,1024]{1,0:T(8,128)(2,1)}, u32[]{:S(2)}) copy-start(bf16[1024,1024]{1,0:T(8,128)(2,1)} %param.12) | copy-start | bytes 6291460
  9.0 29.0 %all-to-all-start = ((bf16[32,2,1536]{2,1,0:T(2,128)(2,1)}), bf16[32,2,1536]{2,1,0:T(2,128)(2,1)S(1)}, u32[]{:S(2)}, u32[]{:S(2)}) async-start(bf16[32,2,1536]{2,1,0:T(2,128)(2,1)} %reshape.1155), calls=%async_computation | async-start | bytes 393216 | tf_op jit(solution)/shard_map/all_to_all | solution.py:37
  22.0 4.3 %copy-start.6 = (bf16[1,2,512,1024]{3,2,1,0:T(8,128)(2,1)S(1)}, bf16[1,2,512,1024]{3,2,1,0:T(8,128)(2,1)}, u32[]{:S(2)}) copy-start(bf16[1,2,512,1024]{3,2,1,0:T(8,128)(2,1)} %param.13) | copy-start | bytes 6291460
  25.0 1.3 copy-start.8
  38.0 10.1 %copy-start.7 = (s32[4]{0:T(128)S(1)}, s32[4]{0:T(128)}, u32[]{:S(2)}) copy-start(s32[4]{0:T(128)} %param.18) | copy-start | bytes 52
  38.0 84.2 %all-to-all-start.1 = ((f32[3,8,32,2,512]{4,3,1,0,2:T(2,128)}), f32[3,8,32,2,512]{4,3,1,0,2:T(2,128)}, u32[]{:S(2)}, u32[]{:S(2)}) async-start(f32[3,8,32,2,512]{4,3,1,0,2:T(2,128)} %pad_maximum_fusion), calls=%async_computation.1 | async-start | bytes 6291456 | tf_op jit(solution)/shard_map/all_to_all | solution.py:66
  48.1 100.8 %all-gather.3.cloned.1.call-start = ((), (), s32[]{:S(2)}) async-start(), calls=%async_computation.6 | async-start | bytes 2162688 | tf_op jit(solution)/shard_map/all_gather | solution.py:45
  141.9 23.1 %all-to-all-start.2 = ((bf16[32,16,512]{2,1,0:T(8,128)(2,1)}), bf16[32,16,512]{2,1,0:T(8,128)(2,1)S(1)}, u32[]{:S(2)}, u32[]{:S(2)}) async-start(bf16[32,16,512]{2,1,0:T(8,128)(2,1)} %broadcast_in_dim.85), calls=%async_computation.2 | async-start | bytes 1048576 | tf_op jit(solution)/shard_map/all_to_all | solution.py:13
  164.9 0.8 copy-start.4
  165.7 7.4 %copy-start.5 = (s32[4,2]{0,1:T(2,128)S(1)}, s32[4,2]{0,1:T(2,128)}, u32[]{:S(2)}) copy-start(s32[4,2]{0,1:T(2,128)} %param.19) | copy-start | bytes 100
  168.4 21.1 %all-to-all-start.3 = ((bf16[32,16,512]{2,1,0:T(8,128)(2,1)}), bf16[32,16,512]{2,1,0:T(8,128)(2,1)}, u32[]{:S(2)}, u32[]{:S(2)}) async-start(bf16[32,16,512]{2,1,0:T(8,128)(2,1)} %broadcast_in_dim.86), calls=%async_computation.3 | async-start | bytes 1048576 | tf_op jit(solution)/shard_map/all_to_all | solution.py:13
  191.1 1.0 copy-start.1
  193.2 21.1 %all-to-all-start.4 = ((bf16[32,16,512]{2,1,0:T(8,128)(2,1)}), bf16[32,16,512]{2,1,0:T(8,128)(2,1)}, u32[]{:S(2)}, u32[]{:S(2)}) async-start(bf16[32,16,512]{2,1,0:T(8,128)(2,1)} %broadcast_in_dim.88), calls=%async_computation.4 | async-start | bytes 1048576 | tf_op jit(solution)/shard_map/all_to_all | solution.py:13
  215.9 1.0 copy-start.2
  217.9 21.0 %all-to-all-start.5 = ((bf16[32,16,512]{2,1,0:T(8,128)(2,1)}), bf16[32,16,512]{2,1,0:T(8,128)(2,1)}, u32[]{:S(2)}, u32[]{:S(2)}) async-start(bf16[32,16,512]{2,1,0:T(8,128)(2,1)} %broadcast_in_dim.89), calls=%async_computation.5 | async-start | bytes 1048576 | tf_op jit(solution)/shard_map/all_to_all | solution.py:13
  226.3 4.8 %copy-start.3 = (f32[512,512]{1,0:T(8,128)S(1)}, f32[512,512]{1,0:T(8,128)}, u32[]{:S(2)}) copy-start(f32[512,512]{1,0:T(8,128)} %copy-done.2) | copy-start | bytes 3145732
Sparse Core Ops, SparseCore 0:
  64.5 84.0 all-gather.2

commit v11 on v7

--- a/solution.py
+++ b/solution.py
@@ -34,8 +34,12 @@
 
     factors = jnp.concatenate([sep_lower, sep_inverse], axis=1)
     width = factors.shape[1]
-    slot_rows = lax.all_to_all(factors.reshape(n_row, PAIR, width), "row", 0, 0, tiled=False)
-    owned = slot_rows[factor_owner_slots]
+    my_list = jnp.zeros((width,), jnp.bfloat16).at[:LINKS].set(update_lists[0].astype(jnp.bfloat16))
+    my_list = jnp.broadcast_to(my_list[None, None], (n_row, 1, width))
+    sent = jnp.concatenate([factors.reshape(n_row, PAIR, width), my_list], axis=1)
+    slot_rows = lax.all_to_all(sent, "row", 0, 0, tiled=False)
+    got_lists = slot_rows[:, PAIR, :LINKS].astype(jnp.float32)
+    owned = slot_rows[:, :PAIR][factor_owner_slots]
     owned = owned.reshape(STEPS, PAIR, width // block, n_src, n_row, PAIR)
     owned = owned.transpose(0, 1, 2, 4, 3, 5).reshape(STEPS, PAIR, width)
     owned = lax.all_gather(owned, "src", axis=0, tiled=False)
@@ -54,13 +58,10 @@
     per_dest = updates.reshape(LINKS, n_src, n_row, PAIR, cols).transpose(2, 0, 1, 3, 4)
     per_dest = per_dest.reshape(n_row, LINKS * span, cols)
     src_rows = sep_source.reshape(n_row, PAIR, cols)
-    lists = jnp.zeros((cols,), jnp.float32).at[:LINKS].set(update_lists[0].astype(jnp.float32))
-    lists = jnp.broadcast_to(lists[None, None], (n_row, 1, cols))
-    payload = jnp.concatenate([per_dest, src_rows, lists], axis=1)
+    payload = jnp.concatenate([per_dest, src_rows], axis=1)
     got = lax.all_to_all(payload, "row", 0, 0, tiled=False)
     got_updates = got[:, : LINKS * span].reshape(n_row, LINKS, span, cols)
     got_src = got[:, LINKS * span : LINKS * span + PAIR].reshape(STEPS, span, cols)
-    got_lists = got[:, LINKS * span + PAIR, :LINKS]
     pending = []
     for k in range(STEPS):
         hit = (got_lists == k)[:, :, None, None]

time: 240 us -> 239 us (level)
  local copies, waits for them, and re-layouts: 43.2 us -> 40 us
  waiting for transfers between devices: 101 us -> 104 us
    transpose x1 -> x0, local copies, waits for them, and re-layouts: 4.12 us -> none  [per_device(): updates.reshape(LINKS, n_src, n_row, PAIR, cols).transpose(2, 0, 1, 3, 4)]
    reshape x1 -> x0, local copies, waits for them, and re-layouts: 3.71 us -> none  [per_device(): per_dest = per_dest.reshape(n_row, LINKS * span, cols)]
    reshape x1 -> x2, local copies, waits for them, and re-layouts: 3.51 us -> 6.81 us  [per_device(): updates.reshape(LINKS, n_src, n_row, PAIR, cols).transpose(2, 0, 1, 3, 4)]
    concatenate x0 -> x1, local copies, waits for them, and re-layouts: none -> 2.82 us  [per_device(): payload = jnp.concatenate([per_dest, src_rows], axis=1)]
    unnamed x28 -> x26, local copies, waits for them, and re-layouts: 4.88 us -> 4.86 us
  transfers between devices with their start and end apart: 7 -> 7, of which waited for: 5 -> 5; matrix products, arithmetic and copies ran while one was open for 20% -> 19% of each run, Pallas kernels for 0% -> 0%
where the time goes in v11:
time: 239 us; the launch traced here: 237 us
  waiting for transfers between devices  104 us (44%)
  starting transfers between devices  43.1 us (18%)
  local copies, waits for them, and re-layouts  40 us (17%)
  between operations  16.4 us (7%)
  matrix products  14.3 us (6%)
  blocking collectives  11.6 us (5%)
  other arithmetic  8.35 us (3%)
    all_to_all x1, waiting for transfers between devices, per_device(): got = lax.all_to_all(payload, 'row', 0, 0, tiled=False)  47 us
    all_to_all x4, waiting for transfers between devices, gather_row(): return lax.all_to_all(spread, 'row', 0, 0, tiled=False)  28.7 us
    all_gather x1, waiting for transfers between devices, per_device(): inverse_all = lax.all_gather(inverse_rows, 'row', axis=0, tiled=False)  27.9 us
    all_to_all x4, starting transfers between devices, gather_row(): return lax.all_to_all(spread, 'row', 0, 0, tiled=False)  21.7 us
    all_gather x1, blocking collectives, per_device(): owned = lax.all_gather(owned, 'src', axis=0, tiled=False)  11.6 us
    all_to_all x1, starting transfers between devices, per_device(): slot_rows = lax.all_to_all(sent, 'row', 0, 0, tiled=False)  11.3 us
    all_to_all x1, starting transfers between devices, per_device(): got = lax.all_to_all(payload, 'row', 0, 0, tiled=False)  10 us
    reshape x2, local copies, waits for them, and re-layouts, per_device(): updates.reshape(LINKS, n_src, n_row, PAIR, cols).transpose(2, 0, 1, 3, 4)  6.81 us
  transfers between devices with their start and end apart: 7, of which 5 were waited for; matrix products, arithmetic and copies ran while one was open for 19% of the time, Pallas kernels for 0%

profile of v11, /device:TPU:16, one launch (start us, length us, event | category | flops | bytes accessed | tf_op | source)
XLA Modules:
  0.0 237.4 jit_solution(2207950618282024747)
XLA Ops:
  10.3 11.3 %all-to-all-start = ((bf16[32,3,1536]{2,1,0:T(4,128)(2,1)}), bf16[32,3,1536]{2,1,0:T(4,128)(2,1)S(1)}, u32[]{:S(2)}, u32[]{:S(2)}) async-start(bf16[32,3,1536]{2,1,0:T(4,128)(2,1)} %pad_maximum_fusion.1), calls=%async_computation | async-start | bytes 786432 | tf_op jit(solution)/shard_map/all_to_all | solution.py:40
  21.6 3.0 %fusion.10 = f32[1024,512]{1,0:T(8,128)S(1)} fusion(bf16[1024,1024]{1,0:T(8,128)(2,1)S(1)} %copy-done, f32[1024,512]{1,0:T(8,128)} %param.11), kind=kOutput, calls=%fused_computation.19 | convolution fusion | flops 1074266112 | bytes 6291456 | tf_op jit(solution)/shard_map/dot_general | solution.py:51
  26.0 2.6 %fusion.2 = f32[2,512,512]{2,1,0:T(8,128)} fusion(bf16[1,2,512,1024]{3,2,1,0:T(8,128)(2,1)S(1)} %copy-done.8, f32[1024,512]{1,0:T(8,128)S(1)} %fusion.10), kind=kOutput, calls=%fused_computation.8 | convolution fusion | flops 1074266112 | bytes 6291456 | tf_op jit(solution)/shard_map/lmf,ft->lmt/dot_general | solution.py:55
  28.5 3.5 %reshape.158 = f32[2,8,32,2,512]{4,3,2,1,0:T(2,128)} reshape(f32[2,512,512]{2,1,0:T(8,128)} %fusion.2) | data formatting | bytes 4194304 | tf_op jit(solution)/shard_map/reshape | solution.py:58
  32.0 3.3 %copy.176 = f32[2,8,32,2,512]{4,2,3,1,0:T(8,128)} copy(f32[2,8,32,2,512]{4,3,2,1,0:T(2,128)} %reshape.158) | data formatting | bytes 4194304 | tf_op jit(solution)/shard_map/reshape | solution.py:58
  35.4 1.8 pad_maximum_fusion
  37.2 2.8 %copy.178 = f32[32,34,512]{2,1,0:T(8,128)} copy(f32[32,34,512]{2,0,1:T(8,128)S(1)} %pad_maximum_fusion) | data formatting | bytes 4456448 | tf_op jit(solution)/shard_map/concatenate | solution.py:61
  40.1 10.0 %all-to-all-start.1 = ((f32[32,34,512]{2,1,0:T(8,128)}), f32[32,34,512]{2,1,0:T(8,128)}, u32[]{:S(2)}, u32[]{:S(2)}) async-start(f32[32,34,512]{2,1,0:T(8,128)} %copy.178), calls=%async_computation.1 | async-start | bytes 5242880 | tf_op jit(solution)/shard_map/all_to_all | solution.py:62
  54.3 11.6 %all_gather.9 = bf16[8,4,2,1536]{3,1,2,0:T(4,128)(2,1)S(1)} all-gather(bf16[1,4,2,1536]{3,1,2,0:T(4,128)(2,1)S(1)} %copy.173), channel_id=1, replica_groups=mesh['row'=32,'src'=8] {'src'}, dimensions={0}, use_global_device_ids=true | all-gather | bytes 221184 | tf_op jit(solution)/shard_map/all_gather | solution.py:45
  67.1 47.0 %all-to-all-done.1 = f32[32,34,512]{2,1,0:T(8,128)} async-done(((f32[32,34,512]{2,1,0:T(8,128)}), f32[32,34,512]{2,1,0:T(8,128)}, u32[]{:S(2)}, u32[]{:S(2)}) %all-to-all-start.1) | async-done | bytes 2228256 | tf_op jit(solution)/shard_map/all_to_all | solution.py:62
  115.3 2.9 %select_reduce_fusion.3 = (f32[32,512]{1,0:T(8,128)S(1)}, f32[32,512]{1,0:T(8,128)S(1)}, f32[32,512]{1,0:T(8,128)S(1)}, f32[32,512]{1,0:T(8,128)S(1)}) fusion(f32[32,34,512]{2,1,0:T(8,128)} %all-to-all-done.1, pred[32,32]{1,0:T(8,128)(4,1)S(1)} %copy.180, pred[32,32]{1,0:T(8,128)(4,1)S(1)} %copy.181, pred[32,32]{1,0:T(8,128)(4,1)S(1)} %copy.182, ...), kind=kLoop, calls=%fused_computation.7 | loop fusion | flops 4128768 | bytes 2363392 | tf_op jit(solution)/shard_map/reduce_sum | solution.py:68
  119.0 5.2 %all-to-all-start.2 = ((bf16[32,16,512]{2,1,0:T(8,128)(2,1)}), bf16[32,16,512]{2,1,0:T(8,128)(2,1)S(1)}, u32[]{:S(2)}, u32[]{:S(2)}) async-start(bf16[32,16,512]{2,1,0:T(8,128)(2,1)} %broadcast_in_dim.99), calls=%async_computation.2 | async-start | bytes 1048576 | tf_op jit(solution)/shard_map/all_to_all | solution.py:13
  125.1 27.9 %all-gather.3.cloned.1.call-done = bf16[128,16,512]{2,1,0:T(8,128)(2,1)} async-done(((bf16[4,16,512]{2,1,0:T(8,128)(2,1)}), bf16[128,16,512]{2,1,0:T(8,128)(2,1)}) %all-gather.3.cloned.1.call-update) | async-done | bytes 2097168 | tf_op jit(solution)/shard_map/all_gather | solution.py:49
  153.0 2.9 %fusion.37 = (bf16[32,1,16,512]{3,2,1,0:T(8,128)(2,1)}, bf16[32,1,16,512]{3,2,1,0:T(8,128)(2,1)}, bf16[32,1,16,512]{3,2,1,0:T(8,128)(2,1)}, bf16[32,1,16,512]{3,2,1,0:T(8,128)(2,1)}) fusion(bf16[32,4,16,512]{3,2,1,0:T(8,128)(2,1)} %bitcast.74), kind=kLoop, calls=%fused_computation.66 | loop fusion | bytes 4194304 | tf_op jit(solution)/shard_map/slice | solution.py:87
  156.7 1.6 fusion.40
  159.4 7.0 %all-to-all-start.3 = ((bf16[32,16,512]{2,1,0:T(8,128)(2,1)}), bf16[32,16,512]{2,1,0:T(8,128)(2,1)}, u32[]{:S(2)}, u32[]{:S(2)}) async-start(bf16[32,16,512]{2,1,0:T(8,128)(2,1)} %broadcast_in_dim.100), calls=%async_computation.3 | async-start | bytes 1048576 | tf_op jit(solution)/shard_map/all_to_all | solution.py:13
  168.0 13.7 %all-to-all-done.3 = bf16[32,16,512]{2,1,0:T(8,128)(2,1)} async-done(((bf16[32,16,512]{2,1,0:T(8,128)(2,1)}), bf16[32,16,512]{2,1,0:T(8,128)(2,1)}, u32[]{:S(2)}, u32[]{:S(2)}) %all-to-all-start.3) | async-done | bytes 524320 | tf_op jit(solution)/shard_map/all_to_all | solution.py:13
  185.3 4.8 %all-to-all-start.4 = ((bf16[32,16,512]{2,1,0:T(8,128)(2,1)}), bf16[32,16,512]{2,1,0:T(8,128)(2,1)}, u32[]{:S(2)}, u32[]{:S(2)}) async-start(bf16[32,16,512]{2,1,0:T(8,128)(2,1)} %broadcast_in_dim.104), calls=%async_computation.4 | async-start | bytes 1048576 | tf_op jit(solution)/shard_map/all_to_all | solution.py:13
  193.0 12.1 %all-to-all-done.4 = bf16[32,16,512]{2,1,0:T(8,128)(2,1)} async-done(((bf16[32,16,512]{2,1,0:T(8,128)(2,1)}), bf16[32,16,512]{2,1,0:T(8,128)(2,1)}, u32[]{:S(2)}, u32[]{:S(2)}) %all-to-all-start.4) | async-done | bytes 524320 | tf_op jit(solution)/shard_map/all_to_all | solution.py:13
  208.8 4.6 %all-to-all-start.5 = ((bf16[32,16,512]{2,1,0:T(8,128)(2,1)}), bf16[32,16,512]{2,1,0:T(8,128)(2,1)}, u32[]{:S(2)}, u32[]{:S(2)}) async-start(bf16[32,16,512]{2,1,0:T(8,128)(2,1)} %broadcast_in_dim.105), calls=%async_computation.5 | async-start | bytes 1048576 | tf_op jit(solution)/shard_map/all_to_all | solution.py:13
  213.4 2.1 copy.175
  218.2 2.8 %reshape.166 = f32[32,8,2,512]{3,2,1,0:T(2,128)} reshape(f32[512,512]{1,0:T(8,128)} %copy-done.1) | data formatting | bytes 2097152 | tf_op jit(solution)/shard_map/reshape | solution.py:97
  224.4 3.0 %all-to-all-done.5 = bf16[32,16,512]{2,1,0:T(8,128)(2,1)} async-done(((bf16[32,16,512]{2,1,0:T(8,128)(2,1)}), bf16[32,16,512]{2,1,0:T(8,128)(2,1)}, u32[]{:S(2)}, u32[]{:S(2)}) %all-to-all-start.5) | async-done | bytes 524320 | tf_op jit(solution)/shard_map/all_to_all | solution.py:13
  227.4 1.7 fusion.12
  (87 shorter events, 31.7 us)
Async XLA Ops:
  7.2 14.5 %copy-start = (bf16[1024,1024]{1,0:T(8,128)(2,1)S(1)}, bf16[1024,1024]{1,0:T(8,128)(2,1)}, u32[]{:S(2)}) copy-start(bf16[1024,1024]{1,0:T(8,128)(2,1)} %param.12) | copy-start | bytes 6291460
  10.3 29.8 %all-to-all-start = ((bf16[32,3,1536]{2,1,0:T(4,128)(2,1)}), bf16[32,3,1536]{2,1,0:T(4,128)(2,1)S(1)}, u32[]{:S(2)}, u32[]{:S(2)}) async-start(bf16[32,3,1536]{2,1,0:T(4,128)(2,1)} %pad_maximum_fusion.1), calls=%async_computation | async-start | bytes 786432 | tf_op jit(solution)/shard_map/all_to_all | solution.py:40
  21.6 4.3 %copy-start.8 = (bf16[1,2,512,1024]{3,2,1,0:T(8,128)(2,1)S(1)}, bf16[1,2,512,1024]{3,2,1,0:T(8,128)(2,1)}, u32[]{:S(2)}) copy-start(bf16[1,2,512,1024]{3,2,1,0:T(8,128)(2,1)} %param.13) | copy-start | bytes 6291460
  24.6 1.3 copy-start.10
  32.0 3.3 %copy-start.5 = (f32[64,512]{1,0:T(8,128)S(1)}, f32[64,512]{1,0:T(8,128)}, u32[]{:S(2)}) copy-start(f32[64,512]{1,0:T(8,128)} %param.15) | copy-start | bytes 393220
  40.1 10.1 %copy-start.9 = (s32[4]{0:T(128)S(1)}, s32[4]{0:T(128)}, u32[]{:S(2)}) copy-start(s32[4]{0:T(128)} %param.18) | copy-start | bytes 52
  40.1 74.0 %all-to-all-start.1 = ((f32[32,34,512]{2,1,0:T(8,128)}), f32[32,34,512]{2,1,0:T(8,128)}, u32[]{:S(2)}, u32[]{:S(2)}) async-start(f32[32,34,512]{2,1,0:T(8,128)} %copy.178), calls=%async_computation.1 | async-start | bytes 5242880 | tf_op jit(solution)/shard_map/all_to_all | solution.py:62
  50.1 102.9 %all-gather.3.cloned.1.call-start = ((), (), s32[]{:S(2)}) async-start(), calls=%async_computation.6 | async-start | bytes 2162688 | tf_op jit(solution)/shard_map/all_gather | solution.py:49
  119.0 36.9 %all-to-all-start.2 = ((bf16[32,16,512]{2,1,0:T(8,128)(2,1)}), bf16[32,16,512]{2,1,0:T(8,128)(2,1)S(1)}, u32[]{:S(2)}, u32[]{:S(2)}) async-start(bf16[32,16,512]{2,1,0:T(8,128)(2,1)} %broadcast_in_dim.99), calls=%async_computation.2 | async-start | bytes 1048576 | tf_op jit(solution)/shard_map/all_to_all | solution.py:13
  155.9 0.8 copy-start.4
  155.9 2.4 %copy-start.6 = (bf16[1,16,1024]{2,1,0:T(8,128)(2,1)S(1)}, bf16[1,16,1024]{2,1,0:T(8,128)(2,1)}, u32[]{:S(2)}) copy-start(bf16[1,16,1024]{2,1,0:T(8,128)(2,1)} %copy.206) | copy-start | bytes 98308
  156.7 9.7 %copy-start.7 = (s32[4,2]{0,1:T(2,128)S(1)}, s32[4,2]{0,1:T(2,128)}, u32[]{:S(2)}) copy-start(s32[4,2]{0,1:T(2,128)} %param.19) | copy-start | bytes 100
  159.4 22.2 %all-to-all-start.3 = ((bf16[32,16,512]{2,1,0:T(8,128)(2,1)}), bf16[32,16,512]{2,1,0:T(8,128)(2,1)}, u32[]{:S(2)}, u32[]{:S(2)}) async-start(bf16[32,16,512]{2,1,0:T(8,128)(2,1)} %broadcast_in_dim.100), calls=%async_computation.3 | async-start | bytes 1048576 | tf_op jit(solution)/shard_map/all_to_all | solution.py:13
  183.3 1.0 copy-start.1
  185.3 19.7 %all-to-all-start.4 = ((bf16[32,16,512]{2,1,0:T(8,128)(2,1)}), bf16[32,16,512]{2,1,0:T(8,128)(2,1)}, u32[]{:S(2)}, u32[]{:S(2)}) async-start(bf16[32,16,512]{2,1,0:T(8,128)(2,1)} %broadcast_in_dim.104), calls=%async_computation.4 | async-start | bytes 1048576 | tf_op jit(solution)/shard_map/all_to_all | solution.py:13
  206.7 1.0 copy-start.2
  208.8 18.7 %all-to-all-start.5 = ((bf16[32,16,512]{2,1,0:T(8,128)(2,1)}), bf16[32,16,512]{2,1,0:T(8,128)(2,1)}, u32[]{:S(2)}, u32[]{:S(2)}) async-start(bf16[32,16,512]{2,1,0:T(8,128)(2,1)} %broadcast_in_dim.105), calls=%async_computation.5 | async-start | bytes 1048576 | tf_op jit(solution)/shard_map/all_to_all | solution.py:13
  217.2 4.8 %copy-start.3 = (f32[512,512]{1,0:T(8,128)S(1)}, f32[512,512]{1,0:T(8,128)}, u32[]{:S(2)}) copy-start(f32[512,512]{1,0:T(8,128)} %copy-done.2) | copy-start | bytes 3145732
Sparse Core Ops, SparseCore 0:
  66.6 86.3 all-gather.2

commit v12 on v11

--- a/solution.py
+++ b/solution.py
@@ -46,7 +46,7 @@
     owned = owned.transpose(1, 0, 2, 3).reshape(STEPS, span, width)
     lower_rows = owned[:, :, : LINKS * block]
     inverse_rows = owned[:, :, LINKS * block :]
-    inverse_all = lax.all_gather(inverse_rows, "row", axis=0, tiled=False)
+    inverse_all = lax.all_gather(inverse_rows, "row", axis=1, tiled=False)
 
     sub_field = jnp.dot(
         sub_inverse, sub_source.astype(jnp.bfloat16), preferred_element_type=jnp.float32
@@ -84,7 +84,7 @@
             )
         everyone = gather_row(residue.astype(jnp.bfloat16), n_row)
         full_residue = everyone.reshape(block, cols)
-        inverse = inverse_all[:, k].reshape(block, block)
+        inverse = inverse_all[k].reshape(block, block)
         result = jnp.dot(inverse, full_residue, preferred_element_type=jnp.float32)
         fields.append(result)
         rounded_fields.append(result.astype(jnp.bfloat16))

time: 239 us -> 248 us (1.038)
  local copies, waits for them, and re-layouts: 40 us -> 49.1 us
    slice x2 -> x1, local copies, waits for them, and re-layouts: 5.03 us -> 12.1 us  [per_device(): inverse = inverse_all[k].reshape(block, block)]
  transfers between devices with their start and end apart: 7 -> 7, of which waited for: 5 -> 5; matrix products, arithmetic and copies ran while one was open for 19% -> 22% of each run, Pallas kernels for 0% -> 0%
where the time goes in v12:
time: 248 us; the launch traced here: 246 us
  waiting for transfers between devices  103 us (42%)
  local copies, waits for them, and re-layouts  49.1 us (20%)
  starting transfers between devices  43.1 us (17%)
  between operations  16.3 us (7%)
  matrix products  14.8 us (6%)
  blocking collectives  11.6 us (5%)
  other arithmetic  8.35 us (3%)
    all_to_all x1, waiting for transfers between devices, per_device(): got = lax.all_to_all(payload, 'row', 0, 0, tiled=False)  47 us
    all_to_all x4, waiting for transfers between devices, gather_row(): return lax.all_to_all(spread, 'row', 0, 0, tiled=False)  27.8 us
    all_gather x1, waiting for transfers between devices, per_device(): inverse_all = lax.all_gather(inverse_rows, 'row', axis=1, tiled=False)  27.7 us
    all_to_all x4, starting transfers between devices, gather_row(): return lax.all_to_all(spread, 'row', 0, 0, tiled=False)  21.7 us
    slice x1, local copies, waits for them, and re-layouts, per_device(): inverse = inverse_all[k].reshape(block, block)  12.1 us
    all_gather x1, blocking collectives, per_device(): owned = lax.all_gather(owned, 'src', axis=0, tiled=False)  11.6 us
    all_to_all x1, starting transfers between devices, per_device(): slot_rows = lax.all_to_all(sent, 'row', 0, 0, tiled=False)  11.3 us
    all_to_all x1, starting transfers between devices, per_device(): got = lax.all_to_all(payload, 'row', 0, 0, tiled=False)  10 us
  transfers between devices with their start and end apart: 7, of which 5 were waited for; matrix products, arithmetic and copies ran while one was open for 22% of the time, Pallas kernels for 0%

profile of v12, /device:TPU:16, one launch (start us, length us, event | category | flops | bytes accessed | tf_op | source)
XLA Modules:
  0.0 245.8 jit_solution(7674009897931278810)
XLA Ops:
  10.3 11.3 %all-to-all-start = ((bf16[32,3,1536]{2,1,0:T(4,128)(2,1)}), bf16[32,3,1536]{2,1,0:T(4,128)(2,1)S(1)}, u32[]{:S(2)}, u32[]{:S(2)}) async-start(bf16[32,3,1536]{2,1,0:T(4,128)(2,1)} %pad_maximum_fusion.1), calls=%async_computation | async-start | bytes 786432 | tf_op jit(solution)/shard_map/all_to_all | solution.py:40
  21.6 3.0 %fusion.10 = f32[1024,512]{1,0:T(8,128)S(1)} fusion(bf16[1024,1024]{1,0:T(8,128)(2,1)S(1)} %copy-done, f32[1024,512]{1,0:T(8,128)} %param.11), kind=kOutput, calls=%fused_computation.20 | convolution fusion | flops 1074266112 | bytes 6291456 | tf_op jit(solution)/shard_map/dot_general | solution.py:51
  26.0 2.6 %fusion.2 = f32[2,512,512]{2,1,0:T(8,128)} fusion(bf16[1,2,512,1024]{3,2,1,0:T(8,128)(2,1)S(1)} %copy-done.8, f32[1024,512]{1,0:T(8,128)S(1)} %fusion.10), kind=kOutput, calls=%fused_computation.8 | convolution fusion | flops 1074266112 | bytes 6291456 | tf_op jit(solution)/shard_map/lmf,ft->lmt/dot_general | solution.py:55
  28.5 3.5 %reshape.158 = f32[2,8,32,2,512]{4,3,2,1,0:T(2,128)} reshape(f32[2,512,512]{2,1,0:T(8,128)} %fusion.2) | data formatting | bytes 4194304 | tf_op jit(solution)/shard_map/reshape | solution.py:58
  32.0 3.3 %copy.152 = f32[2,8,32,2,512]{4,2,3,1,0:T(8,128)} copy(f32[2,8,32,2,512]{4,3,2,1,0:T(2,128)} %reshape.158) | data formatting | bytes 4194304 | tf_op jit(solution)/shard_map/reshape | solution.py:58
  35.4 1.8 pad_maximum_fusion
  37.3 2.8 %copy.154 = f32[32,34,512]{2,1,0:T(8,128)} copy(f32[32,34,512]{2,0,1:T(8,128)S(1)} %pad_maximum_fusion) | data formatting | bytes 4456448 | tf_op jit(solution)/shard_map/concatenate | solution.py:61
  40.1 10.0 %all-to-all-start.1 = ((f32[32,34,512]{2,1,0:T(8,128)}), f32[32,34,512]{2,1,0:T(8,128)}, u32[]{:S(2)}, u32[]{:S(2)}) async-start(f32[32,34,512]{2,1,0:T(8,128)} %copy.154), calls=%async_computation.1 | async-start | bytes 5242880 | tf_op jit(solution)/shard_map/all_to_all | solution.py:62
  54.2 11.6 %all_gather.9 = bf16[8,4,2,1536]{3,1,2,0:T(4,128)(2,1)S(1)} all-gather(bf16[1,4,2,1536]{3,1,2,0:T(4,128)(2,1)S(1)} %copy.151), channel_id=1, replica_groups=mesh['row'=32,'src'=8] {'src'}, dimensions={0}, use_global_device_ids=true | all-gather | bytes 221184 | tf_op jit(solution)/shard_map/all_gather | solution.py:45
  67.0 47.0 %all-to-all-done.1 = f32[32,34,512]{2,1,0:T(8,128)} async-done(((f32[32,34,512]{2,1,0:T(8,128)}), f32[32,34,512]{2,1,0:T(8,128)}, u32[]{:S(2)}, u32[]{:S(2)}) %all-to-all-start.1) | async-done | bytes 2228256 | tf_op jit(solution)/shard_map/all_to_all | solution.py:62
  115.2 2.9 %select_reduce_fusion.3 = (f32[32,512]{1,0:T(8,128)S(1)}, f32[32,512]{1,0:T(8,128)S(1)}, f32[32,512]{1,0:T(8,128)S(1)}, f32[32,512]{1,0:T(8,128)S(1)}) fusion(f32[32,34,512]{2,1,0:T(8,128)} %all-to-all-done.1, pred[32,32]{1,0:T(8,128)(4,1)S(1)} %copy.156, pred[32,32]{1,0:T(8,128)(4,1)S(1)} %copy.158, pred[32,32]{1,0:T(8,128)(4,1)S(1)} %copy.160, ...), kind=kLoop, calls=%fused_computation.7 | loop fusion | flops 4128768 | bytes 2363392 | tf_op jit(solution)/shard_map/reduce_sum | solution.py:68
  119.0 5.4 %all-to-all-start.2 = ((bf16[32,16,512]{2,1,0:T(8,128)(2,1)}), bf16[32,16,512]{2,1,0:T(8,128)(2,1)S(1)}, u32[]{:S(2)}, u32[]{:S(2)}) async-start(bf16[32,16,512]{2,1,0:T(8,128)(2,1)} %broadcast_in_dim.99), calls=%async_computation.2 | async-start | bytes 1048576 | tf_op jit(solution)/shard_map/all_to_all | solution.py:13
  125.3 27.7 %all-gather.3.cloned.1.call-done = bf16[4,512,512]{2,0,1:T(4,128)(2,1)} async-done(((bf16[4,16,512]{2,0,1:T(4,128)(2,1)}), bf16[4,512,512]{2,0,1:T(4,128)(2,1)}) %all-gather.3.cloned.1.call-update) | async-done | bytes 2097168 | tf_op jit(solution)/shard_map/all_gather | solution.py:49
  153.0 12.1 %slice_reduce_fusion = (bf16[512,512]{1,0:T(8,128)(2,1)}, bf16[1,512,512]{2,0,1:T(2,128)(2,1)}, bf16[1,512,512]{2,0,1:T(2,128)(2,1)}, bf16[1,512,512]{2,0,1:T(2,128)(2,1)}) fusion(bf16[4,512,512]{2,0,1:T(4,128)(2,1)} %all-gather.3.cloned.1.call-done), kind=kLoop, calls=%fused_computation.17 | loop fusion | bytes 4194304 | tf_op jit(solution)/shard_map/slice | solution.py:87
  165.9 1.8 fusion.13
  168.8 7.0 %all-to-all-start.3 = ((bf16[32,16,512]{2,1,0:T(8,128)(2,1)}), bf16[32,16,512]{2,1,0:T(8,128)(2,1)}, u32[]{:S(2)}, u32[]{:S(2)}) async-start(bf16[32,16,512]{2,1,0:T(8,128)(2,1)} %broadcast_in_dim.100), calls=%async_computation.3 | async-start | bytes 1048576 | tf_op jit(solution)/shard_map/all_to_all | solution.py:13
  177.3 13.6 %all-to-all-done.3 = bf16[32,16,512]{2,1,0:T(8,128)(2,1)} async-done(((bf16[32,16,512]{2,1,0:T(8,128)(2,1)}), bf16[32,16,512]{2,1,0:T(8,128)(2,1)}, u32[]{:S(2)}, u32[]{:S(2)}) %all-to-all-start.3) | async-done | bytes 524320 | tf_op jit(solution)/shard_map/all_to_all | solution.py:13
  190.9 1.8 fusion.14
  194.7 4.6 %all-to-all-start.4 = ((bf16[32,16,512]{2,1,0:T(8,128)(2,1)}), bf16[32,16,512]{2,1,0:T(8,128)(2,1)}, u32[]{:S(2)}, u32[]{:S(2)}) async-start(bf16[32,16,512]{2,1,0:T(8,128)(2,1)} %broadcast_in_dim.104), calls=%async_computation.4 | async-start | bytes 1048576 | tf_op jit(solution)/shard_map/all_to_all | solution.py:13
  202.2 11.4 %all-to-all-done.4 = bf16[32,16,512]{2,1,0:T(8,128)(2,1)} async-done(((bf16[32,16,512]{2,1,0:T(8,128)(2,1)}), bf16[32,16,512]{2,1,0:T(8,128)(2,1)}, u32[]{:S(2)}, u32[]{:S(2)}) %all-to-all-start.4) | async-done | bytes 524320 | tf_op jit(solution)/shard_map/all_to_all | solution.py:13
  217.4 4.6 %all-to-all-start.5 = ((bf16[32,16,512]{2,1,0:T(8,128)(2,1)}), bf16[32,16,512]{2,1,0:T(8,128)(2,1)}, u32[]{:S(2)}, u32[]{:S(2)}) async-start(bf16[32,16,512]{2,1,0:T(8,128)(2,1)} %broadcast_in_dim.105), calls=%async_computation.5 | async-start | bytes 1048576 | tf_op jit(solution)/shard_map/all_to_all | solution.py:13
  222.0 2.1 dot_general.38
  226.7 2.8 %reshape.166 = f32[32,8,2,512]{3,2,1,0:T(2,128)} reshape(f32[512,512]{1,0:T(8,128)} %copy-done.1) | data formatting | bytes 2097152 | tf_op jit(solution)/shard_map/reshape | solution.py:97
  233.0 2.9 %all-to-all-done.5 = bf16[32,16,512]{2,1,0:T(8,128)(2,1)} async-done(((bf16[32,16,512]{2,1,0:T(8,128)(2,1)}), bf16[32,16,512]{2,1,0:T(8,128)(2,1)}, u32[]{:S(2)}, u32[]{:S(2)}) %all-to-all-start.5) | async-done | bytes 524320 | tf_op jit(solution)/shard_map/all_to_all | solution.py:13
  (86 shorter events, 31.8 us)
Async XLA Ops:
  7.2 14.5 %copy-start = (bf16[1024,1024]{1,0:T(8,128)(2,1)S(1)}, bf16[1024,1024]{1,0:T(8,128)(2,1)}, u32[]{:S(2)}) copy-start(bf16[1024,1024]{1,0:T(8,128)(2,1)} %param.12) | copy-start | bytes 6291460
  10.3 29.8 %all-to-all-start = ((bf16[32,3,1536]{2,1,0:T(4,128)(2,1)}), bf16[32,3,1536]{2,1,0:T(4,128)(2,1)S(1)}, u32[]{:S(2)}, u32[]{:S(2)}) async-start(bf16[32,3,1536]{2,1,0:T(4,128)(2,1)} %pad_maximum_fusion.1), calls=%async_computation | async-start | bytes 786432 | tf_op jit(solution)/shard_map/all_to_all | solution.py:40
  21.6 4.3 %copy-start.8 = (bf16[1,2,512,1024]{3,2,1,0:T(8,128)(2,1)S(1)}, bf16[1,2,512,1024]{3,2,1,0:T(8,128)(2,1)}, u32[]{:S(2)}) copy-start(bf16[1,2,512,1024]{3,2,1,0:T(8,128)(2,1)} %param.13) | copy-start | bytes 6291460
  24.6 1.3 copy-start.10
  32.0 3.3 %copy-start.5 = (f32[64,512]{1,0:T(8,128)S(1)}, f32[64,512]{1,0:T(8,128)}, u32[]{:S(2)}) copy-start(f32[64,512]{1,0:T(8,128)} %param.15) | copy-start | bytes 393220
  40.1 10.1 %copy-start.9 = (s32[4]{0:T(128)S(1)}, s32[4]{0:T(128)}, u32[]{:S(2)}) copy-start(s32[4]{0:T(128)} %param.18) | copy-start | bytes 52
  40.1 74.0 %all-to-all-start.1 = ((f32[32,34,512]{2,1,0:T(8,128)}), f32[32,34,512]{2,1,0:T(8,128)}, u32[]{:S(2)}, u32[]{:S(2)}) async-start(f32[32,34,512]{2,1,0:T(8,128)} %copy.154), calls=%async_computation.1 | async-start | bytes 5242880 | tf_op jit(solution)/shard_map/all_to_all | solution.py:62
  50.1 102.9 %all-gather.3.cloned.1.call-start = ((), (), s32[]{:S(2)}) async-start(), calls=%async_computation.6 | async-start | bytes 2162688 | tf_op jit(solution)/shard_map/all_gather | solution.py:49
  119.0 46.1 %all-to-all-start.2 = ((bf16[32,16,512]{2,1,0:T(8,128)(2,1)}), bf16[32,16,512]{2,1,0:T(8,128)(2,1)S(1)}, u32[]{:S(2)}, u32[]{:S(2)}) async-start(bf16[32,16,512]{2,1,0:T(8,128)(2,1)} %broadcast_in_dim.99), calls=%async_computation.2 | async-start | bytes 1048576 | tf_op jit(solution)/shard_map/all_to_all | solution.py:13
  165.1 0.8 copy-start.4
  165.1 2.6 %copy-start.6 = (bf16[1,16,1024]{2,1,0:T(8,128)(2,1)S(1)}, bf16[1,16,1024]{2,1,0:T(8,128)(2,1)}, u32[]{:S(2)}) copy-start(bf16[1,16,1024]{2,1,0:T(8,128)(2,1)} %copy.195) | copy-start | bytes 98308
  165.9 9.9 %copy-start.7 = (s32[4,2]{0,1:T(2,128)S(1)}, s32[4,2]{0,1:T(2,128)}, u32[]{:S(2)}) copy-start(s32[4,2]{0,1:T(2,128)} %param.19) | copy-start | bytes 100
  168.8 22.1 %all-to-all-start.3 = ((bf16[32,16,512]{2,1,0:T(8,128)(2,1)}), bf16[32,16,512]{2,1,0:T(8,128)(2,1)}, u32[]{:S(2)}, u32[]{:S(2)}) async-start(bf16[32,16,512]{2,1,0:T(8,128)(2,1)} %broadcast_in_dim.100), calls=%async_computation.3 | async-start | bytes 1048576 | tf_op jit(solution)/shard_map/all_to_all | solution.py:13
  192.7 1.0 copy-start.1
  194.7 18.8 %all-to-all-start.4 = ((bf16[32,16,512]{2,1,0:T(8,128)(2,1)}), bf16[32,16,512]{2,1,0:T(8,128)(2,1)}, u32[]{:S(2)}, u32[]{:S(2)}) async-start(bf16[32,16,512]{2,1,0:T(8,128)(2,1)} %broadcast_in_dim.104), calls=%async_computation.4 | async-start | bytes 1048576 | tf_op jit(solution)/shard_map/all_to_all | solution.py:13
  215.3 1.0 copy-start.2
  217.4 18.5 %all-to-all-start.5 = ((bf16[32,16,512]{2,1,0:T(8,128)(2,1)}), bf16[32,16,512]{2,1,0:T(8,128)(2,1)}, u32[]{:S(2)}, u32[]{:S(2)}) async-start(bf16[32,16,512]{2,1,0:T(8,128)(2,1)} %broadcast_in_dim.105), calls=%async_computation.5 | async-start | bytes 1048576 | tf_op jit(solution)/shard_map/all_to_all | solution.py:13
  225.7 4.8 %copy-start.3 = (f32[512,512]{1,0:T(8,128)S(1)}, f32[512,512]{1,0:T(8,128)}, u32[]{:S(2)}) copy-start(f32[512,512]{1,0:T(8,128)} %copy-done.2) | copy-start | bytes 3145732
Sparse Core Ops, SparseCore 0:
  66.6 86.3 all-gather.2

commit v13 on v11

--- a/solution.py
+++ b/solution.py
@@ -62,10 +62,12 @@
     got = lax.all_to_all(payload, "row", 0, 0, tiled=False)
     got_updates = got[:, : LINKS * span].reshape(n_row, LINKS, span, cols)
     got_src = got[:, LINKS * span : LINKS * span + PAIR].reshape(STEPS, span, cols)
-    pending = []
-    for k in range(STEPS):
-        hit = (got_lists == k)[:, :, None, None]
-        pending.append(got_src[k] - jnp.sum(jnp.where(hit, got_updates, 0.0), axis=(0, 1)))
+    hit = (got_lists[:, :, None] == jnp.arange(STEPS, dtype=jnp.float32)).astype(jnp.float32)
+    summed = jnp.einsum(
+        "ilk,ilpc->kpc", hit, got_updates, precision=lax.Precision.HIGHEST,
+        preferred_element_type=jnp.float32,
+    )
+    pending = [got_src[k] - summed[k] for k in range(STEPS)]
 
     fields, rounded_fields = [], []
     for k in range(STEPS):

time: 239 us -> 238 us (level)
  other arithmetic: 8.35 us -> 5.53 us
    reduce_sum x5 -> x0, other arithmetic: 2.92 us -> none  [per_device(): jnp.sum(jnp.where(hit, got_updates, 0.0), axis=(0, 1))]
    unnamed x26 -> x25, local copies, waits for them, and re-layouts: 4.86 us -> 4.24 us
where the time goes in v13:
time: 238 us; the launch traced here: 236 us
  waiting for transfers between devices  102 us (43%)
  starting transfers between devices  43.6 us (18%)
  local copies, waits for them, and re-layouts  40.7 us (17%)
  matrix products  16.3 us (7%)
  between operations  16.3 us (7%)
  blocking collectives  11.6 us (5%)
  other arithmetic  5.53 us (2%)
    all_to_all x1, waiting for transfers between devices, per_device(): got = lax.all_to_all(payload, 'row', 0, 0, tiled=False)  47.5 us
    all_to_all x4, waiting for transfers between devices, gather_row(): return lax.all_to_all(spread, 'row', 0, 0, tiled=False)  27.8 us
    all_gather x1, waiting for transfers between devices, per_device(): inverse_all = lax.all_gather(inverse_rows, 'row', axis=0, tiled=False)  27.2 us
    all_to_all x4, starting transfers between devices, gather_row(): return lax.all_to_all(spread, 'row', 0, 0, tiled=False)  22.2 us
    all_gather x1, blocking collectives, per_device(): owned = lax.all_gather(owned, 'src', axis=0, tiled=False)  11.6 us
    all_to_all x1, starting transfers between devices, per_device(): slot_rows = lax.all_to_all(sent, 'row', 0, 0, tiled=False)  11.3 us
    all_to_all x1, starting transfers between devices, per_device(): got = lax.all_to_all(payload, 'row', 0, 0, tiled=False)  10 us
    reshape x2, local copies, waits for them, and re-layouts, per_device(): updates.reshape(LINKS, n_src, n_row, PAIR, cols).transpose(2, 0, 1, 3, 4)  6.73 us
  transfers between devices with their start and end apart: 7, of which 5 were waited for; matrix products, arithmetic and copies ran while one was open for 19% of the time, Pallas kernels for 0%

profile of v13, /device:TPU:16, one launch (start us, length us, event | category | flops | bytes accessed | tf_op | source)
XLA Modules:
  0.0 236.4 jit_solution(14040412314762100437)
XLA Ops:
  10.3 11.3 %all-to-all-start = ((bf16[32,3,1536]{2,1,0:T(4,128)(2,1)}), bf16[32,3,1536]{2,1,0:T(4,128)(2,1)S(1)}, u32[]{:S(2)}, u32[]{:S(2)}) async-start(bf16[32,3,1536]{2,1,0:T(4,128)(2,1)} %pad_maximum_fusion.1), calls=%async_computation | async-start | bytes 786432 | tf_op jit(solution)/shard_map/all_to_all | solution.py:40
  21.6 3.0 %fusion.15 = f32[1024,512]{1,0:T(8,128)S(1)} fusion(bf16[1024,1024]{1,0:T(8,128)(2,1)S(1)} %copy-done, f32[1024,512]{1,0:T(8,128)} %param.11), kind=kOutput, calls=%fused_computation.18 | convolution fusion | flops 1074266112 | bytes 6291456 | tf_op jit(solution)/shard_map/dot_general | solution.py:51
  26.0 2.5 %fusion.4 = f32[2,512,512]{2,1,0:T(8,128)} fusion(bf16[1,2,512,1024]{3,2,1,0:T(8,128)(2,1)S(1)} %copy-done.7, f32[1024,512]{1,0:T(8,128)S(1)} %fusion.15), kind=kOutput, calls=%fused_computation.6 | convolution fusion | flops 1074266112 | bytes 6291456 | tf_op jit(solution)/shard_map/lmf,ft->lmt/dot_general | solution.py:55
  28.5 3.4 %reshape.125 = f32[2,8,32,2,512]{4,3,2,1,0:T(2,128)} reshape(f32[2,512,512]{2,1,0:T(8,128)} %fusion.4) | data formatting | bytes 4194304 | tf_op jit(solution)/shard_map/reshape | solution.py:58
  31.9 3.3 %copy.130 = f32[2,8,32,2,512]{4,2,3,1,0:T(8,128)} copy(f32[2,8,32,2,512]{4,3,2,1,0:T(2,128)} %reshape.125) | data formatting | bytes 4194304 | tf_op jit(solution)/shard_map/reshape | solution.py:58
  35.4 1.8 pad_maximum_fusion
  37.2 2.8 %copy.132 = f32[32,34,512]{2,1,0:T(8,128)} copy(f32[32,34,512]{2,0,1:T(8,128)S(1)} %pad_maximum_fusion) | data formatting | bytes 4456448 | tf_op jit(solution)/shard_map/concatenate | solution.py:61
  40.0 10.0 %all-to-all-start.1 = ((f32[32,34,512]{2,1,0:T(8,128)}), f32[32,34,512]{2,1,0:T(8,128)}, u32[]{:S(2)}, u32[]{:S(2)}) async-start(f32[32,34,512]{2,1,0:T(8,128)} %copy.132), calls=%async_computation.1 | async-start | bytes 5242880 | tf_op jit(solution)/shard_map/all_to_all | solution.py:62
  54.1 11.6 %all_gather.9 = bf16[8,4,2,1536]{3,1,2,0:T(4,128)(2,1)S(1)} all-gather(bf16[1,4,2,1536]{3,1,2,0:T(4,128)(2,1)S(1)} %copy.127), channel_id=1, replica_groups=mesh['row'=32,'src'=8] {'src'}, dimensions={0}, use_global_device_ids=true | all-gather | bytes 221184 | tf_op jit(solution)/shard_map/all_gather | solution.py:45
  66.5 47.5 %all-to-all-done.1 = f32[32,34,512]{2,1,0:T(8,128)} async-done(((f32[32,34,512]{2,1,0:T(8,128)}), f32[32,34,512]{2,1,0:T(8,128)}, u32[]{:S(2)}, u32[]{:S(2)}) %all-to-all-start.1) | async-done | bytes 2228256 | tf_op jit(solution)/shard_map/all_to_all | solution.py:62
  115.2 1.8 slice.137
  117.0 2.0 fusion.7
  120.0 5.4 %all-to-all-start.2 = ((bf16[32,16,512]{2,1,0:T(8,128)(2,1)}), bf16[32,16,512]{2,1,0:T(8,128)(2,1)S(1)}, u32[]{:S(2)}, u32[]{:S(2)}) async-start(bf16[32,16,512]{2,1,0:T(8,128)(2,1)} %broadcast_in_dim.19), calls=%async_computation.2 | async-start | bytes 1048576 | tf_op jit(solution)/shard_map/all_to_all | solution.py:13
  125.6 27.2 %all-gather.3.cloned.1.call-done = bf16[128,16,512]{2,1,0:T(8,128)(2,1)} async-done(((bf16[4,16,512]{2,1,0:T(8,128)(2,1)}), bf16[128,16,512]{2,1,0:T(8,128)(2,1)}) %all-gather.3.cloned.1.call-update) | async-done | bytes 2097168 | tf_op jit(solution)/shard_map/all_gather | solution.py:49
  152.8 2.9 %fusion.46 = (bf16[32,1,16,512]{3,2,1,0:T(8,128)(2,1)}, bf16[32,1,16,512]{3,2,1,0:T(8,128)(2,1)}, bf16[32,1,16,512]{3,2,1,0:T(8,128)(2,1)}, bf16[32,1,16,512]{3,2,1,0:T(8,128)(2,1)}) fusion(bf16[32,4,16,512]{3,2,1,0:T(8,128)(2,1)} %bitcast.84), kind=kLoop, calls=%fused_computation.70 | loop fusion | bytes 4194304 | tf_op jit(solution)/shard_map/slice | solution.py:89
  159.2 7.6 %all-to-all-start.3 = ((bf16[32,16,512]{2,1,0:T(8,128)(2,1)}), bf16[32,16,512]{2,1,0:T(8,128)(2,1)}, u32[]{:S(2)}, u32[]{:S(2)}) async-start(bf16[32,16,512]{2,1,0:T(8,128)(2,1)} %broadcast_in_dim.20), calls=%async_computation.3 | async-start | bytes 1048576 | tf_op jit(solution)/shard_map/all_to_all | solution.py:13
  168.2 13.6 %all-to-all-done.3 = bf16[32,16,512]{2,1,0:T(8,128)(2,1)} async-done(((bf16[32,16,512]{2,1,0:T(8,128)(2,1)}), bf16[32,16,512]{2,1,0:T(8,128)(2,1)}, u32[]{:S(2)}, u32[]{:S(2)}) %all-to-all-start.3) | async-done | bytes 524320 | tf_op jit(solution)/shard_map/all_to_all | solution.py:13
  185.5 4.6 %all-to-all-start.4 = ((bf16[32,16,512]{2,1,0:T(8,128)(2,1)}), bf16[32,16,512]{2,1,0:T(8,128)(2,1)}, u32[]{:S(2)}, u32[]{:S(2)}) async-start(bf16[32,16,512]{2,1,0:T(8,128)(2,1)} %broadcast_in_dim.21), calls=%async_computation.4 | async-start | bytes 1048576 | tf_op jit(solution)/shard_map/all_to_all | solution.py:13
  192.9 11.4 %all-to-all-done.4 = bf16[32,16,512]{2,1,0:T(8,128)(2,1)} async-done(((bf16[32,16,512]{2,1,0:T(8,128)(2,1)}), bf16[32,16,512]{2,1,0:T(8,128)(2,1)}, u32[]{:S(2)}, u32[]{:S(2)}) %all-to-all-start.4) | async-done | bytes 524320 | tf_op jit(solution)/shard_map/all_to_all | solution.py:13
  208.0 4.6 %all-to-all-start.5 = ((bf16[32,16,512]{2,1,0:T(8,128)(2,1)}), bf16[32,16,512]{2,1,0:T(8,128)(2,1)}, u32[]{:S(2)}, u32[]{:S(2)}) async-start(bf16[32,16,512]{2,1,0:T(8,128)(2,1)} %broadcast_in_dim.22), calls=%async_computation.5 | async-start | bytes 1048576 | tf_op jit(solution)/shard_map/all_to_all | solution.py:13
  212.6 2.1 copy.129
  217.4 2.8 %reshape.134 = f32[32,8,2,512]{3,2,1,0:T(2,128)} reshape(f32[512,512]{1,0:T(8,128)} %copy-done.1) | data formatting | bytes 2097152 | tf_op jit(solution)/shard_map/reshape | solution.py:99
  223.7 2.8 %all-to-all-done.5 = bf16[32,16,512]{2,1,0:T(8,128)(2,1)} async-done(((bf16[32,16,512]{2,1,0:T(8,128)(2,1)}), bf16[32,16,512]{2,1,0:T(8,128)(2,1)}, u32[]{:S(2)}, u32[]{:S(2)}) %all-to-all-start.5) | async-done | bytes 524320 | tf_op jit(solution)/shard_map/all_to_all | solution.py:13
  226.5 1.7 fusion.17
  (75 shorter events, 32.4 us)
Async XLA Ops:
  7.2 14.5 %copy-start = (bf16[1024,1024]{1,0:T(8,128)(2,1)S(1)}, bf16[1024,1024]{1,0:T(8,128)(2,1)}, u32[]{:S(2)}) copy-start(bf16[1024,1024]{1,0:T(8,128)(2,1)} %param.12) | copy-start | bytes 6291460
  10.3 29.7 %all-to-all-start = ((bf16[32,3,1536]{2,1,0:T(4,128)(2,1)}), bf16[32,3,1536]{2,1,0:T(4,128)(2,1)S(1)}, u32[]{:S(2)}, u32[]{:S(2)}) async-start(bf16[32,3,1536]{2,1,0:T(4,128)(2,1)} %pad_maximum_fusion.1), calls=%async_computation | async-start | bytes 786432 | tf_op jit(solution)/shard_map/all_to_all | solution.py:40
  21.6 4.3 %copy-start.7 = (bf16[1,2,512,1024]{3,2,1,0:T(8,128)(2,1)S(1)}, bf16[1,2,512,1024]{3,2,1,0:T(8,128)(2,1)}, u32[]{:S(2)}) copy-start(bf16[1,2,512,1024]{3,2,1,0:T(8,128)(2,1)} %param.13) | copy-start | bytes 6291460
  24.6 1.3 copy-start.9
  31.9 3.3 %copy-start.5 = (f32[64,512]{1,0:T(8,128)S(1)}, f32[64,512]{1,0:T(8,128)}, u32[]{:S(2)}) copy-start(f32[64,512]{1,0:T(8,128)} %param.15) | copy-start | bytes 393220
  40.0 10.1 %copy-start.8 = (s32[4]{0:T(128)S(1)}, s32[4]{0:T(128)}, u32[]{:S(2)}) copy-start(s32[4]{0:T(128)} %param.18) | copy-start | bytes 52
  40.0 74.0 %all-to-all-start.1 = ((f32[32,34,512]{2,1,0:T(8,128)}), f32[32,34,512]{2,1,0:T(8,128)}, u32[]{:S(2)}, u32[]{:S(2)}) async-start(f32[32,34,512]{2,1,0:T(8,128)} %copy.132), calls=%async_computation.1 | async-start | bytes 5242880 | tf_op jit(solution)/shard_map/all_to_all | solution.py:62
  50.0 102.8 %all-gather.3.cloned.1.call-start = ((), (), s32[]{:S(2)}) async-start(), calls=%async_computation.6 | async-start | bytes 2162688 | tf_op jit(solution)/shard_map/all_gather | solution.py:49
  120.0 35.7 %all-to-all-start.2 = ((bf16[32,16,512]{2,1,0:T(8,128)(2,1)}), bf16[32,16,512]{2,1,0:T(8,128)(2,1)S(1)}, u32[]{:S(2)}, u32[]{:S(2)}) async-start(bf16[32,16,512]{2,1,0:T(8,128)(2,1)} %broadcast_in_dim.19), calls=%async_computation.2 | async-start | bytes 1048576 | tf_op jit(solution)/shard_map/all_to_all | solution.py:13
  155.7 0.8 copy-start.4
  156.5 10.3 %copy-start.6 = (s32[4,2]{0,1:T(2,128)S(1)}, s32[4,2]{0,1:T(2,128)}, u32[]{:S(2)}) copy-start(s32[4,2]{0,1:T(2,128)} %param.19) | copy-start | bytes 100
  159.2 22.6 %all-to-all-start.3 = ((bf16[32,16,512]{2,1,0:T(8,128)(2,1)}), bf16[32,16,512]{2,1,0:T(8,128)(2,1)}, u32[]{:S(2)}, u32[]{:S(2)}) async-start(bf16[32,16,512]{2,1,0:T(8,128)(2,1)} %broadcast_in_dim.20), calls=%async_computation.3 | async-start | bytes 1048576 | tf_op jit(solution)/shard_map/all_to_all | solution.py:13
  183.5 1.0 copy-start.1
  185.5 18.8 %all-to-all-start.4 = ((bf16[32,16,512]{2,1,0:T(8,128)(2,1)}), bf16[32,16,512]{2,1,0:T(8,128)(2,1)}, u32[]{:S(2)}, u32[]{:S(2)}) async-start(bf16[32,16,512]{2,1,0:T(8,128)(2,1)} %broadcast_in_dim.21), calls=%async_computation.4 | async-start | bytes 1048576 | tf_op jit(solution)/shard_map/all_to_all | solution.py:13
  206.0 0.9 copy-start.2
  208.0 18.5 %all-to-all-start.5 = ((bf16[32,16,512]{2,1,0:T(8,128)(2,1)}), bf16[32,16,512]{2,1,0:T(8,128)(2,1)}, u32[]{:S(2)}, u32[]{:S(2)}) async-start(bf16[32,16,512]{2,1,0:T(8,128)(2,1)} %broadcast_in_dim.22), calls=%async_computation.5 | async-start | bytes 1048576 | tf_op jit(solution)/shard_map/all_to_all | solution.py:13
  216.4 4.8 %copy-start.3 = (f32[512,512]{1,0:T(8,128)S(1)}, f32[512,512]{1,0:T(8,128)}, u32[]{:S(2)}) copy-start(f32[512,512]{1,0:T(8,128)} %copy-done.2) | copy-start | bytes 3145732
Sparse Core Ops, SparseCore 0:
  66.5 86.2 all-gather.2
